TPU v7x, 128 devices: a whole 4x4x4 slice. The times are simulated.
128 devices in a mesh: outer: 2 (over y_hi), inner: 64 (over z, x, y_lo, core).
Axes of the slice: x: 4, y: 4 (y_hi: 2, y_lo: 2; y = y_hi * 2 + y_lo), z: 4, core: 2. Of those that a mesh axis runs over, the one named last changes fastest.
Arguments:
- tile_counts: int32 [128, 4, 1024, 512], P(('outer', 'inner')), may hold values from 0 to 63, as said below
- row_counts: int32 [131072], P(('outer', 'inner')), may hold values from 100 to 19999
- col_counts: int32 [65536], P(('outer', 'inner')), may hold values from 100 to 19999
- row_factors: float32 [131072, 256], P(('outer', 'inner')), may hold values from -1.8 to 1.8
- row_accum: float32 [131072, 256], P(('outer', 'inner')), may hold values from 1 to 10
- col_factors: float32 [65536, 256], P(('outer', 'inner')), may hold values from -1.8 to 1.8
- col_accum: float32 [65536, 256], P(('outer', 'inner')), may hold values from 1 to 10
Outputs:
- rows_final: float32 [131072, 256], P(('outer', 'inner'))
- row_accum_final: float32 [131072, 256], P(('outer', 'inner'))
- cols_final: float32 [65536, 256], P(('outer', 'inner'))
- col_accum_final: float32 [65536, 256], P(('outer', 'inner'))
Inputs may be any that keep to these rules, and one draw needn't show every extreme that they name: `tile_counts`: Co-occurrence counts; about half of them are zero.
All inputs are finite; a program needn't handle non-finite values.
Results may differ from a plain program's by a relative error of at most 0.0003.
Values sent between devices are 32-bit elements; how exact they have to be, the bound alone decides.
No kernel may reach another device: no remote copies, remote signals or barrier semaphores. Data moves between devices by JAX's collectives and lax.ppermute only.
A program may use at most 64 MiB of HBM per device.

v0:
```python
import jax
import jax.numpy as jnp
from jax import lax
from jax.sharding import PartitionSpec as P

LOG_TOTAL = 17.0
LEARNING = 0.05
HIGH = lax.Precision.HIGH


def local_terms(count_tile, row_logs):
    count_float = count_tile.astype(jnp.float32)
    positive = count_tile > 0
    offset = jnp.log(jnp.maximum(count_float, 1.0)) - row_logs[:, None] + LOG_TOTAL
    confidence = 0.1 + 0.25 * jnp.sqrt(count_float)
    return (offset, confidence, positive)


def error_terms(scores, offset, confidence, positive, col_logs):
    gap = scores - (offset - col_logs[None, :])
    return jnp.where(positive, confidence * gap, jax.nn.sigmoid(gap))


def dot(a, b, ca, cb):
    return lax.dot_general(
        a, b, (((ca,), (cb,)), ((), ())), precision=HIGH, preferred_element_type=jnp.float32
    )


def body(tile_counts, row_counts, col_counts, row_factors, row_accum, col_factors, col_accum):
    total_steps = tile_counts.shape[1]
    halfway = total_steps // 2
    n_outer, n_inner = lax.axis_size("outer"), lax.axis_size("inner")

    def move(block, across):
        route = [
            (o * n_inner + i, (o + across) % n_outer * n_inner + (i + 1) % n_inner)
            for o in range(n_outer)
            for i in range(n_inner)
        ]
        return lax.ppermute(block, ("outer", "inner"), route)

    row_logs = jnp.log(row_counts.astype(jnp.float32))
    col_logs = jnp.log(col_counts.astype(jnp.float32))
    W, A, C, B = row_factors, row_accum, col_factors, col_accum
    for step in range(total_steps):
        offset, confidence, positive = local_terms(tile_counts[0, step], row_logs)
        e = error_terms(dot(W, C, 1, 1), offset, confidence, positive, col_logs)
        g = dot(e, C, 1, 0)
        A = A + g * g
        W = W - LEARNING * g / jnp.sqrt(A)
        e = error_terms(dot(W, C, 1, 1), offset, confidence, positive, col_logs)
        h = dot(e, W, 0, 0)
        B = B + h * h
        C = C - LEARNING * h / jnp.sqrt(B)
        if step + 1 < total_steps:
            across = int(step + 1 == halfway)
            col_logs = move(col_logs, across)
            C = move(C, across)
            C, B = lax.optimization_barrier((C, B))
            B = move(B, across)
    return (W, A, C, B)


def solution(mesh):
    both = ("outer", "inner")
    return jax.shard_map(
        body,
        mesh=mesh,
        in_specs=(P(both, None, None, None), P(both), P(both)) + (P(both, None),) * 4,
        out_specs=(P(both, None),) * 4,
        check_vma=False,
    )
```

profile of v0, /device:TPU:0, one launch (start us, length us, event | category | flops | bytes accessed | tf_op | source)
XLA Modules:
  0.0 112.7 jit_solution(1968982564402141589)
XLA Ops:
  1.3 4.1 %slice_compare_fusion = (pred[1,1,1024,512]{3,2,1,0:T(32,128)(4,1)S(1)}, pred[1,1,1024,512]{3,2,1,0:T(32,128)(4,1)S(1)}, pred[1,1,1024,512]{3,2,1,0:T(32,128)(4,1)S(1)}, pred[1,1,1024,512]{3,2,1,0:T(32,128)(4,1)S(1)}) fusion(s32[1,4,1024,512]{3,2,1,0:T(8,128)} %param.7), kind=kLoop, calls=%fused_computation.88 | loop fusion | flops 2097152 | bytes 10485760 | tf_op jit(solution)/shard_map/gt | solution.py:13
  5.5 1.0 fusion.176
  6.6 1.1 copy-done
  8.1 2.8 %multiply_subtract_fusion.3 = (f32[1024,256]{1,0:T(8,128)S(1)}, f32[1024,256]{1,0:T(8,128)S(1)}) fusion(f32[1024,256]{1,0:T(8,128)S(1)} %copy-done.2, f32[1024,256]{1,0:T(8,128)S(1)} %copy-done.5, f32[512,256]{1,0:T(8,128)S(1)} %copy-done.1, f32[1024,512]{1,0:T(8,128)S(1)} %fusion.176, pred[1,1,1024,512]{3,2,1,0:T(32,128)(4,1)S(1)} %get-tuple-element.30, ...), kind=kOutput, calls=%fused_computation.104 | convolution fusion | flops 813432832 | bytes 9443328 | tf_op jit(solution)/shard_map/dot_general | solution.py:25
  10.9 1.0 fusion.177
  12.0 3.3 %multiply_subtract_fusion.7 = (f32[512,256]{1,0:T(8,128)S(1)}, f32[512,256]{1,0:T(8,128)S(1)}) fusion(f32[512,256]{1,0:T(8,128)S(1)} %copy-done.1, f32[512,256]{1,0:T(8,128)S(1)} %copy-done.6, f32[1024,256]{1,0:T(8,128)S(1)} %get-tuple-element.32, f32[1024,512]{1,0:T(8,128)S(1)} %fusion.177, pred[1,1,1024,512]{3,2,1,0:T(32,128)(4,1)S(1)} %get-tuple-element.30, ...), kind=kOutput, calls=%fused_computation.162 | convolution fusion | flops 812777472 | bytes 7870464 | tf_op jit(solution)/shard_map/dot_general | solution.py:25
  15.3 1.8 %collective-permute-start.1 = (f32[512]{0:T(512)S(1)}, f32[512]{0:T(512)S(1)}, u32[]{:S(2)}, u32[]{:S(2)}) collective-permute-start(f32[512]{0:T(512)S(1)} %convert_log_fusion.1), channel_id=1, source_target_pairs={{0,1},{1,2},{2,3},{3,4},{4,5},{5,6},{6,7},{7,8},{8,9},{9,10},{10,1... | collective-permute-start | bytes 6152 | tf_op jit(solution)/shard_map/ppermute | solution.py:41
  17.1 11.9 %collective-permute-done = f32[512,256]{1,0:T(8,128)S(1)} collective-permute-done((f32[512,256]{1,0:T(8,128)S(1)}, f32[512,256]{1,0:T(8,128)S(1)}, u32[]{:S(2)}, u32[]{:S(2)}) %collective-permute-start) | collective-permute-done | bytes 524320 | tf_op jit(solution)/shard_map/ppermute | solution.py:41
  29.0 1.0 fusion.178
  30.3 2.8 %multiply_subtract_fusion.2 = (f32[1024,256]{1,0:T(8,128)S(1)}, f32[1024,256]{1,0:T(8,128)S(1)}) fusion(f32[1024,256]{1,0:T(8,128)S(1)} %get-tuple-element.32, f32[1024,256]{1,0:T(8,128)S(1)} %copy-done.5, f32[1024,256]{1,0:T(8,128)S(1)} %get-tuple-element.33, f32[512,256]{1,0:T(8,128)S(1)} %collective-permute-done, f32[1024,512]{1,0:T(8,128)S(1)} %fusion.178, ...), kind=kOutput, calls=%fused_computation.100 | convolution fusion | flops 813957120 | bytes 10491904 | tf_op jit(solution)/shard_map/dot_general | solution.py:25
  33.1 1.0 fusion.179
  34.2 8.9 %collective-permute-done.2 = f32[512,256]{1,0:T(8,128)S(1)} collective-permute-done((f32[512,256]{1,0:T(8,128)S(1)}, f32[512,256]{1,0:T(8,128)S(1)}, u32[]{:S(2)}, u32[]{:S(2)}) %collective-permute-start.2) | collective-permute-done | bytes 524320 | tf_op jit(solution)/shard_map/ppermute | solution.py:41
  43.1 3.3 %multiply_subtract_fusion.6 = (f32[512,256]{1,0:T(8,128)S(1)}, f32[512,256]{1,0:T(8,128)S(1)}) fusion(f32[512,256]{1,0:T(8,128)S(1)} %collective-permute-done, f32[512,256]{1,0:T(8,128)S(1)} %collective-permute-done.2, f32[1024,256]{1,0:T(8,128)S(1)} %get-tuple-element.24, f32[1024,512]{1,0:T(8,128)S(1)} %fusion.179, ...), kind=kOutput, calls=%fused_computation.160 | convolution fusion | flops 812777472 | bytes 7870464 | tf_op jit(solution)/shard_map/dot_general | solution.py:25
  46.5 16.2 %collective-permute-done.3 = f32[512,256]{1,0:T(8,128)S(1)} collective-permute-done((f32[512,256]{1,0:T(8,128)S(1)}, f32[512,256]{1,0:T(8,128)S(1)}, u32[]{:S(2)}, u32[]{:S(2)}) %collective-permute-start.3) | collective-permute-done | bytes 524320 | tf_op jit(solution)/shard_map/ppermute | solution.py:41
  62.8 1.0 fusion.180
  64.1 2.8 %multiply_subtract_fusion.1 = (f32[1024,256]{1,0:T(8,128)S(1)}, f32[1024,256]{1,0:T(8,128)S(1)}) fusion(f32[1024,256]{1,0:T(8,128)S(1)} %get-tuple-element.24, f32[1024,256]{1,0:T(8,128)S(1)} %get-tuple-element.25, f32[512,256]{1,0:T(8,128)S(1)} %collective-permute-done.3, f32[1024,512]{1,0:T(8,128)S(1)} %fusion.180, ...), kind=kOutput, calls=%fused_computation.96 | convolution fusion | flops 813432832 | bytes 9443328 | tf_op jit(solution)/shard_map/dot_general | solution.py:25
  66.9 1.0 fusion.181
  68.0 10.2 %collective-permute-done.5 = f32[512,256]{1,0:T(8,128)S(1)} collective-permute-done((f32[512,256]{1,0:T(8,128)S(1)}, f32[512,256]{1,0:T(8,128)S(1)}, u32[]{:S(2)}, u32[]{:S(2)}) %collective-permute-start.5) | collective-permute-done | bytes 524320 | tf_op jit(solution)/shard_map/ppermute | solution.py:41
  78.1 3.3 %multiply_subtract_fusion.5 = (f32[512,256]{1,0:T(8,128)S(1)}, f32[512,256]{1,0:T(8,128)S(1)}) fusion(f32[512,256]{1,0:T(8,128)S(1)} %collective-permute-done.3, f32[512,256]{1,0:T(8,128)S(1)} %collective-permute-done.5, f32[1024,256]{1,0:T(8,128)S(1)} %get-tuple-element.34, f32[1024,512]{1,0:T(8,128)S(1)} %fusion.181, ...), kind=kOutput, calls=%fused_computation.158 | convolution fusion | flops 812777472 | bytes 7870464 | tf_op jit(solution)/shard_map/dot_general | solution.py:25
  81.4 1.2 %collective-permute-start.6 = (f32[512,256]{1,0:T(8,128)S(1)}, f32[512,256]{1,0:T(8,128)S(1)}, u32[]{:S(2)}, u32[]{:S(2)}) collective-permute-start(f32[512,256]{1,0:T(8,128)S(1)} %get-tuple-element.20), channel_id=1, source_target_pairs={{0,1},{1,2},{2,3},{3,4},{4,5},{5,6},{6,7},{7,8},{8,9},{9,10},{10,1... | collective-permute-start | bytes 1572872 | tf_op jit(solution)/shard_map/ppermute | solution.py:41
  82.7 11.6 %collective-permute-done.6 = f32[512,256]{1,0:T(8,128)S(1)} collective-permute-done((f32[512,256]{1,0:T(8,128)S(1)}, f32[512,256]{1,0:T(8,128)S(1)}, u32[]{:S(2)}, u32[]{:S(2)}) %collective-permute-start.6) | collective-permute-done | bytes 524320 | tf_op jit(solution)/shard_map/ppermute | solution.py:41
  95.7 4.0 %multiply_subtract_fusion = (f32[1024,256]{1,0:T(8,128)S(1)}, f32[1024,256]{1,0:T(8,128)}) fusion(f32[1024,256]{1,0:T(8,128)S(1)} %get-tuple-element.34, f32[1024,256]{1,0:T(8,128)S(1)} %get-tuple-element.25, f32[1024,256]{1,0:T(8,128)S(1)} %get-tuple-element.35, f32[512,256]{1,0:T(8,128)S(1)} %collective-permute-done.6, f32[1024,512]{1,0:T(8,128)S(1)} %fusion.182, ...), kind=kOutput, calls=%fused_computation.92 | convolution fusion | flops 813957120 | bytes 10491904 | tf_op jit(solution)/shard_map/dot_general | solution.py:25
  100.7 7.7 %collective-permute-done.8 = f32[512,256]{1,0:T(8,128)S(1)} collective-permute-done((f32[512,256]{1,0:T(8,128)S(1)}, f32[512,256]{1,0:T(8,128)S(1)}, u32[]{:S(2)}, u32[]{:S(2)}) %collective-permute-start.8) | collective-permute-done | bytes 524320 | tf_op jit(solution)/shard_map/ppermute | solution.py:41
  108.5 4.2 %multiply_subtract_fusion.4 = (f32[512,256]{1,0:T(8,128)}, f32[512,256]{1,0:T(8,128)}) fusion(f32[512,256]{1,0:T(8,128)S(1)} %collective-permute-done.6, f32[512,256]{1,0:T(8,128)S(1)} %collective-permute-done.8, f32[1024,256]{1,0:T(8,128)S(1)} %get-tuple-element.18, f32[1024,512]{1,0:T(8,128)S(1)} %fusion.183, ...), kind=kOutput, calls=%fused_computation.156 | convolution fusion | flops 812777472 | bytes 7870464 | tf_op jit(solution)/shard_map/dot_general | solution.py:25
  (27 shorter events, 4.4 us)
Async XLA Ops:
  1.3 4.2 %copy-start.4 = (s32[512]{0:T(512)S(1)}, s32[512]{0:T(512)}, u32[]{:S(2)}) copy-start(s32[512]{0:T(512)} %param.9) | copy-start | bytes 6148
  1.3 4.2 %copy-start.1 = (f32[512,256]{1,0:T(8,128)S(1)}, f32[512,256]{1,0:T(8,128)}, u32[]{:S(2)}) copy-start(f32[512,256]{1,0:T(8,128)} %param.12) | copy-start | bytes 1572868
  1.3 4.2 %copy-start.2 = (f32[1024,256]{1,0:T(8,128)S(1)}, f32[1024,256]{1,0:T(8,128)}, u32[]{:S(2)}) copy-start(f32[1024,256]{1,0:T(8,128)} %param.10) | copy-start | bytes 3145732
  1.3 6.4 %copy-start = (s32[1,4,1024,512]{3,2,1,0:T(8,128)S(1)}, s32[1,4,1024,512]{3,2,1,0:T(8,128)}, u32[]{:S(2)}) copy-start(s32[1,4,1024,512]{3,2,1,0:T(8,128)} %param.7) | copy-start | bytes 25165828
  5.5 2.6 %copy-start.5 = (f32[1024,256]{1,0:T(8,128)S(1)}, f32[1024,256]{1,0:T(8,128)}, u32[]{:S(2)}) copy-start(f32[1024,256]{1,0:T(8,128)} %param.11) | copy-start | bytes 3145732
  10.9 1.1 copy-start.6
  15.2 13.7 %collective-permute-start = (f32[512,256]{1,0:T(8,128)S(1)}, f32[512,256]{1,0:T(8,128)S(1)}, u32[]{:S(2)}, u32[]{:S(2)}) collective-permute-start(f32[512,256]{1,0:T(8,128)S(1)} %get-tuple-element.26), channel_id=1, source_target_pairs={{0,1},{1,2},{2,3},{3,4},{4,5},{5,6},{6,7},{7,8},{8,9},{9,10},{10,1... | collective-permute-start | bytes 1572872 | tf_op jit(solution)/shard_map/ppermute | solution.py:41
  15.3 15.0 %collective-permute-start.1 = (f32[512]{0:T(512)S(1)}, f32[512]{0:T(512)S(1)}, u32[]{:S(2)}, u32[]{:S(2)}) collective-permute-start(f32[512]{0:T(512)S(1)} %convert_log_fusion.1), channel_id=1, source_target_pairs={{0,1},{1,2},{2,3},{3,4},{4,5},{5,6},{6,7},{7,8},{8,9},{9,10},{10,1... | collective-permute-start | bytes 6152 | tf_op jit(solution)/shard_map/ppermute | solution.py:41
  30.0 13.1 %collective-permute-start.2 = (f32[512,256]{1,0:T(8,128)S(1)}, f32[512,256]{1,0:T(8,128)S(1)}, u32[]{:S(2)}, u32[]{:S(2)}) collective-permute-start(f32[512,256]{1,0:T(8,128)S(1)} %get-tuple-element.11), channel_id=1, source_target_pairs={{0,1},{1,2},{2,3},{3,4},{4,5},{5,6},{6,7},{7,8},{8,9},{9,10},{10,1... | collective-permute-start | bytes 1572872 | tf_op jit(solution)/shard_map/ppermute | solution.py:41
  46.4 16.4 %collective-permute-start.3 = (f32[512,256]{1,0:T(8,128)S(1)}, f32[512,256]{1,0:T(8,128)S(1)}, u32[]{:S(2)}, u32[]{:S(2)}) collective-permute-start(f32[512,256]{1,0:T(8,128)S(1)} %get-tuple-element.22), channel_id=1, source_target_pairs={{0,65},{1,66},{2,67},{3,68},{4,69},{5,70},{6,71},{7,72},{8,73},{9,... | collective-permute-start | bytes 1572872 | tf_op jit(solution)/shard_map/ppermute | solution.py:41
  46.5 17.7 %collective-permute-start.4 = (f32[512]{0:T(512)S(1)}, f32[512]{0:T(512)S(1)}, u32[]{:S(2)}, u32[]{:S(2)}) collective-permute-start(f32[512]{0:T(512)S(1)} %collective-permute-done.1), channel_id=1, source_target_pairs={{0,65},{1,66},{2,67},{3,68},{4,69},{5,70},{6,71},{7,72},{8,73},{9,... | collective-permute-start | bytes 6152 | tf_op jit(solution)/shard_map/ppermute | solution.py:41
  63.8 14.3 %collective-permute-start.5 = (f32[512,256]{1,0:T(8,128)S(1)}, f32[512,256]{1,0:T(8,128)S(1)}, u32[]{:S(2)}, u32[]{:S(2)}) collective-permute-start(f32[512,256]{1,0:T(8,128)S(1)} %get-tuple-element.13), channel_id=1, source_target_pairs={{0,65},{1,66},{2,67},{3,68},{4,69},{5,70},{6,71},{7,72},{8,73},{9,... | collective-permute-start | bytes 1572872 | tf_op jit(solution)/shard_map/ppermute | solution.py:41
  81.4 12.9 %collective-permute-start.6 = (f32[512,256]{1,0:T(8,128)S(1)}, f32[512,256]{1,0:T(8,128)S(1)}, u32[]{:S(2)}, u32[]{:S(2)}) collective-permute-start(f32[512,256]{1,0:T(8,128)S(1)} %get-tuple-element.20), channel_id=1, source_target_pairs={{0,1},{1,2},{2,3},{3,4},{4,5},{5,6},{6,7},{7,8},{8,9},{9,10},{10,1... | collective-permute-start | bytes 1572872 | tf_op jit(solution)/shard_map/ppermute | solution.py:41
  82.6 13.1 %collective-permute-start.7 = (f32[512]{0:T(512)S(1)}, f32[512]{0:T(512)S(1)}, u32[]{:S(2)}, u32[]{:S(2)}) collective-permute-start(f32[512]{0:T(512)S(1)} %collective-permute-done.4), channel_id=1, source_target_pairs={{0,1},{1,2},{2,3},{3,4},{4,5},{5,6},{6,7},{7,8},{8,9},{9,10},{10,1... | collective-permute-start | bytes 6152 | tf_op jit(solution)/shard_map/ppermute | solution.py:41
  95.3 13.2 %collective-permute-start.8 = (f32[512,256]{1,0:T(8,128)S(1)}, f32[512,256]{1,0:T(8,128)S(1)}, u32[]{:S(2)}, u32[]{:S(2)}) collective-permute-start(f32[512,256]{1,0:T(8,128)S(1)} %get-tuple-element.15), channel_id=1, source_target_pairs={{0,1},{1,2},{2,3},{3,4},{4,5},{5,6},{6,7},{7,8},{8,9},{9,10},{10,1... | collective-permute-start | bytes 1572872 | tf_op jit(solution)/shard_map/ppermute | solution.py:41
  99.7 13.0 %copy-start.3 = (f32[1024,256]{1,0:T(8,128)}, f32[1024,256]{1,0:T(8,128)S(1)}, u32[]{:S(2)}) copy-start(f32[1024,256]{1,0:T(8,128)S(1)} %get-tuple-element.18) | copy-start | bytes 3145732
where the time goes:
time: 113 us
  waiting for transfers between devices  66.5 us (59%)
  matrix products  34.7 us (31%)
  other arithmetic  4.84 us (4%)
  starting transfers between devices  4.19 us (4%)
  local copies, waits for them, and re-layouts  1.57 us (1%)
    ppermute x9, waiting for transfers between devices, move(): return lax.ppermute(block, ('outer', 'inner'), route)  66.5 us
    dot_general x16, matrix products, dot(): lax.dot_general(a, b, (((ca,), (cb,)), ((), ())), precision=HIGH, preferr...  34.7 us
    ppermute x9, starting transfers between devices, move(): return lax.ppermute(block, ('outer', 'inner'), route)  4.19 us
    gt x1, other arithmetic, local_terms(): positive = count_tile > 0  4.14 us
  transfers between devices with their start and end apart: 9, of which 6 were waited for; matrix products, arithmetic and copies ran while one was open for 14% of the time, Pallas kernels for 0%

commit v1 on v0

v1 whole, which is shorter than its diff:
```python
import functools

import jax
import jax.numpy as jnp
from jax import lax
from jax.experimental import pallas as pl
from jax.experimental.pallas import tpu as pltpu
from jax.sharding import PartitionSpec as P

LOG_TOTAL = 17.0
LEARNING = 0.05
CHUNK = 512
f32 = jnp.float32
MIB = 28


def dot(a, b, ca, cb):
    return lax.dot_general(
        a, b, (((ca,), (cb,)), ((), ())), precision=lax.Precision.HIGH, preferred_element_type=f32
    )


def adagrad(value, total, grad):
    total = total + grad * grad
    return value - LEARNING * (grad * lax.rsqrt(total)), total


def fetches(pairs, sems):
    copies = [pltpu.make_async_copy(src, dst, sems.at[i]) for i, (src, dst) in enumerate(pairs)]
    for copy in copies:
        copy.start()
    return copies


def chunks(n):
    return [pl.ds(start, CHUNK) for start in range(0, n, CHUNK)]


def tile_pass(before, x_buf, rows_ref, col_logs, C, W_ref, A_ref, Wo_ref, Ao_ref, after):
    row_logs = jnp.log(rows_ref[...].astype(f32)).T - LOG_TOTAL
    per = CHUNK // row_logs.shape[0]
    grad = None
    for i, rows in enumerate(chunks(x_buf.shape[0])):
        before(i)
        x = x_buf[rows, :]
        positive = x > 0
        m = jnp.maximum(x.astype(f32), 1.0)
        logs = [row_logs[:, j : j + 1] for j in range(i * per, (i + 1) * per)]
        target = (jnp.log(m) - jnp.concatenate(logs, axis=0)) - col_logs
        confidence = 0.1 + 0.25 * (m * lax.rsqrt(m))

        def errors(z):
            gap = z - target
            return jnp.where(positive, confidence * gap, 0.5 * jnp.tanh(0.5 * gap) + 0.5)

        W = W_ref[rows, :]
        g = dot(errors(dot(W, C, 1, 1)), C, 1, 0)
        W, A = adagrad(W, A_ref[rows, :], g)
        Ao_ref[rows, :] = A
        Wo_ref[rows, :] = W
        after(i)
        part = dot(W, errors(dot(W, C, 1, 1)), 0, 0)
        grad = part if grad is None else grad + part
    return grad.T


def first_kernel(
    x_hbm, rows_ref, cols_ref, W_hbm, A_hbm, C_hbm, B_hbm,
    Wo_ref, Ao_ref, Co_ref, Bo_ref, x_buf, W_buf, A_buf, C_buf, B_buf, sems,
):
    n, width = C_buf.shape
    parts = chunks(x_buf.shape[0])
    pairs = [(C_hbm, C_buf)]
    for rows in parts:
        pairs.append((W_hbm.at[rows], W_buf.at[rows]))
        pairs.append((x_hbm.at[0, 0, rows], x_buf.at[rows]))
        pairs.append((A_hbm.at[rows], A_buf.at[rows]))
    pairs.append((B_hbm, B_buf))
    copies = fetches(pairs, sems)
    col_logs = jnp.log(cols_ref[...].astype(f32))
    copies[0].wait()
    C = C_buf[...]

    def before(i):
        for copy in copies[1 + 3 * i : 4 + 3 * i]:
            copy.wait()

    h = tile_pass(
        before, x_buf, rows_ref, col_logs, C, W_buf, A_buf, Wo_ref, Ao_ref, lambda i: None
    )
    copies[-1].wait()
    Co_ref[:n, :], Bo_ref[...] = adagrad(C, B_buf[...], h)
    logs = [jnp.broadcast_to(col_logs[:, i : i + width], (8, width)) for i in range(0, n, width)]
    Co_ref[n:, :] = jnp.concatenate(logs, axis=0)


def step_kernel(step, x_hbm, rows_ref, M_ref, W_ref, A_ref, Wo_ref, Ao_ref, h_ref, x_buf, sems):
    n = h_ref.shape[0]
    parts = chunks(x_buf.shape[0])
    copies = fetches([(x_hbm.at[0, step, rows], x_buf.at[rows]) for rows in parts], sems)
    logs = [M_ref[i : i + 1, :] for i in range(n, M_ref.shape[0], 8)]
    col_logs = jnp.concatenate(logs, axis=1)
    h_ref[...] = tile_pass(
        lambda i: copies[i].wait(), x_buf, rows_ref, col_logs, M_ref[:n, :],
        W_ref, A_ref, Wo_ref, Ao_ref, lambda i: None,
    )


def last_kernel(
    step, x_hbm, rows_ref, M_ref, W_ref, A_ref, Wo_hbm, Ao_hbm, h_ref, x_buf, W_buf, A_buf, sems, out_sems
):
    n = h_ref.shape[0]
    parts = chunks(x_buf.shape[0])
    copies = fetches([(x_hbm.at[0, step, rows], x_buf.at[rows]) for rows in parts], sems)
    logs = [M_ref[i : i + 1, :] for i in range(n, M_ref.shape[0], 8)]
    col_logs = jnp.concatenate(logs, axis=1)
    stores = []

    def after(i):
        rows = parts[i]
        pairs = [(W_buf.at[rows], Wo_hbm.at[rows]), (A_buf.at[rows], Ao_hbm.at[rows])]
        stores.extend(fetches(pairs, out_sems.at[i]))

    h_ref[...] = tile_pass(
        lambda i: copies[i].wait(), x_buf, rows_ref, col_logs, M_ref[:n, :],
        W_ref, A_ref, W_buf, A_buf, after,
    )
    for copy in stores:
        copy.wait()


def update_kernel(h_ref, M_ref, B_ref, Mo_ref, Bo_ref):
    n = h_ref.shape[0]
    C, Bo_ref[...] = adagrad(M_ref[:n, :], B_ref[...], h_ref[...])
    Mo_ref[:n, :] = C
    if Mo_ref.shape[0] > n:
        Mo_ref[n:, :] = M_ref[n:, :]


def call(kernel, operands, spaces, outs, out_spaces, scratch, mib, name):
    return pl.pallas_call(
        kernel,
        in_specs=[pl.BlockSpec(memory_space=s) for s in spaces],
        out_specs=[pl.BlockSpec(memory_space=s) for s in out_spaces],
        out_shape=[jax.ShapeDtypeStruct(s, f32) for s in outs],
        scratch_shapes=scratch,
        compiler_params=pltpu.CompilerParams(vmem_limit_bytes=mib << 20),
        name=name,
    )(*operands)


def body(tile_counts, row_counts, col_counts, row_factors, row_accum, col_factors, col_accum):
    steps = tile_counts.shape[1]
    n_outer, n_inner = lax.axis_size("outer"), lax.axis_size("inner")

    def move(block, across):
        route = [
            (o * n_inner + i, (o + across) % n_outer * n_inner + (i + 1) % n_inner)
            for o in range(n_outer)
            for i in range(n_inner)
        ]
        return lax.ppermute(block, ("outer", "inner"), route)

    rows = row_counts.reshape(-1, 128)
    cols = col_counts.reshape(1, -1)
    wide, tall = row_factors.shape, col_factors.shape
    message = (tall[0] + 8 * (tall[0] // tall[1]), tall[1])
    hbm = [tile_counts, row_factors, row_accum, col_factors, col_accum]
    hbm = [pltpu.with_memory_space_constraint(a, pltpu.HBM) for a in hbm]
    tile_counts, row_factors, row_accum, col_factors, col_accum = hbm
    V, H, DMA = pltpu.VMEM, pltpu.HBM, pltpu.SemaphoreType.DMA
    tile = V(tile_counts.shape[2:], jnp.int32)
    n = wide[0] // CHUNK
    W, A, M, B = call(
        first_kernel,
        (tile_counts, rows, cols, row_factors, row_accum, col_factors, col_accum),
        [H, V, V, H, H, H, H], [wide, wide, message, tall], [V] * 4,
        [tile, V(wide, f32), V(wide, f32), V(tall, f32), V(tall, f32), DMA((3 * n + 2,))],
        MIB, "first",
    )
    for step in range(1, steps):
        across = int(step == steps // 2)
        M = move(M, across)
        B = move(B, across)
        last = step + 1 == steps
        if last:
            kernel, out_space = last_kernel, H
            scratch = [V(wide, f32), V(wide, f32), DMA((n,)), DMA((n, 2))]
        else:
            kernel, out_space, scratch = step_kernel, V, [DMA((n,))]
        W, A, h = call(
            functools.partial(kernel, step), (tile_counts, rows, M, W, A), [H, V, V, V, V],
            [wide, wide, tall], [out_space, out_space, V], [tile] + scratch, MIB, "tile",
        )
        M, B = call(
            update_kernel, (h, M, B), [V] * 3, [tall if last else message, tall], [V] * 2, [], 8, "update"
        )
    return W, A, M, B


def solution(mesh):
    both = ("outer", "inner")
    return jax.shard_map(
        body,
        mesh=mesh,
        in_specs=(P(both, None, None, None), P(both), P(both)) + (P(both, None),) * 4,
        out_specs=(P(both, None),) * 4,
        check_vma=False,
    )
```

time: 113 us -> 81.1 us (0.72)
  matrix products: 34.7 us -> 0 us
  Pallas kernels: 0 us -> 31.6 us
  waiting for transfers between devices: 66.5 us -> 44.6 us
  other arithmetic: 4.84 us -> 0 us
  starting transfers between devices: 4.19 us -> 2.64 us
    dot_general x16 -> x0, matrix products: 34.7 us -> none  [dot(): lax.dot_general(a, b, (((ca,), (cb,)), ((), ())), precision=HIGH, preferr...]
    pallas_call x0 -> x7, Pallas kernels: none -> 31.6 us  [call(): pl.pallas_call(kernel, in_specs=[pl.BlockSpec(memory_space=s) for s in sp...]
    ppermute x9 -> x6, waiting for transfers between devices: 66.5 us -> 44.6 us  [move(): return lax.ppermute(block, ('outer', 'inner'), route)]
    gt x1 -> x0, other arithmetic: 4.14 us -> none  [local_terms(): positive = count_tile > 0]
    ppermute x9 -> x6, starting transfers between devices: 4.19 us -> 2.64 us  [move(): return lax.ppermute(block, ('outer', 'inner'), route)]
  transfers between devices with their start and end apart: 9 -> 6, of which waited for: 6 -> 4; matrix products, arithmetic and copies ran while one was open for 14% -> 0% of each run, Pallas kernels for 0% -> 27%
where the time goes in v1:
time: 81.1 us; the launch traced here: 80.9 us
  waiting for transfers between devices  44.6 us (55%)
  Pallas kernels  31.6 us (39%)
  starting transfers between devices  2.64 us (3%)
  local copies, waits for them, and re-layouts  1.36 us (2%)
    ppermute x6, waiting for transfers between devices, move(): return lax.ppermute(block, ('outer', 'inner'), route)  44.6 us
    pallas_call x7, Pallas kernels, call(): pl.pallas_call(kernel, in_specs=[pl.BlockSpec(memory_space=s) for s in sp...  31.6 us
    ppermute x6, starting transfers between devices, move(): return lax.ppermute(block, ('outer', 'inner'), route)  2.64 us
  transfers between devices with their start and end apart: 6, of which 4 were waited for; matrix products, arithmetic and copies ran while one was open for 0% of the time, Pallas kernels for 27%

profile of v1, /device:TPU:0, one launch (start us, length us, event | category | flops | bytes accessed | tf_op | source)
XLA Modules:
  0.0 80.9 jit_solution(6515711883528209591)
XLA Ops:
  0.6 0.0 copy-start
  0.6 0.7 copy-done
  1.3 0.0 copy-start.1
  1.3 0.7 copy-done.1
  2.0 8.0 %first.1 = (f32[1024,256]{1,0:T(8,128)S(1)}, f32[1024,256]{1,0:T(8,128)S(1)}, f32[528,256]{1,0:T(8,128)S(1)}, f32[512,256]{1,0:T(8,128)S(1)}) custom-call(s32[1,4,1024,512]{3,2,1,0:T(8,128)} %x_hbm.7, s32[8,128]{1,0:T(8,128)S(1)} %bitcast.2, s32[1,512]{1,0:T(1,128)S(1)} %bitcast.6, f32[1024,256]{1,0:T(8,128)} %W_hbm.1, f32[1024,256]{1,0:T(8,128)} %A_hbm.1, ...), custom_call_target="tpu_custom_call" | custom-call | tf_op jit(solution)/shard_map/first/pallas_call | solution.py:141
  10.0 0.1 collective-permute-start
  10.1 1.8 %collective-permute-start.1 = (f32[512,256]{1,0:T(8,128)S(1)}, f32[512,256]{1,0:T(8,128)S(1)}, u32[]{:S(2)}, u32[]{:S(2)}) collective-permute-start(f32[512,256]{1,0:T(8,128)S(1)} %get-tuple-element.27), channel_id=1, source_target_pairs={{0,1},{1,2},{2,3},{3,4},{4,5},{5,6},{6,7},{7,8},{8,9},{9,10},{10,1... | collective-permute-start | bytes 1572872 | tf_op jit(solution)/shard_map/ppermute | solution.py:162
  11.9 12.0 %collective-permute-done.M_ref = f32[528,256]{1,0:T(8,128)S(1)} collective-permute-done((f32[528,256]{1,0:T(8,128)S(1)}, f32[528,256]{1,0:T(8,128)S(1)}, u32[]{:S(2)}, u32[]{:S(2)}) %collective-permute-start) | collective-permute-done | bytes 540704 | tf_op jit(solution)/shard_map/ppermute | solution.py:162
  23.9 7.4 %tile.3 = (f32[1024,256]{1,0:T(8,128)S(1)}, f32[1024,256]{1,0:T(8,128)S(1)}, f32[512,256]{1,0:T(8,128)S(1)}) custom-call(s32[1,4,1024,512]{3,2,1,0:T(8,128)} %x_hbm.7, s32[8,128]{1,0:T(8,128)S(1)} %bitcast.3, f32[528,256]{1,0:T(8,128)S(1)} %collective-permute-done.M_ref, f32[1024,256]{1,0:T(8,128)S(1)} %get-tuple-element.24.W_ref, ...), custom_call_target="tpu_custom_call" | custom-call | tf_op jit(solution)/shard_map/tile/pallas_call | solution.py:141
  31.3 0.0 collective-permute-done.1.B_ref
  31.3 0.2 update.3
  31.5 0.1 collective-permute-start.2
  31.6 0.3 collective-permute-start.3
  31.9 17.9 %collective-permute-done.2.M_ref = f32[528,256]{1,0:T(8,128)S(1)} collective-permute-done((f32[528,256]{1,0:T(8,128)S(1)}, f32[528,256]{1,0:T(8,128)S(1)}, u32[]{:S(2)}, u32[]{:S(2)}) %collective-permute-start.2) | collective-permute-done | bytes 540704 | tf_op jit(solution)/shard_map/ppermute | solution.py:162
  49.8 7.4 %tile.4 = (f32[1024,256]{1,0:T(8,128)S(1)}, f32[1024,256]{1,0:T(8,128)S(1)}, f32[512,256]{1,0:T(8,128)S(1)}) custom-call(s32[1,4,1024,512]{3,2,1,0:T(8,128)} %x_hbm.7, s32[8,128]{1,0:T(8,128)S(1)} %bitcast.4, f32[528,256]{1,0:T(8,128)S(1)} %collective-permute-done.2.M_ref, f32[1024,256]{1,0:T(8,128)S(1)} %get-tuple-element.29.W_ref, ...), custom_call_target="tpu_custom_call" | custom-call | tf_op jit(solution)/shard_map/tile/pallas_call | solution.py:141
  57.2 2.0 %collective-permute-done.3.B_ref = f32[512,256]{1,0:T(8,128)S(1)} collective-permute-done((f32[512,256]{1,0:T(8,128)S(1)}, f32[512,256]{1,0:T(8,128)S(1)}, u32[]{:S(2)}, u32[]{:S(2)}) %collective-permute-start.3) | collective-permute-done | bytes 524320 | tf_op jit(solution)/shard_map/ppermute | solution.py:162
  59.2 0.2 update.4
  59.3 0.1 collective-permute-start.4
  59.4 0.3 collective-permute-start.5
  59.7 12.6 %collective-permute-done.4.M_ref = f32[528,256]{1,0:T(8,128)S(1)} collective-permute-done((f32[528,256]{1,0:T(8,128)S(1)}, f32[528,256]{1,0:T(8,128)S(1)}, u32[]{:S(2)}, u32[]{:S(2)}) %collective-permute-start.4) | collective-permute-done | bytes 540704 | tf_op jit(solution)/shard_map/ppermute | solution.py:162
  72.4 7.4 %tile.5 = (f32[1024,256]{1,0:T(8,128)}, f32[1024,256]{1,0:T(8,128)}, f32[512,256]{1,0:T(8,128)S(1)}) custom-call(s32[1,4,1024,512]{3,2,1,0:T(8,128)} %x_hbm.7, s32[8,128]{1,0:T(8,128)S(1)} %bitcast.5, f32[528,256]{1,0:T(8,128)S(1)} %collective-permute-done.4.M_ref, f32[1024,256]{1,0:T(8,128)S(1)} %get-tuple-element.34.W_ref, ...), custom_call_target="tpu_custom_call" | custom-call | tf_op jit(solution)/shard_map/tile/pallas_call | solution.py:141
  79.8 0.0 collective-permute-done.5.B_ref
  79.8 1.1 %update.5 = (f32[512,256]{1,0:T(8,128)}, f32[512,256]{1,0:T(8,128)}) custom-call(f32[512,256]{1,0:T(8,128)S(1)} %get-tuple-element.38.h_ref, f32[528,256]{1,0:T(8,128)S(1)} %collective-permute-done.4.M_ref, f32[512,256]{1,0:T(8,128)S(1)} %collective-permute-done.5.B_ref), custom_call_target="tpu_custom_call" | custom-call | tf_op jit(solution)/shard_map/update/pallas_call | solution.py:141
Async XLA Ops:
  0.6 0.7 copy-start
  1.3 0.7 copy-start.1
  10.0 13.9 %collective-permute-start = (f32[528,256]{1,0:T(8,128)S(1)}, f32[528,256]{1,0:T(8,128)S(1)}, u32[]{:S(2)}, u32[]{:S(2)}) collective-permute-start(f32[528,256]{1,0:T(8,128)S(1)} %get-tuple-element.23), channel_id=1, source_target_pairs={{0,1},{1,2},{2,3},{3,4},{4,5},{5,6},{6,7},{7,8},{8,9},{9,10},{10,1... | collective-permute-start | bytes 1622024 | tf_op jit(solution)/shard_map/ppermute | solution.py:162
  10.1 21.2 %collective-permute-start.1 = (f32[512,256]{1,0:T(8,128)S(1)}, f32[512,256]{1,0:T(8,128)S(1)}, u32[]{:S(2)}, u32[]{:S(2)}) collective-permute-start(f32[512,256]{1,0:T(8,128)S(1)} %get-tuple-element.27), channel_id=1, source_target_pairs={{0,1},{1,2},{2,3},{3,4},{4,5},{5,6},{6,7},{7,8},{8,9},{9,10},{10,1... | collective-permute-start | bytes 1572872 | tf_op jit(solution)/shard_map/ppermute | solution.py:162
  31.5 18.3 %collective-permute-start.2 = (f32[528,256]{1,0:T(8,128)S(1)}, f32[528,256]{1,0:T(8,128)S(1)}, u32[]{:S(2)}, u32[]{:S(2)}) collective-permute-start(f32[528,256]{1,0:T(8,128)S(1)} %get-tuple-element.28), channel_id=1, source_target_pairs={{0,65},{1,66},{2,67},{3,68},{4,69},{5,70},{6,71},{7,72},{8,73},{9,... | collective-permute-start | bytes 1622024 | tf_op jit(solution)/shard_map/ppermute | solution.py:162
  31.6 27.6 %collective-permute-start.3 = (f32[512,256]{1,0:T(8,128)S(1)}, f32[512,256]{1,0:T(8,128)S(1)}, u32[]{:S(2)}, u32[]{:S(2)}) collective-permute-start(f32[512,256]{1,0:T(8,128)S(1)} %get-tuple-element.32), channel_id=1, source_target_pairs={{0,65},{1,66},{2,67},{3,68},{4,69},{5,70},{6,71},{7,72},{8,73},{9,... | collective-permute-start | bytes 1572872 | tf_op jit(solution)/shard_map/ppermute | solution.py:162
  59.3 13.1 %collective-permute-start.4 = (f32[528,256]{1,0:T(8,128)S(1)}, f32[528,256]{1,0:T(8,128)S(1)}, u32[]{:S(2)}, u32[]{:S(2)}) collective-permute-start(f32[528,256]{1,0:T(8,128)S(1)} %get-tuple-element.33), channel_id=1, source_target_pairs={{0,1},{1,2},{2,3},{3,4},{4,5},{5,6},{6,7},{7,8},{8,9},{9,10},{10,1... | collective-permute-start | bytes 1622024 | tf_op jit(solution)/shard_map/ppermute | solution.py:162
  59.4 20.4 %collective-permute-start.5 = (f32[512,256]{1,0:T(8,128)S(1)}, f32[512,256]{1,0:T(8,128)S(1)}, u32[]{:S(2)}, u32[]{:S(2)}) collective-permute-start(f32[512,256]{1,0:T(8,128)S(1)} %get-tuple-element.39), channel_id=1, source_target_pairs={{0,1},{1,2},{2,3},{3,4},{4,5},{5,6},{6,7},{7,8},{8,9},{9,10},{10,1... | collective-permute-start | bytes 1572872 | tf_op jit(solution)/shard_map/ppermute | solution.py:162

commit v2 on v0

v2 whole, which is shorter than its diff:
```python
import functools

import jax
import jax.numpy as jnp
from jax import lax
from jax.experimental import pallas as pl
from jax.experimental.pallas import tpu as pltpu
from jax.sharding import PartitionSpec as P

LOG_TOTAL = 17.0
LEARNING = 0.05
HALVES = 2
f32 = jnp.float32
V, H, DMA = pltpu.VMEM, pltpu.HBM, pltpu.SemaphoreType.DMA


def dot(a, b, ca, cb):
    return lax.dot_general(
        a, b, (((ca,), (cb,)), ((), ())), precision=lax.Precision.HIGH, preferred_element_type=f32
    )


def adagrad(value, total, grad):
    total = total + grad * grad
    return value - LEARNING * (grad * lax.rsqrt(total)), total


def fetches(pairs, sems):
    copies = [pltpu.make_async_copy(src, dst, sems.at[i]) for i, (src, dst) in enumerate(pairs)]
    for copy in copies:
        copy.start()
    return copies


def row_spans(n, size):
    return [pl.ds(start, size) for start in range(0, n, size)]


def put_terms(x, row_logs, first, t_ref, c_ref, rows):
    m = jnp.maximum(x.astype(f32), 1.0)
    lanes = row_logs.shape[0]
    logs = [row_logs[:, j : j + 1] for j in range(first, first + x.shape[0] // lanes)]
    t_ref[rows, :] = jnp.log(m) - jnp.concatenate(logs, axis=0)
    c_ref[rows, :] = jnp.where(x > 0, 0.1 + 0.25 * (m * lax.rsqrt(m)), 0.0)


def errors(z, target, confidence, col_logs):
    gap = (z - target) + col_logs
    return jnp.where(confidence > 0.0, confidence * gap, 0.5 * jnp.tanh(0.5 * gap) + 0.5)


def shifted_row_logs(rows_ref):
    return jnp.log(rows_ref[...].astype(f32)).T - LOG_TOTAL


def terms_kernel(step, x_hbm, rows_ref, t_ref, c_ref, x_buf, sems):
    spans = row_spans(x_buf.shape[0], 256)
    copies = fetches([(x_hbm.at[0, step, rows], x_buf.at[rows]) for rows in spans], sems)
    row_logs = shifted_row_logs(rows_ref)
    for i, rows in enumerate(spans):
        copies[i].wait()
        put_terms(x_buf[rows, :], row_logs, 2 * i, t_ref, c_ref, rows)


def first_kernel(
    x_hbm, rows_hbm, cols_hbm, W_hbm, A_hbm, C_hbm, B_hbm,
    Wo_ref, Ao_ref, t_ref, c_ref, *rest,
):
    M_refs, B_refs = rest[:HALVES], rest[HALVES : 2 * HALVES]
    x_buf, W_buf, A_buf, rows_buf, cols_buf, sems, out_sems = rest[2 * HALVES :]
    n, width = B_refs[0].shape
    spans = row_spans(x_buf.shape[0], 512)
    pairs = [(cols_hbm, cols_buf), (rows_hbm, rows_buf)]
    pairs += [(C_hbm.at[pl.ds(j * n, n)], M_refs[j].at[pl.ds(0, n)]) for j in range(HALVES)]
    head = len(pairs)
    for rows in spans:
        pairs.append((W_hbm.at[rows], W_buf.at[rows]))
        pairs.append((x_hbm.at[0, 0, rows], x_buf.at[rows]))
        pairs.append((A_hbm.at[rows], A_buf.at[rows]))
    copies = fetches(pairs, sems)
    late = fetches([(B_hbm.at[pl.ds(j * n, n)], B_refs[j]) for j in range(HALVES)], out_sems)
    for copy in copies[:head]:
        copy.wait()
    col_logs = jnp.log(cols_buf[...].astype(f32))
    row_logs = shifted_row_logs(rows_buf)
    for j in range(HALVES):
        M_refs[j][n:, :] = jnp.broadcast_to(col_logs[:, j * n : (j + 1) * n], (8, width))
    C = jnp.concatenate([ref[:n, :] for ref in M_refs], axis=0)
    for i, rows in enumerate(spans):
        for copy in copies[head + 3 * i : head + 3 * i + 3]:
            copy.wait()
        put_terms(x_buf[rows, :], row_logs, 4 * i, t_ref, c_ref, rows)
        W = W_buf[rows, :]
        e = errors(dot(W, C, 1, 1), t_ref[rows, :], c_ref[rows, :], col_logs)
        Wo_ref[rows, :], Ao_ref[rows, :] = adagrad(W, A_buf[rows, :], dot(e, C, 1, 0))
    for copy in late:
        copy.wait()


def half_errors(j, W, t_ref, c_ref, M_ref, rows):
    n = M_ref.shape[1]
    cols = pl.ds(j * n, n)
    C = M_ref[:n, :]
    e = errors(dot(W, C, 1, 1), t_ref[rows, cols], c_ref[rows, cols], M_ref[n : n + 1, :])
    return e, C


def row_part_kernel(j, t_ref, c_ref, M_ref, W_ref, g_ref):
    for rows in row_spans(W_ref.shape[0], 512):
        e, C = half_errors(j, W_ref[rows, :], t_ref, c_ref, M_ref, rows)
        g_ref[rows, :] = dot(e, C, 1, 0)


def row_last_kernel(j, t_ref, c_ref, M_ref, W_ref, A_ref, g_ref, Wo_ref, Ao_ref):
    for rows in row_spans(W_ref.shape[0], 512):
        W = W_ref[rows, :]
        e, C = half_errors(j, W, t_ref, c_ref, M_ref, rows)
        g = g_ref[rows, :] + dot(e, C, 1, 0)
        Wo_ref[rows, :], Ao_ref[rows, :] = adagrad(W, A_ref[rows, :], g)


def col_kernel(j, t_ref, c_ref, M_ref, W_ref, h_ref):
    grad = None
    for rows in row_spans(W_ref.shape[0], 512):
        W = W_ref[rows, :]
        e, _ = half_errors(j, W, t_ref, c_ref, M_ref, rows)
        part = dot(W, e, 0, 0)
        grad = part if grad is None else grad + part
    h_ref[...] = grad.T


def col_store_kernel(j, t_ref, c_ref, M_ref, W_ref, A_ref, h_ref, Wo_hbm, Ao_hbm, sems):
    copies = fetches([(W_ref, Wo_hbm), (A_ref, Ao_hbm)], sems)
    col_kernel(j, t_ref, c_ref, M_ref, W_ref, h_ref)
    for copy in copies:
        copy.wait()


def update_kernel(h_ref, M_ref, B_ref, Mo_ref, Bo_ref):
    n = h_ref.shape[0]
    Mo_ref[:n, :], Bo_ref[...] = adagrad(M_ref[:n, :], B_ref[...], h_ref[...])
    Mo_ref[n:, :] = M_ref[n:, :]


def final_kernel(*refs):
    ins, (Co_ref, Bo_ref) = refs[:-2], refs[-2:]
    n = ins[0].shape[0]
    for j in range(HALVES):
        h_ref, M_ref, B_ref = ins[3 * j : 3 * j + 3]
        rows = pl.ds(j * n, n)
        Co_ref[rows, :], Bo_ref[rows, :] = adagrad(M_ref[:n, :], B_ref[...], h_ref[...])


def call(kernel, operands, spaces, outs, out_spaces, scratch, mib, name):
    return pl.pallas_call(
        kernel,
        in_specs=[pl.BlockSpec(memory_space=s) for s in spaces],
        out_specs=[pl.BlockSpec(memory_space=s) for s in out_spaces],
        out_shape=[jax.ShapeDtypeStruct(s, f32) for s in outs],
        scratch_shapes=scratch,
        compiler_params=pltpu.CompilerParams(vmem_limit_bytes=mib << 20),
        name=name,
    )(*operands)


def body(tile_counts, row_counts, col_counts, row_factors, row_accum, col_factors, col_accum):
    steps = tile_counts.shape[1]
    n_outer, n_inner = lax.axis_size("outer"), lax.axis_size("inner")

    def move(block, across):
        route = [
            (o * n_inner + i, (o + across) % n_outer * n_inner + (i + 1) % n_inner)
            for o in range(n_outer)
            for i in range(n_inner)
        ]
        return lax.ppermute(block, ("outer", "inner"), route)

    rows = row_counts.reshape(-1, 128)
    cols = col_counts.reshape(1, -1)
    hbm = [tile_counts, rows, cols, row_factors, row_accum, col_factors, col_accum]
    hbm = [pltpu.with_memory_space_constraint(a, H) for a in hbm]
    wide, tall = row_factors.shape, col_factors.shape
    tile = tile_counts.shape[2:]
    half = (tall[0] // HALVES, tall[1])
    message = (half[0] + 8, half[1])
    W, A, t, c, *blocks = call(
        first_kernel, hbm, [H] * 7,
        [wide, wide, tile, tile] + [message] * HALVES + [half] * HALVES, [V] * (4 + 2 * HALVES),
        [V(tile, jnp.int32), V(wide, f32), V(wide, f32), V(rows.shape, jnp.int32),
         V(cols.shape, jnp.int32), DMA((4 + 3 * 2,)), DMA((HALVES,))],
        24, "first",
    )
    M, B = blocks[:HALVES], blocks[HALVES:]
    for step in range(steps):
        if step > 0:
            part = call(
                functools.partial(row_part_kernel, 0), (t, c, M[0], W), [V] * 4, [wide], [V], [], 12, "row0"
            )[0]
            W, A = call(
                functools.partial(row_last_kernel, 1), (t, c, M[1], W, A, part), [V] * 6,
                [wide, wide], [V] * 2, [], 12, "row1",
            )
        if step + 1 == steps:
            break
        across = int(step + 1 == steps // 2)
        sent, sums = [], []
        for j in range(HALVES):
            h = call(functools.partial(col_kernel, j), (t, c, M[j], W), [V] * 4, [half], [V], [], 12, "col%d" % j)[0]
            value, total = call(
                update_kernel, (h, M[j], B[j]), [V] * 3, [message, half], [V] * 2, [], 4, "update%d" % j
            )
            sent.append(move(value, across))
            sums.append(total)
        row_tie = lax.optimization_barrier((rows, *sums))[0]
        t, c = call(
            functools.partial(terms_kernel, step + 1), (hbm[0], row_tie), [H, V], [tile, tile], [V] * 2,
            [V(tile, jnp.int32), DMA((4,))], 12, "terms",
        )
        M, B = sent, [move(total, across) for total in sums]
    h0, W_out, A_out = call(
        functools.partial(col_store_kernel, 0), (t, c, M[0], W, A), [V] * 5, [half, wide, wide], [V, H, H],
        [DMA((2,))], 12, "col0",
    )
    h1 = call(functools.partial(col_kernel, 1), (t, c, M[1], W), [V] * 4, [half], [V], [], 12, "col1")[0]
    C, B = call(final_kernel, (h0, M[0], B[0], h1, M[1], B[1]), [V] * 6, [tall, tall], [V] * 2, [], 6, "final")
    return W_out, A_out, C, B


def solution(mesh):
    both = ("outer", "inner")
    return jax.shard_map(
        body,
        mesh=mesh,
        in_specs=(P(both, None, None, None), P(both), P(both)) + (P(both, None),) * 4,
        out_specs=(P(both, None),) * 4,
        check_vma=False,
    )
```

time: 113 us -> 71.6 us (0.63)
  waiting for transfers between devices: 66.5 us -> 22.4 us
  Pallas kernels: 0 us -> 40.9 us
  matrix products: 34.7 us -> 0 us
  other arithmetic: 4.84 us -> 0 us
  starting transfers between devices: 4.19 us -> 7.19 us
  local copies, waits for them, and re-layouts: 1.57 us -> 0.01 us
    ppermute x9 -> x12, waiting for transfers between devices: 66.5 us -> 22.4 us  [move(): return lax.ppermute(block, ('outer', 'inner'), route)]
    pallas_call x0 -> x25, Pallas kernels: none -> 40.9 us  [call(): pl.pallas_call(kernel, in_specs=[pl.BlockSpec(memory_space=s) for s in sp...]
    dot_general x16 -> x0, matrix products: 34.7 us -> none  [dot(): lax.dot_general(a, b, (((ca,), (cb,)), ((), ())), precision=HIGH, preferr...]
    gt x1 -> x0, other arithmetic: 4.14 us -> none  [local_terms(): positive = count_tile > 0]
    ppermute x9 -> x12, starting transfers between devices: 4.19 us -> 7.19 us  [move(): return lax.ppermute(block, ('outer', 'inner'), route)]
    unnamed x14 -> x2, local copies, waits for them, and re-layouts: 1.57 us -> 0.01 us
  transfers between devices with their start and end apart: 9 -> 12, of which waited for: 6 -> 8; matrix products, arithmetic and copies ran while one was open for 14% -> 0% of each run, Pallas kernels for 0% -> 45%
where the time goes in v2:
time: 71.6 us; the launch traced here: 71.4 us
  Pallas kernels  40.9 us (57%)
  waiting for transfers between devices  22.4 us (31%)
  starting transfers between devices  7.19 us (10%)
  between operations  0.89 us (1%)
    pallas_call x25, Pallas kernels, call(): pl.pallas_call(kernel, in_specs=[pl.BlockSpec(memory_space=s) for s in sp...  40.9 us
    ppermute x12, waiting for transfers between devices, move(): return lax.ppermute(block, ('outer', 'inner'), route)  22.4 us
    ppermute x12, starting transfers between devices, move(): return lax.ppermute(block, ('outer', 'inner'), route)  7.19 us
  transfers between devices with their start and end apart: 12, of which 8 were waited for; matrix products, arithmetic and copies ran while one was open for 0% of the time, Pallas kernels for 45%

profile of v2, /device:TPU:0, one launch (start us, length us, event | category | flops | bytes accessed | tf_op | source)
XLA Modules:
  0.0 71.4 jit_solution(17524725374919700341)
XLA Ops:
  0.6 5.2 %first.1 = (f32[1024,256]{1,0:T(8,128)S(1)}, f32[1024,256]{1,0:T(8,128)S(1)}, f32[1024,512]{1,0:T(8,128)S(1)}, f32[1024,512]{1,0:T(8,128)S(1)}, f32[264,256]{1,0...) custom-call(s32[1,4,1024,512]{3,2,1,0:T(8,128)} %x_hbm.7, ...), custom_call_target="tpu_custom_call" | custom-call | tf_op jit(solution)/shard_map/first/pallas_call | solution.py:155
  5.9 2.1 %col0.4.h_ref = f32[256,256]{1,0:T(8,128)S(1)} custom-call(f32[1024,512]{1,0:T(8,128)S(1)} %get-tuple-element.44.t_ref, f32[1024,512]{1,0:T(8,128)S(1)} %get-tuple-element.45.c_ref, f32[264,256]{1,0:T(8,128)S(1)} %get-tuple-element.46.M_ref, f32[1024,256]{1,0:T(8,128)S(1)} %get-tuple-element.47.W_ref), custom_call_target="tpu_custom_call" | custom-call | tf_op jit(solution)/shard_map/col0/pallas_call | solution.py:155
  8.1 2.1 %col1.4.h_ref = f32[256,256]{1,0:T(8,128)S(1)} custom-call(f32[1024,512]{1,0:T(8,128)S(1)} %get-tuple-element.44.t_ref, f32[1024,512]{1,0:T(8,128)S(1)} %get-tuple-element.45.c_ref, f32[264,256]{1,0:T(8,128)S(1)} %get-tuple-element.50.M_ref, f32[1024,256]{1,0:T(8,128)S(1)} %get-tuple-element.47.W_ref), custom_call_target="tpu_custom_call" | custom-call | tf_op jit(solution)/shard_map/col1/pallas_call | solution.py:155
  10.2 1.8 %collective-permute-start.1 = (f32[264,256]{1,0:T(8,128)S(1)}, f32[264,256]{1,0:T(8,128)S(1)}, u32[]{:S(2)}, u32[]{:S(2)}) collective-permute-start(f32[264,256]{1,0:T(8,128)S(1)} %get-tuple-element.57), channel_id=1, source_target_pairs={{0,1},{1,2},{2,3},{3,4},{4,5},{5,6},{6,7},{7,8},{8,9},{9,10},{10,1... | collective-permute-start | bytes 811016 | tf_op jit(solution)/shard_map/ppermute | solution.py:176
  13.6 1.9 %terms.3 = (f32[1024,512]{1,0:T(8,128)S(1)}, f32[1024,512]{1,0:T(8,128)S(1)}) custom-call(s32[1,4,1024,512]{3,2,1,0:T(8,128)} %x_hbm.7, s32[8,128]{1,0:T(8,128)S(1)} %bitcast.3), custom_call_target="tpu_custom_call" | custom-call | tf_op jit(solution)/shard_map/terms/pallas_call | solution.py:155
  15.5 3.5 %collective-permute-done.M_ref = f32[264,256]{1,0:T(8,128)S(1)} collective-permute-done((f32[264,256]{1,0:T(8,128)S(1)}, f32[264,256]{1,0:T(8,128)S(1)}, u32[]{:S(2)}, u32[]{:S(2)}) %collective-permute-start) | collective-permute-done | bytes 270368 | tf_op jit(solution)/shard_map/ppermute | solution.py:176
  19.0 1.9 %row0.3.g_ref = f32[1024,256]{1,0:T(8,128)S(1)} custom-call(f32[1024,512]{1,0:T(8,128)S(1)} %get-tuple-element.54.t_ref, f32[1024,512]{1,0:T(8,128)S(1)} %get-tuple-element.55.c_ref, f32[264,256]{1,0:T(8,128)S(1)} %collective-permute-done.M_ref, f32[1024,256]{1,0:T(8,128)S(1)} %get-tuple-element.47.W_ref), custom_call_target="tpu_custom_call" | custom-call | tf_op jit(solution)/shard_map/row0/pallas_call | solution.py:155
  21.9 1.9 %row1.3 = (f32[1024,256]{1,0:T(8,128)S(1)}, f32[1024,256]{1,0:T(8,128)S(1)}) custom-call(f32[1024,512]{1,0:T(8,128)S(1)} %get-tuple-element.54.t_ref, f32[1024,512]{1,0:T(8,128)S(1)} %get-tuple-element.55.c_ref, f32[264,256]{1,0:T(8,128)S(1)} %collective-permute-done.1.M_ref, f32[1024,256]{1,0:T(8,128)S(1)} %get-tuple-element.47.W_ref, ...), custom_call_target="tpu_custom_call" | custom-call | tf_op jit(solution)/shard_map/row1/pallas_call | solution.py:155
  23.8 2.1 %col0.5.h_ref = f32[256,256]{1,0:T(8,128)S(1)} custom-call(f32[1024,512]{1,0:T(8,128)S(1)} %get-tuple-element.54.t_ref, f32[1024,512]{1,0:T(8,128)S(1)} %get-tuple-element.55.c_ref, f32[264,256]{1,0:T(8,128)S(1)} %collective-permute-done.M_ref, f32[1024,256]{1,0:T(8,128)S(1)} %get-tuple-element.59.W_ref), custom_call_target="tpu_custom_call" | custom-call | tf_op jit(solution)/shard_map/col0/pallas_call | solution.py:155
  26.1 2.1 %col1.5.h_ref = f32[256,256]{1,0:T(8,128)S(1)} custom-call(f32[1024,512]{1,0:T(8,128)S(1)} %get-tuple-element.54.t_ref, f32[1024,512]{1,0:T(8,128)S(1)} %get-tuple-element.55.c_ref, f32[264,256]{1,0:T(8,128)S(1)} %collective-permute-done.1.M_ref, f32[1024,256]{1,0:T(8,128)S(1)} %get-tuple-element.59.W_ref), custom_call_target="tpu_custom_call" | custom-call | tf_op jit(solution)/shard_map/col1/pallas_call | solution.py:155
  30.9 1.9 %terms.4 = (f32[1024,512]{1,0:T(8,128)S(1)}, f32[1024,512]{1,0:T(8,128)S(1)}) custom-call(s32[1,4,1024,512]{3,2,1,0:T(8,128)} %x_hbm.7, s32[8,128]{1,0:T(8,128)S(1)} %bitcast.4), custom_call_target="tpu_custom_call" | custom-call | tf_op jit(solution)/shard_map/terms/pallas_call | solution.py:155
  32.8 6.8 %collective-permute-done.4.M_ref = f32[264,256]{1,0:T(8,128)S(1)} collective-permute-done((f32[264,256]{1,0:T(8,128)S(1)}, f32[264,256]{1,0:T(8,128)S(1)}, u32[]{:S(2)}, u32[]{:S(2)}) %collective-permute-start.4) | collective-permute-done | bytes 270368 | tf_op jit(solution)/shard_map/ppermute | solution.py:176
  39.6 1.9 %row0.4.g_ref = f32[1024,256]{1,0:T(8,128)S(1)} custom-call(f32[1024,512]{1,0:T(8,128)S(1)} %get-tuple-element.63.t_ref, f32[1024,512]{1,0:T(8,128)S(1)} %get-tuple-element.64.c_ref, f32[264,256]{1,0:T(8,128)S(1)} %collective-permute-done.4.M_ref, f32[1024,256]{1,0:T(8,128)S(1)} %get-tuple-element.59.W_ref), custom_call_target="tpu_custom_call" | custom-call | tf_op jit(solution)/shard_map/row0/pallas_call | solution.py:155
  41.5 2.9 %collective-permute-done.5.M_ref = f32[264,256]{1,0:T(8,128)S(1)} collective-permute-done((f32[264,256]{1,0:T(8,128)S(1)}, f32[264,256]{1,0:T(8,128)S(1)}, u32[]{:S(2)}, u32[]{:S(2)}) %collective-permute-start.5) | collective-permute-done | bytes 270368 | tf_op jit(solution)/shard_map/ppermute | solution.py:176
  44.4 2.0 %row1.4 = (f32[1024,256]{1,0:T(8,128)S(1)}, f32[1024,256]{1,0:T(8,128)S(1)}) custom-call(f32[1024,512]{1,0:T(8,128)S(1)} %get-tuple-element.63.t_ref, f32[1024,512]{1,0:T(8,128)S(1)} %get-tuple-element.64.c_ref, f32[264,256]{1,0:T(8,128)S(1)} %collective-permute-done.5.M_ref, f32[1024,256]{1,0:T(8,128)S(1)} %get-tuple-element.59.W_ref, ...), custom_call_target="tpu_custom_call" | custom-call | tf_op jit(solution)/shard_map/row1/pallas_call | solution.py:155
  46.4 2.1 %col0.6.h_ref = f32[256,256]{1,0:T(8,128)S(1)} custom-call(f32[1024,512]{1,0:T(8,128)S(1)} %get-tuple-element.63.t_ref, f32[1024,512]{1,0:T(8,128)S(1)} %get-tuple-element.64.c_ref, f32[264,256]{1,0:T(8,128)S(1)} %collective-permute-done.4.M_ref, f32[1024,256]{1,0:T(8,128)S(1)} %get-tuple-element.68.W_ref), custom_call_target="tpu_custom_call" | custom-call | tf_op jit(solution)/shard_map/col0/pallas_call | solution.py:155
  49.8 2.1 %col1.6.h_ref = f32[256,256]{1,0:T(8,128)S(1)} custom-call(f32[1024,512]{1,0:T(8,128)S(1)} %get-tuple-element.63.t_ref, f32[1024,512]{1,0:T(8,128)S(1)} %get-tuple-element.64.c_ref, f32[264,256]{1,0:T(8,128)S(1)} %collective-permute-done.5.M_ref, f32[1024,256]{1,0:T(8,128)S(1)} %get-tuple-element.68.W_ref), custom_call_target="tpu_custom_call" | custom-call | tf_op jit(solution)/shard_map/col1/pallas_call | solution.py:155
  54.3 1.9 %terms.5 = (f32[1024,512]{1,0:T(8,128)S(1)}, f32[1024,512]{1,0:T(8,128)S(1)}) custom-call(s32[1,4,1024,512]{3,2,1,0:T(8,128)} %x_hbm.7, s32[8,128]{1,0:T(8,128)S(1)} %bitcast.5), custom_call_target="tpu_custom_call" | custom-call | tf_op jit(solution)/shard_map/terms/pallas_call | solution.py:155
  56.2 3.1 %collective-permute-done.8.M_ref.refs_1_ = f32[264,256]{1,0:T(8,128)S(1)} collective-permute-done((f32[264,256]{1,0:T(8,128)S(1)}, f32[264,256]{1,0:T(8,128)S(1)}, u32[]{:S(2)}, u32[]{:S(2)}) %collective-permute-start.8) | collective-permute-done | bytes 270368 | tf_op jit(solution)/shard_map/ppermute | solution.py:176
  59.3 1.9 %row0.5.g_ref = f32[1024,256]{1,0:T(8,128)S(1)} custom-call(f32[1024,512]{1,0:T(8,128)S(1)} %get-tuple-element.72.t_ref, f32[1024,512]{1,0:T(8,128)S(1)} %get-tuple-element.73.c_ref, f32[264,256]{1,0:T(8,128)S(1)} %collective-permute-done.8.M_ref.refs_1_, f32[1024,256]{1,0:T(8,128)S(1)} %get-tuple-element.68.W_ref), custom_call_target="tpu_custom_call" | custom-call | tf_op jit(solution)/shard_map/row0/pallas_call | solution.py:155
  61.2 2.8 %collective-permute-done.9.M_ref.refs_4_ = f32[264,256]{1,0:T(8,128)S(1)} collective-permute-done((f32[264,256]{1,0:T(8,128)S(1)}, f32[264,256]{1,0:T(8,128)S(1)}, u32[]{:S(2)}, u32[]{:S(2)}) %collective-permute-start.9) | collective-permute-done | bytes 270368 | tf_op jit(solution)/shard_map/ppermute | solution.py:176
  64.0 2.0 %row1.5 = (f32[1024,256]{1,0:T(8,128)S(1)}, f32[1024,256]{1,0:T(8,128)S(1)}) custom-call(f32[1024,512]{1,0:T(8,128)S(1)} %get-tuple-element.72.t_ref, f32[1024,512]{1,0:T(8,128)S(1)} %get-tuple-element.73.c_ref, f32[264,256]{1,0:T(8,128)S(1)} %collective-permute-done.9.M_ref.refs_4_, f32[1024,256]{1,0:T(8,128)S(1)} %get-tuple-element.68.W_ref, ...), custom_call_target="tpu_custom_call" | custom-call | tf_op jit(solution)/shard_map/row1/pallas_call | solution.py:155
  66.0 2.1 %col1.7.refs_3_ = f32[256,256]{1,0:T(8,128)S(1)} custom-call(f32[1024,512]{1,0:T(8,128)S(1)} %get-tuple-element.72.t_ref, f32[1024,512]{1,0:T(8,128)S(1)} %get-tuple-element.73.c_ref, f32[264,256]{1,0:T(8,128)S(1)} %collective-permute-done.9.M_ref.refs_4_, f32[1024,256]{1,0:T(8,128)S(1)} %get-tuple-element.77.W_ref), custom_call_target="tpu_custom_call" | custom-call | tf_op jit(solution)/shard_map/col1/pallas_call | solution.py:155
  68.1 2.1 %col0.7 = (f32[256,256]{1,0:T(8,128)S(1)}, f32[1024,256]{1,0:T(8,128)}, f32[1024,256]{1,0:T(8,128)}) custom-call(f32[1024,512]{1,0:T(8,128)S(1)} %get-tuple-element.72.t_ref, f32[1024,512]{1,0:T(8,128)S(1)} %get-tuple-element.73.c_ref, f32[264,256]{1,0:T(8,128)S(1)} %collective-permute-done.8.M_ref.refs_1_, f32[1024,256]{1,0:T(8,128)S(1)} %get-tuple-element.77.W_ref, ...), custom_call_target="tpu_custom_call" | custom-call | tf_op jit(solution)/shard_map/col0/pallas_call | solution.py:155
  (27 shorter events, 10.2 us)
Async XLA Ops:
  8.0 11.0 %collective-permute-start = (f32[264,256]{1,0:T(8,128)S(1)}, f32[264,256]{1,0:T(8,128)S(1)}, u32[]{:S(2)}, u32[]{:S(2)}) collective-permute-start(f32[264,256]{1,0:T(8,128)S(1)} %get-tuple-element.56), channel_id=1, source_target_pairs={{0,1},{1,2},{2,3},{3,4},{4,5},{5,6},{6,7},{7,8},{8,9},{9,10},{10,1... | collective-permute-start | bytes 811016 | tf_op jit(solution)/shard_map/ppermute | solution.py:176
  8.1 5.5 %copy-start = (s32[1024]{0:T(1024)S(1)}, s32[1024]{0:T(1024)}, u32[]{:S(2)}) copy-start(s32[1024]{0:T(1024)} %param.8) | copy-start | bytes 12292
  10.2 11.7 %collective-permute-start.1 = (f32[264,256]{1,0:T(8,128)S(1)}, f32[264,256]{1,0:T(8,128)S(1)}, u32[]{:S(2)}, u32[]{:S(2)}) collective-permute-start(f32[264,256]{1,0:T(8,128)S(1)} %get-tuple-element.57), channel_id=1, source_target_pairs={{0,1},{1,2},{2,3},{3,4},{4,5},{5,6},{6,7},{7,8},{8,9},{9,10},{10,1... | collective-permute-start | bytes 811016 | tf_op jit(solution)/shard_map/ppermute | solution.py:176
  12.1 13.9 %collective-permute-start.2 = (f32[256,256]{1,0:T(8,128)S(1)}, f32[256,256]{1,0:T(8,128)S(1)}, u32[]{:S(2)}, u32[]{:S(2)}) collective-permute-start(f32[256,256]{1,0:T(8,128)S(1)} %get-tuple-element.49), channel_id=1, source_target_pairs={{0,1},{1,2},{2,3},{3,4},{4,5},{5,6},{6,7},{7,8},{8,9},{9,10},{10,1... | collective-permute-start | bytes 786440 | tf_op jit(solution)/shard_map/ppermute | solution.py:176
  12.2 16.1 %collective-permute-start.3 = (f32[256,256]{1,0:T(8,128)S(1)}, f32[256,256]{1,0:T(8,128)S(1)}, u32[]{:S(2)}, u32[]{:S(2)}) collective-permute-start(f32[256,256]{1,0:T(8,128)S(1)} %get-tuple-element.52), channel_id=1, source_target_pairs={{0,1},{1,2},{2,3},{3,4},{4,5},{5,6},{6,7},{7,8},{8,9},{9,10},{10,1... | collective-permute-start | bytes 786440 | tf_op jit(solution)/shard_map/ppermute | solution.py:176
  26.1 13.6 %collective-permute-start.4 = (f32[264,256]{1,0:T(8,128)S(1)}, f32[264,256]{1,0:T(8,128)S(1)}, u32[]{:S(2)}, u32[]{:S(2)}) collective-permute-start(f32[264,256]{1,0:T(8,128)S(1)} %get-tuple-element.65), channel_id=1, source_target_pairs={{0,65},{1,66},{2,67},{3,68},{4,69},{5,70},{6,71},{7,72},{8,73},{9,... | collective-permute-start | bytes 811016 | tf_op jit(solution)/shard_map/ppermute | solution.py:176
  28.4 16.0 %collective-permute-start.5 = (f32[264,256]{1,0:T(8,128)S(1)}, f32[264,256]{1,0:T(8,128)S(1)}, u32[]{:S(2)}, u32[]{:S(2)}) collective-permute-start(f32[264,256]{1,0:T(8,128)S(1)} %get-tuple-element.66), channel_id=1, source_target_pairs={{0,65},{1,66},{2,67},{3,68},{4,69},{5,70},{6,71},{7,72},{8,73},{9,... | collective-permute-start | bytes 811016 | tf_op jit(solution)/shard_map/ppermute | solution.py:176
  28.5 20.6 %collective-permute-start.6 = (f32[256,256]{1,0:T(8,128)S(1)}, f32[256,256]{1,0:T(8,128)S(1)}, u32[]{:S(2)}, u32[]{:S(2)}) collective-permute-start(f32[256,256]{1,0:T(8,128)S(1)} %get-tuple-element.60), channel_id=1, source_target_pairs={{0,65},{1,66},{2,67},{3,68},{4,69},{5,70},{6,71},{7,72},{8,73},{9,... | collective-permute-start | bytes 786440 | tf_op jit(solution)/shard_map/ppermute | solution.py:176
  29.3 24.5 %collective-permute-start.7 = (f32[256,256]{1,0:T(8,128)S(1)}, f32[256,256]{1,0:T(8,128)S(1)}, u32[]{:S(2)}, u32[]{:S(2)}) collective-permute-start(f32[256,256]{1,0:T(8,128)S(1)} %get-tuple-element.61), channel_id=1, source_target_pairs={{0,65},{1,66},{2,67},{3,68},{4,69},{5,70},{6,71},{7,72},{8,73},{9,... | collective-permute-start | bytes 786440 | tf_op jit(solution)/shard_map/ppermute | solution.py:176
  49.1 10.2 %collective-permute-start.8 = (f32[264,256]{1,0:T(8,128)S(1)}, f32[264,256]{1,0:T(8,128)S(1)}, u32[]{:S(2)}, u32[]{:S(2)}) collective-permute-start(f32[264,256]{1,0:T(8,128)S(1)} %get-tuple-element.74), channel_id=1, source_target_pairs={{0,1},{1,2},{2,3},{3,4},{4,5},{5,6},{6,7},{7,8},{8,9},{9,10},{10,1... | collective-permute-start | bytes 811016 | tf_op jit(solution)/shard_map/ppermute | solution.py:176
  53.8 10.2 %collective-permute-start.9 = (f32[264,256]{1,0:T(8,128)S(1)}, f32[264,256]{1,0:T(8,128)S(1)}, u32[]{:S(2)}, u32[]{:S(2)}) collective-permute-start(f32[264,256]{1,0:T(8,128)S(1)} %get-tuple-element.75), channel_id=1, source_target_pairs={{0,1},{1,2},{2,3},{3,4},{4,5},{5,6},{6,7},{7,8},{8,9},{9,10},{10,1... | collective-permute-start | bytes 811016 | tf_op jit(solution)/shard_map/ppermute | solution.py:176
  53.9 16.4 %collective-permute-start.10 = (f32[256,256]{1,0:T(8,128)S(1)}, f32[256,256]{1,0:T(8,128)S(1)}, u32[]{:S(2)}, u32[]{:S(2)}) collective-permute-start(f32[256,256]{1,0:T(8,128)S(1)} %get-tuple-element.69), channel_id=1, source_target_pairs={{0,1},{1,2},{2,3},{3,4},{4,5},{5,6},{6,7},{7,8},{8,9},{9,10},{10,1... | collective-permute-start | bytes 786440 | tf_op jit(solution)/shard_map/ppermute | solution.py:176
  54.0 16.3 %collective-permute-start.11 = (f32[256,256]{1,0:T(8,128)S(1)}, f32[256,256]{1,0:T(8,128)S(1)}, u32[]{:S(2)}, u32[]{:S(2)}) collective-permute-start(f32[256,256]{1,0:T(8,128)S(1)} %get-tuple-element.70), channel_id=1, source_target_pairs={{0,1},{1,2},{2,3},{3,4},{4,5},{5,6},{6,7},{7,8},{8,9},{9,10},{10,1... | collective-permute-start | bytes 786440 | tf_op jit(solution)/shard_map/ppermute | solution.py:176

commit v3 on v2

--- a/solution.py
+++ b/solution.py
@@ -105,35 +105,52 @@
     return e, C
 
 
-def row_part_kernel(j, t_ref, c_ref, M_ref, W_ref, g_ref):
-    for rows in row_spans(W_ref.shape[0], 512):
-        e, C = half_errors(j, W_ref[rows, :], t_ref, c_ref, M_ref, rows)
+def row_part_kernel(t_ref, c_ref, M_ref, W_ref, g_ref):
+    for rows in row_spans(W_ref.shape[0], 256):
+        e, C = half_errors(0, W_ref[rows, :], t_ref, c_ref, M_ref, rows)
         g_ref[rows, :] = dot(e, C, 1, 0)
 
 
-def row_last_kernel(j, t_ref, c_ref, M_ref, W_ref, A_ref, g_ref, Wo_ref, Ao_ref):
-    for rows in row_spans(W_ref.shape[0], 512):
+def row_col_kernel(
+    size, halves, after, t_ref, c_ref, M0_ref, M1_ref, W_ref, A_ref, g_ref, Wo_ref, Ao_ref, *h_refs
+):
+    M_refs = (M0_ref, M1_ref)
+    grads = [None] * len(halves)
+    for rows in row_spans(W_ref.shape[0], size):
         W = W_ref[rows, :]
-        e, C = half_errors(j, W, t_ref, c_ref, M_ref, rows)
-        g = g_ref[rows, :] + dot(e, C, 1, 0)
-        Wo_ref[rows, :], Ao_ref[rows, :] = adagrad(W, A_ref[rows, :], g)
+        e, C = half_errors(1, W, t_ref, c_ref, M1_ref, rows)
+        W, A = adagrad(W, A_ref[rows, :], g_ref[rows, :] + dot(e, C, 1, 0))
+        Wo_ref[rows, :] = W
+        Ao_ref[rows, :] = A
+        after(rows)
+        for k, j in enumerate(halves):
+            part = dot(W, half_errors(j, W, t_ref, c_ref, M_refs[j], rows)[0], 0, 0)
+            grads[k] = part if grads[k] is None else grads[k] + part
+    for grad, h_ref in zip(grads, h_refs):
+        h_ref[...] = grad.T
+
+
+def last_kernel(*refs):
+    ins, (Wo_hbm, Ao_hbm, h0_ref, h1_ref, W_buf, A_buf, sems) = refs[:7], refs[7:]
+    stores = []
+
+    def after(rows):
+        pairs = [(W_buf.at[rows], Wo_hbm.at[rows]), (A_buf.at[rows], Ao_hbm.at[rows])]
+        stores.extend(fetches(pairs, sems.at[len(stores) // 2]))
+
+    row_col_kernel(512, (0, 1), after, *ins, W_buf, A_buf, h0_ref, h1_ref)
+    for copy in stores:
+        copy.wait()
 
 
 def col_kernel(j, t_ref, c_ref, M_ref, W_ref, h_ref):
     grad = None
-    for rows in row_spans(W_ref.shape[0], 512):
+    for rows in row_spans(W_ref.shape[0], 256):
         W = W_ref[rows, :]
         e, _ = half_errors(j, W, t_ref, c_ref, M_ref, rows)
         part = dot(W, e, 0, 0)
         grad = part if grad is None else grad + part
     h_ref[...] = grad.T
-
-
-def col_store_kernel(j, t_ref, c_ref, M_ref, W_ref, A_ref, h_ref, Wo_hbm, Ao_hbm, sems):
-    copies = fetches([(W_ref, Wo_hbm), (A_ref, Ao_hbm)], sems)
-    col_kernel(j, t_ref, c_ref, M_ref, W_ref, h_ref)
-    for copy in copies:
-        copy.wait()
 
 
 def update_kernel(h_ref, M_ref, B_ref, Mo_ref, Bo_ref):
@@ -192,22 +209,28 @@
     )
     M, B = blocks[:HALVES], blocks[HALVES:]
     for step in range(steps):
+        h = None
         if step > 0:
-            part = call(
-                functools.partial(row_part_kernel, 0), (t, c, M[0], W), [V] * 4, [wide], [V], [], 12, "row0"
-            )[0]
-            W, A = call(
-                functools.partial(row_last_kernel, 1), (t, c, M[1], W, A, part), [V] * 6,
-                [wide, wide], [V] * 2, [], 12, "row1",
+            part = call(row_part_kernel, (t, c, M[0], W), [V] * 4, [wide], [V], [], 12, "row")[0]
+            operands = (t, c, M[0], M[1], W, A, part)
+            if step + 1 == steps:
+                W, A, *grads = call(
+                    last_kernel, operands, [V] * 7, [wide, wide, half, half], [H, H, V, V],
+                    [V(wide, f32), V(wide, f32), DMA((2, 2))], 20, "last",
+                )
+                break
+            W, A, h = call(
+                functools.partial(row_col_kernel, 256, (0,), lambda rows: None), operands, [V] * 7,
+                [wide, wide, half], [V] * 3, [], 16, "row_col",
             )
-        if step + 1 == steps:
-            break
         across = int(step + 1 == steps // 2)
         sent, sums = [], []
         for j in range(HALVES):
-            h = call(functools.partial(col_kernel, j), (t, c, M[j], W), [V] * 4, [half], [V], [], 12, "col%d" % j)[0]
+            if h is None or j > 0:
+                operands = (t, c, M[j], W)
+                h = call(functools.partial(col_kernel, j), operands, [V] * 4, [half], [V], [], 12, "col")[0]
             value, total = call(
-                update_kernel, (h, M[j], B[j]), [V] * 3, [message, half], [V] * 2, [], 4, "update%d" % j
+                update_kernel, (h, M[j], B[j]), [V] * 3, [message, half], [V] * 2, [], 4, "update"
             )
             sent.append(move(value, across))
             sums.append(total)
@@ -217,13 +240,9 @@
             [V(tile, jnp.int32), DMA((4,))], 12, "terms",
         )
         M, B = sent, [move(total, across) for total in sums]
-    h0, W_out, A_out = call(
-        functools.partial(col_store_kernel, 0), (t, c, M[0], W, A), [V] * 5, [half, wide, wide], [V, H, H],
-        [DMA((2,))], 12, "col0",
-    )
-    h1 = call(functools.partial(col_kernel, 1), (t, c, M[1], W), [V] * 4, [half], [V], [], 12, "col1")[0]
-    C, B = call(final_kernel, (h0, M[0], B[0], h1, M[1], B[1]), [V] * 6, [tall, tall], [V] * 2, [], 6, "final")
-    return W_out, A_out, C, B
+    operands = (grads[0], M[0], B[0], grads[1], M[1], B[1])
+    C, B = call(final_kernel, operands, [V] * 6, [tall, tall], [V] * 2, [], 6, "final")
+    return W, A, C, B
 
 
 def solution(mesh):

time: 71.6 us -> 69.7 us (0.973)
  Pallas kernels: 40.9 us -> 35.4 us
  waiting for transfers between devices: 22.4 us -> 25.8 us
    pallas_call x25 -> x21, Pallas kernels: 40.9 us -> 35.4 us  [call(): pl.pallas_call(kernel, in_specs=[pl.BlockSpec(memory_space=s) for s in sp...]
    ppermute x12, waiting for transfers between devices: 22.4 us -> 25.8 us  [move(): return lax.ppermute(block, ('outer', 'inner'), route)]
  transfers between devices with their start and end apart: 12 -> 12, of which waited for: 8 -> 10; matrix products, arithmetic and copies ran while one was open for 0% -> 0% of each run, Pallas kernels for 45% -> 39%
where the time goes in v3:
time: 69.7 us; the launch traced here: 69.5 us
  Pallas kernels  35.4 us (51%)
  waiting for transfers between devices  25.8 us (37%)
  starting transfers between devices  7.52 us (11%)
  between operations  0.82 us (1%)
    pallas_call x21, Pallas kernels, call(): pl.pallas_call(kernel, in_specs=[pl.BlockSpec(memory_space=s) for s in sp...  35.4 us
    ppermute x12, waiting for transfers between devices, move(): return lax.ppermute(block, ('outer', 'inner'), route)  25.8 us
    ppermute x12, starting transfers between devices, move(): return lax.ppermute(block, ('outer', 'inner'), route)  7.52 us
  transfers between devices with their start and end apart: 12, of which 10 were waited for; matrix products, arithmetic and copies ran while one was open for 0% of the time, Pallas kernels for 39%

profile of v3, /device:TPU:0, one launch (start us, length us, event | category | flops | bytes accessed | tf_op | source)
XLA Modules:
  0.0 69.5 jit_solution(11717127037130938290)
XLA Ops:
  0.6 5.2 %first.1 = (f32[1024,256]{1,0:T(8,128)S(1)}, f32[1024,256]{1,0:T(8,128)S(1)}, f32[1024,512]{1,0:T(8,128)S(1)}, f32[1024,512]{1,0:T(8,128)S(1)}, f32[264,256]{1,0...) custom-call(s32[1,4,1024,512]{3,2,1,0:T(8,128)} %x_hbm.7, ...), custom_call_target="tpu_custom_call" | custom-call | tf_op jit(solution)/shard_map/first/pallas_call | solution.py:172
  5.9 1.7 %col.4.h_ref = f32[256,256]{1,0:T(8,128)S(1)} custom-call(f32[1024,512]{1,0:T(8,128)S(1)} %get-tuple-element.45.t_ref, f32[1024,512]{1,0:T(8,128)S(1)} %get-tuple-element.46.c_ref, f32[264,256]{1,0:T(8,128)S(1)} %get-tuple-element.47.M_ref, f32[1024,256]{1,0:T(8,128)S(1)} %get-tuple-element.48.W_ref), custom_call_target="tpu_custom_call" | custom-call | tf_op jit(solution)/shard_map/col/pallas_call | solution.py:172
  7.8 1.7 %col.5.h_ref = f32[256,256]{1,0:T(8,128)S(1)} custom-call(f32[1024,512]{1,0:T(8,128)S(1)} %get-tuple-element.45.t_ref, f32[1024,512]{1,0:T(8,128)S(1)} %get-tuple-element.46.c_ref, f32[264,256]{1,0:T(8,128)S(1)} %get-tuple-element.51.M_ref, f32[1024,256]{1,0:T(8,128)S(1)} %get-tuple-element.48.W_ref), custom_call_target="tpu_custom_call" | custom-call | tf_op jit(solution)/shard_map/col/pallas_call | solution.py:172
  9.6 1.8 %collective-permute-start.1 = (f32[264,256]{1,0:T(8,128)S(1)}, f32[264,256]{1,0:T(8,128)S(1)}, u32[]{:S(2)}, u32[]{:S(2)}) collective-permute-start(f32[264,256]{1,0:T(8,128)S(1)} %get-tuple-element.58), channel_id=1, source_target_pairs={{0,1},{1,2},{2,3},{3,4},{4,5},{5,6},{6,7},{7,8},{8,9},{9,10},{10,1... | collective-permute-start | bytes 811016 | tf_op jit(solution)/shard_map/ppermute | solution.py:193
  11.5 1.4 %collective-permute-start.3 = (f32[256,256]{1,0:T(8,128)S(1)}, f32[256,256]{1,0:T(8,128)S(1)}, u32[]{:S(2)}, u32[]{:S(2)}) collective-permute-start(f32[256,256]{1,0:T(8,128)S(1)} %get-tuple-element.53), channel_id=1, source_target_pairs={{0,1},{1,2},{2,3},{3,4},{4,5},{5,6},{6,7},{7,8},{8,9},{9,10},{10,1... | collective-permute-start | bytes 786440 | tf_op jit(solution)/shard_map/ppermute | solution.py:193
  12.9 1.9 %terms.3 = (f32[1024,512]{1,0:T(8,128)S(1)}, f32[1024,512]{1,0:T(8,128)S(1)}) custom-call(s32[1,4,1024,512]{3,2,1,0:T(8,128)} %x_hbm.7, s32[8,128]{1,0:T(8,128)S(1)} %bitcast.3), custom_call_target="tpu_custom_call" | custom-call | tf_op jit(solution)/shard_map/terms/pallas_call | solution.py:172
  14.8 3.9 %collective-permute-done.M_ref.M0_ref = f32[264,256]{1,0:T(8,128)S(1)} collective-permute-done((f32[264,256]{1,0:T(8,128)S(1)}, f32[264,256]{1,0:T(8,128)S(1)}, u32[]{:S(2)}, u32[]{:S(2)}) %collective-permute-start) | collective-permute-done | bytes 270368 | tf_op jit(solution)/shard_map/ppermute | solution.py:193
  18.7 1.6 %row.3.g_ref = f32[1024,256]{1,0:T(8,128)S(1)} custom-call(f32[1024,512]{1,0:T(8,128)S(1)} %get-tuple-element.55.t_ref, f32[1024,512]{1,0:T(8,128)S(1)} %get-tuple-element.56.c_ref, f32[264,256]{1,0:T(8,128)S(1)} %collective-permute-done.M_ref.M0_ref, f32[1024,256]{1,0:T(8,128)S(1)} %get-tuple-element.48.W_ref), custom_call_target="tpu_custom_call" | custom-call | tf_op jit(solution)/shard_map/row/pallas_call | solution.py:172
  21.6 3.2 %row_col.2 = (f32[1024,256]{1,0:T(8,128)S(1)}, f32[1024,256]{1,0:T(8,128)S(1)}, f32[256,256]{1,0:T(8,128)S(1)}) custom-call(f32[1024,512]{1,0:T(8,128)S(1)} %get-tuple-element.55.t_ref, f32[1024,512]{1,0:T(8,128)S(1)} %get-tuple-element.56.c_ref, f32[264,256]{1,0:T(8,128)S(1)} %collective-permute-done.M_ref.M0_ref, ...), custom_call_target="tpu_custom_call" | custom-call | tf_op jit(solution)/shard_map/row_col/pallas_call | solution.py:172
  25.0 1.7 %col.6.h_ref = f32[256,256]{1,0:T(8,128)S(1)} custom-call(f32[1024,512]{1,0:T(8,128)S(1)} %get-tuple-element.55.t_ref, f32[1024,512]{1,0:T(8,128)S(1)} %get-tuple-element.56.c_ref, f32[264,256]{1,0:T(8,128)S(1)} %collective-permute-done.1.M1_ref.M_ref, f32[1024,256]{1,0:T(8,128)S(1)} %get-tuple-element.62.W_ref), custom_call_target="tpu_custom_call" | custom-call | tf_op jit(solution)/shard_map/col/pallas_call | solution.py:172
  27.4 1.9 %collective-permute-start.7 = (f32[256,256]{1,0:T(8,128)S(1)}, f32[256,256]{1,0:T(8,128)S(1)}, u32[]{:S(2)}, u32[]{:S(2)}) collective-permute-start(f32[256,256]{1,0:T(8,128)S(1)} %get-tuple-element.63), channel_id=1, source_target_pairs={{0,65},{1,66},{2,67},{3,68},{4,69},{5,70},{6,71},{7,72},{8,73},{9,... | collective-permute-start | bytes 786440 | tf_op jit(solution)/shard_map/ppermute | solution.py:193
  29.3 1.9 %terms.4 = (f32[1024,512]{1,0:T(8,128)S(1)}, f32[1024,512]{1,0:T(8,128)S(1)}) custom-call(s32[1,4,1024,512]{3,2,1,0:T(8,128)} %x_hbm.7, s32[8,128]{1,0:T(8,128)S(1)} %bitcast.4), custom_call_target="tpu_custom_call" | custom-call | tf_op jit(solution)/shard_map/terms/pallas_call | solution.py:172
  31.2 7.2 %collective-permute-done.4.M_ref.M0_ref = f32[264,256]{1,0:T(8,128)S(1)} collective-permute-done((f32[264,256]{1,0:T(8,128)S(1)}, f32[264,256]{1,0:T(8,128)S(1)}, u32[]{:S(2)}, u32[]{:S(2)}) %collective-permute-start.4) | collective-permute-done | bytes 270368 | tf_op jit(solution)/shard_map/ppermute | solution.py:193
  38.5 1.6 %row.4.g_ref = f32[1024,256]{1,0:T(8,128)S(1)} custom-call(f32[1024,512]{1,0:T(8,128)S(1)} %get-tuple-element.65.t_ref, f32[1024,512]{1,0:T(8,128)S(1)} %get-tuple-element.66.c_ref, f32[264,256]{1,0:T(8,128)S(1)} %collective-permute-done.4.M_ref.M0_ref, f32[1024,256]{1,0:T(8,128)S(1)} %get-tuple-element.62.W_ref), custom_call_target="tpu_custom_call" | custom-call | tf_op jit(solution)/shard_map/row/pallas_call | solution.py:172
  40.0 3.2 %collective-permute-done.5.M1_ref.M_ref = f32[264,256]{1,0:T(8,128)S(1)} collective-permute-done((f32[264,256]{1,0:T(8,128)S(1)}, f32[264,256]{1,0:T(8,128)S(1)}, u32[]{:S(2)}, u32[]{:S(2)}) %collective-permute-start.5) | collective-permute-done | bytes 270368 | tf_op jit(solution)/shard_map/ppermute | solution.py:193
  43.2 3.3 %row_col.3 = (f32[1024,256]{1,0:T(8,128)S(1)}, f32[1024,256]{1,0:T(8,128)S(1)}, f32[256,256]{1,0:T(8,128)S(1)}) custom-call(f32[1024,512]{1,0:T(8,128)S(1)} %get-tuple-element.65.t_ref, f32[1024,512]{1,0:T(8,128)S(1)} %get-tuple-element.66.c_ref, f32[264,256]{1,0:T(8,128)S(1)} %collective-permute-done.4.M_ref.M0_ref, ...), custom_call_target="tpu_custom_call" | custom-call | tf_op jit(solution)/shard_map/row_col/pallas_call | solution.py:172
  46.5 1.4 %collective-permute-done.6.B_ref = f32[256,256]{1,0:T(8,128)S(1)} collective-permute-done((f32[256,256]{1,0:T(8,128)S(1)}, f32[256,256]{1,0:T(8,128)S(1)}, u32[]{:S(2)}, u32[]{:S(2)}) %collective-permute-start.6) | collective-permute-done | bytes 262176 | tf_op jit(solution)/shard_map/ppermute | solution.py:193
  48.7 1.7 %col.7.h_ref = f32[256,256]{1,0:T(8,128)S(1)} custom-call(f32[1024,512]{1,0:T(8,128)S(1)} %get-tuple-element.65.t_ref, f32[1024,512]{1,0:T(8,128)S(1)} %get-tuple-element.66.c_ref, f32[264,256]{1,0:T(8,128)S(1)} %collective-permute-done.5.M1_ref.M_ref, f32[1024,256]{1,0:T(8,128)S(1)} %get-tuple-element.72.W_ref.refs_4_), custom_call_target="tpu_custom_call" | custom-call | tf_op jit(solution)/shard_map/col/pallas_call | solution.py:172
  50.4 2.2 %collective-permute-done.7.B_ref = f32[256,256]{1,0:T(8,128)S(1)} collective-permute-done((f32[256,256]{1,0:T(8,128)S(1)}, f32[256,256]{1,0:T(8,128)S(1)}, u32[]{:S(2)}, u32[]{:S(2)}) %collective-permute-start.7) | collective-permute-done | bytes 262176 | tf_op jit(solution)/shard_map/ppermute | solution.py:193
  54.0 1.9 %terms.5 = (f32[1024,512]{1,0:T(8,128)S(1)}, f32[1024,512]{1,0:T(8,128)S(1)}) custom-call(s32[1,4,1024,512]{3,2,1,0:T(8,128)} %x_hbm.7, s32[8,128]{1,0:T(8,128)S(1)} %bitcast.5), custom_call_target="tpu_custom_call" | custom-call | tf_op jit(solution)/shard_map/terms/pallas_call | solution.py:172
  55.9 2.3 %collective-permute-done.8.M_ref.refs_2_.refs_1_ = f32[264,256]{1,0:T(8,128)S(1)} collective-permute-done((f32[264,256]{1,0:T(8,128)S(1)}, f32[264,256]{1,0:T(8,128)S(1)}, u32[]{:S(2)}, u32[]{:S(2)}) %collective-permute-start.8) | collective-permute-done | bytes 270368 | tf_op jit(solution)/shard_map/ppermute | solution.py:193
  58.2 1.6 %row.5.refs_6_ = f32[1024,256]{1,0:T(8,128)S(1)} custom-call(f32[1024,512]{1,0:T(8,128)S(1)} %get-tuple-element.75.t_ref.refs_0_, f32[1024,512]{1,0:T(8,128)S(1)} %get-tuple-element.76.c_ref.refs_1_, f32[264,256]{1,0:T(8,128)S(1)} %collective-permute-done.8.M_ref.refs_2_.refs_1_, f32[1024,256]{1,0:T(8,128)S(1)} %get-tuple-element.72.W_ref.refs_4_), custom_call_target="tpu_custom_call" | custom-call | tf_op jit(solution)/shard_map/row/pallas_call | solution.py:172
  59.7 3.1 %collective-permute-done.9.refs_3_.refs_4_ = f32[264,256]{1,0:T(8,128)S(1)} collective-permute-done((f32[264,256]{1,0:T(8,128)S(1)}, f32[264,256]{1,0:T(8,128)S(1)}, u32[]{:S(2)}, u32[]{:S(2)}) %collective-permute-start.9) | collective-permute-done | bytes 270368 | tf_op jit(solution)/shard_map/ppermute | solution.py:193
  62.8 4.8 %last.1 = (f32[1024,256]{1,0:T(8,128)}, f32[1024,256]{1,0:T(8,128)}, f32[256,256]{1,0:T(8,128)S(1)}, f32[256,256]{1,0:T(8,128)S(1)}) custom-call(f32[1024,512]{1,0:T(8,128)S(1)} %get-tuple-element.75.t_ref.refs_0_, f32[1024,512]{1,0:T(8,128)S(1)} %get-tuple-element.76.c_ref.refs_1_, f32[264,256]{1,0:T(8,128)S(1)} %collective-permute-done.8.M_ref.refs_2_.refs_1_, ...), custom_call_target="tpu_custom_call" | custom-call | tf_op jit(solution)/shard_map/last/pallas_call | solution.py:172
  (23 shorter events, 6.5 us)
Async XLA Ops:
  7.7 11.0 %collective-permute-start = (f32[264,256]{1,0:T(8,128)S(1)}, f32[264,256]{1,0:T(8,128)S(1)}, u32[]{:S(2)}, u32[]{:S(2)}) collective-permute-start(f32[264,256]{1,0:T(8,128)S(1)} %get-tuple-element.57), channel_id=1, source_target_pairs={{0,1},{1,2},{2,3},{3,4},{4,5},{5,6},{6,7},{7,8},{8,9},{9,10},{10,1... | collective-permute-start | bytes 811016 | tf_op jit(solution)/shard_map/ppermute | solution.py:193
  7.7 5.2 %copy-start = (s32[1024]{0:T(1024)S(1)}, s32[1024]{0:T(1024)}, u32[]{:S(2)}) copy-start(s32[1024]{0:T(1024)} %param.8) | copy-start | bytes 12292
  9.6 12.0 %collective-permute-start.1 = (f32[264,256]{1,0:T(8,128)S(1)}, f32[264,256]{1,0:T(8,128)S(1)}, u32[]{:S(2)}, u32[]{:S(2)}) collective-permute-start(f32[264,256]{1,0:T(8,128)S(1)} %get-tuple-element.58), channel_id=1, source_target_pairs={{0,1},{1,2},{2,3},{3,4},{4,5},{5,6},{6,7},{7,8},{8,9},{9,10},{10,1... | collective-permute-start | bytes 811016 | tf_op jit(solution)/shard_map/ppermute | solution.py:193
  11.4 13.4 %collective-permute-start.2 = (f32[256,256]{1,0:T(8,128)S(1)}, f32[256,256]{1,0:T(8,128)S(1)}, u32[]{:S(2)}, u32[]{:S(2)}) collective-permute-start(f32[256,256]{1,0:T(8,128)S(1)} %get-tuple-element.50), channel_id=1, source_target_pairs={{0,1},{1,2},{2,3},{3,4},{4,5},{5,6},{6,7},{7,8},{8,9},{9,10},{10,1... | collective-permute-start | bytes 786440 | tf_op jit(solution)/shard_map/ppermute | solution.py:193
  11.5 15.7 %collective-permute-start.3 = (f32[256,256]{1,0:T(8,128)S(1)}, f32[256,256]{1,0:T(8,128)S(1)}, u32[]{:S(2)}, u32[]{:S(2)}) collective-permute-start(f32[256,256]{1,0:T(8,128)S(1)} %get-tuple-element.53), channel_id=1, source_target_pairs={{0,1},{1,2},{2,3},{3,4},{4,5},{5,6},{6,7},{7,8},{8,9},{9,10},{10,1... | collective-permute-start | bytes 786440 | tf_op jit(solution)/shard_map/ppermute | solution.py:193
  24.9 13.6 %collective-permute-start.4 = (f32[264,256]{1,0:T(8,128)S(1)}, f32[264,256]{1,0:T(8,128)S(1)}, u32[]{:S(2)}, u32[]{:S(2)}) collective-permute-start(f32[264,256]{1,0:T(8,128)S(1)} %get-tuple-element.67), channel_id=1, source_target_pairs={{0,65},{1,66},{2,67},{3,68},{4,69},{5,70},{6,71},{7,72},{8,73},{9,... | collective-permute-start | bytes 811016 | tf_op jit(solution)/shard_map/ppermute | solution.py:193
  27.3 16.0 %collective-permute-start.5 = (f32[264,256]{1,0:T(8,128)S(1)}, f32[264,256]{1,0:T(8,128)S(1)}, u32[]{:S(2)}, u32[]{:S(2)}) collective-permute-start(f32[264,256]{1,0:T(8,128)S(1)} %get-tuple-element.68), channel_id=1, source_target_pairs={{0,65},{1,66},{2,67},{3,68},{4,69},{5,70},{6,71},{7,72},{8,73},{9,... | collective-permute-start | bytes 811016 | tf_op jit(solution)/shard_map/ppermute | solution.py:193
  27.3 20.6 %collective-permute-start.6 = (f32[256,256]{1,0:T(8,128)S(1)}, f32[256,256]{1,0:T(8,128)S(1)}, u32[]{:S(2)}, u32[]{:S(2)}) collective-permute-start(f32[256,256]{1,0:T(8,128)S(1)} %get-tuple-element.61), channel_id=1, source_target_pairs={{0,65},{1,66},{2,67},{3,68},{4,69},{5,70},{6,71},{7,72},{8,73},{9,... | collective-permute-start | bytes 786440 | tf_op jit(solution)/shard_map/ppermute | solution.py:193
  27.4 25.2 %collective-permute-start.7 = (f32[256,256]{1,0:T(8,128)S(1)}, f32[256,256]{1,0:T(8,128)S(1)}, u32[]{:S(2)}, u32[]{:S(2)}) collective-permute-start(f32[256,256]{1,0:T(8,128)S(1)} %get-tuple-element.63), channel_id=1, source_target_pairs={{0,65},{1,66},{2,67},{3,68},{4,69},{5,70},{6,71},{7,72},{8,73},{9,... | collective-permute-start | bytes 786440 | tf_op jit(solution)/shard_map/ppermute | solution.py:193
  48.0 10.2 %collective-permute-start.8 = (f32[264,256]{1,0:T(8,128)S(1)}, f32[264,256]{1,0:T(8,128)S(1)}, u32[]{:S(2)}, u32[]{:S(2)}) collective-permute-start(f32[264,256]{1,0:T(8,128)S(1)} %get-tuple-element.77), channel_id=1, source_target_pairs={{0,1},{1,2},{2,3},{3,4},{4,5},{5,6},{6,7},{7,8},{8,9},{9,10},{10,1... | collective-permute-start | bytes 811016 | tf_op jit(solution)/shard_map/ppermute | solution.py:193
  52.7 10.2 %collective-permute-start.9 = (f32[264,256]{1,0:T(8,128)S(1)}, f32[264,256]{1,0:T(8,128)S(1)}, u32[]{:S(2)}, u32[]{:S(2)}) collective-permute-start(f32[264,256]{1,0:T(8,128)S(1)} %get-tuple-element.78), channel_id=1, source_target_pairs={{0,1},{1,2},{2,3},{3,4},{4,5},{5,6},{6,7},{7,8},{8,9},{9,10},{10,1... | collective-permute-start | bytes 811016 | tf_op jit(solution)/shard_map/ppermute | solution.py:193
  53.5 14.1 %collective-permute-start.10 = (f32[256,256]{1,0:T(8,128)S(1)}, f32[256,256]{1,0:T(8,128)S(1)}, u32[]{:S(2)}, u32[]{:S(2)}) collective-permute-start(f32[256,256]{1,0:T(8,128)S(1)} %get-tuple-element.71), channel_id=1, source_target_pairs={{0,1},{1,2},{2,3},{3,4},{4,5},{5,6},{6,7},{7,8},{8,9},{9,10},{10,1... | collective-permute-start | bytes 786440 | tf_op jit(solution)/shard_map/ppermute | solution.py:193
  53.6 14.8 %collective-permute-start.11 = (f32[256,256]{1,0:T(8,128)S(1)}, f32[256,256]{1,0:T(8,128)S(1)}, u32[]{:S(2)}, u32[]{:S(2)}) collective-permute-start(f32[256,256]{1,0:T(8,128)S(1)} %get-tuple-element.73), channel_id=1, source_target_pairs={{0,1},{1,2},{2,3},{3,4},{4,5},{5,6},{6,7},{7,8},{8,9},{9,10},{10,1... | collective-permute-start | bytes 786440 | tf_op jit(solution)/shard_map/ppermute | solution.py:193

commit v4 on v3

--- a/solution.py
+++ b/solution.py
@@ -6,6 +6,7 @@
 from jax.experimental import pallas as pl
 from jax.experimental.pallas import tpu as pltpu
 from jax.sharding import PartitionSpec as P
+
 
 LOG_TOTAL = 17.0
 LEARNING = 0.05
@@ -168,7 +169,7 @@
         Co_ref[rows, :], Bo_ref[rows, :] = adagrad(M_ref[:n, :], B_ref[...], h_ref[...])
 
 
-def call(kernel, operands, spaces, outs, out_spaces, scratch, mib, name):
+def call(kernel, operands, spaces, outs, out_spaces, scratch, mib):
     return pl.pallas_call(
         kernel,
         in_specs=[pl.BlockSpec(memory_space=s) for s in spaces],
@@ -176,7 +177,6 @@
         out_shape=[jax.ShapeDtypeStruct(s, f32) for s in outs],
         scratch_shapes=scratch,
         compiler_params=pltpu.CompilerParams(vmem_limit_bytes=mib << 20),
-        name=name,
     )(*operands)
 
 
@@ -184,9 +184,9 @@
     steps = tile_counts.shape[1]
     n_outer, n_inner = lax.axis_size("outer"), lax.axis_size("inner")
 
-    def move(block, across):
+    def move(block, across, by=1):
         route = [
-            (o * n_inner + i, (o + across) % n_outer * n_inner + (i + 1) % n_inner)
+            (o * n_inner + i, (o + across) % n_outer * n_inner + (i + by) % n_inner)
             for o in range(n_outer)
             for i in range(n_inner)
         ]
@@ -205,43 +205,55 @@
         [wide, wide, tile, tile] + [message] * HALVES + [half] * HALVES, [V] * (4 + 2 * HALVES),
         [V(tile, jnp.int32), V(wide, f32), V(wide, f32), V(rows.shape, jnp.int32),
          V(cols.shape, jnp.int32), DMA((4 + 3 * 2,)), DMA((HALVES,))],
-        24, "first",
+        24,
     )
     M, B = blocks[:HALVES], blocks[HALVES:]
+
+    def update(h, value, total):
+        return call(update_kernel, (h, value, total), [V] * 3, [message, half], [V] * 2, [], 4)
+
+    halfway = steps // 2
+    early = None
     for step in range(steps):
         h = None
         if step > 0:
-            part = call(row_part_kernel, (t, c, M[0], W), [V] * 4, [wide], [V], [], 12, "row")[0]
+            if step == halfway:
+                M[0], B[0] = update(M[0], *early)
+            part = call(row_part_kernel, (t, c, M[0], W), [V] * 4, [wide], [V], [], 12)[0]
             operands = (t, c, M[0], M[1], W, A, part)
             if step + 1 == steps:
                 W, A, *grads = call(
                     last_kernel, operands, [V] * 7, [wide, wide, half, half], [H, H, V, V],
-                    [V(wide, f32), V(wide, f32), DMA((2, 2))], 20, "last",
+                    [V(wide, f32), V(wide, f32), DMA((2, 2))], 20,
                 )
                 break
             W, A, h = call(
                 functools.partial(row_col_kernel, 256, (0,), lambda rows: None), operands, [V] * 7,
-                [wide, wide, half], [V] * 3, [], 16, "row_col",
+                [wide, wide, half], [V] * 3, [], 16,
             )
-        across = int(step + 1 == steps // 2)
-        sent, sums = [], []
-        for j in range(HALVES):
-            if h is None or j > 0:
-                operands = (t, c, M[j], W)
-                h = call(functools.partial(col_kernel, j), operands, [V] * 4, [half], [V], [], 12, "col")[0]
-            value, total = call(
-                update_kernel, (h, M[j], B[j]), [V] * 3, [message, half], [V] * 2, [], 4, "update"
-            )
-            sent.append(move(value, across))
-            sums.append(total)
-        row_tie = lax.optimization_barrier((rows, *sums))[0]
+        if h is None:
+            h = call(functools.partial(col_kernel, 0), (t, c, M[0], W), [V] * 4, [half], [V], [], 12)[0]
+        across = int(step + 1 == halfway)
+        if across:
+            sent = [move(h, across)]
+        else:
+            value, total = update(h, M[0], B[0])
+            sent = [move(value, across)]
+        h = call(functools.partial(col_kernel, 1), (t, c, M[1], W), [V] * 4, [half], [V], [], 12)[0]
+        last_value, last_total = update(h, M[1], B[1])
+        sent.append(move(last_value, across))
+        row_tie = lax.optimization_barrier((rows, last_total))[0]
         t, c = call(
             functools.partial(terms_kernel, step + 1), (hbm[0], row_tie), [H, V], [tile, tile], [V] * 2,
-            [V(tile, jnp.int32), DMA((4,))], 12, "terms",
+            [V(tile, jnp.int32), DMA((4,))], 12,
         )
-        M, B = sent, [move(total, across) for total in sums]
+        M, B = sent, [None, move(last_total, across)]
+        if step + 2 == halfway:
+            early = [move(value, 1, 2), move(total, 1, 2)]
+        elif not across:
+            B[0] = move(total, across)
     operands = (grads[0], M[0], B[0], grads[1], M[1], B[1])
-    C, B = call(final_kernel, operands, [V] * 6, [tall, tall], [V] * 2, [], 6, "final")
+    C, B = call(final_kernel, operands, [V] * 6, [tall, tall], [V] * 2, [], 6)
     return W, A, C, B
 
 

time: 69.7 us -> 79.9 us (1.15)
  waiting for transfers between devices: 25.8 us -> 35.2 us
    ppermute x12, waiting for transfers between devices: 25.8 us -> 35.2 us  [move(): return lax.ppermute(block, ('outer', 'inner'), route)]
  transfers between devices with their start and end apart: 12 -> 12, of which waited for: 10 -> 7; matrix products, arithmetic and copies ran while one was open for 0% -> 0% of each run, Pallas kernels for 39% -> 34%
where the time goes in v4:
time: 79.9 us; the launch traced here: 79.7 us
  Pallas kernels  35.4 us (44%)
  waiting for transfers between devices  35.2 us (44%)
  starting transfers between devices  8.26 us (10%)
  between operations  0.86 us (1%)
    pallas_call x21, Pallas kernels, call(): pl.pallas_call(kernel, in_specs=[pl.BlockSpec(memory_space=s) for s in sp...  35.4 us
    ppermute x12, waiting for transfers between devices, move(): return lax.ppermute(block, ('outer', 'inner'), route)  35.2 us
    ppermute x12, starting transfers between devices, move(): return lax.ppermute(block, ('outer', 'inner'), route)  8.26 us
  transfers between devices with their start and end apart: 12, of which 7 were waited for; matrix products, arithmetic and copies ran while one was open for 0% of the time, Pallas kernels for 34%

profile of v4, /device:TPU:0, one launch (start us, length us, event | category | flops | bytes accessed | tf_op | source)
XLA Modules:
  0.0 79.7 jit_solution(9172104697392772291)
XLA Ops:
  0.6 5.2 %shard_map.102 = (f32[1024,256]{1,0:T(8,128)S(1)}, f32[1024,256]{1,0:T(8,128)S(1)}, f32[1024,512]{1,0:T(8,128)S(1)}, f32[1024,512]{1,0:T(8,128)S(1)}, f32[264,25...) custom-call(s32[1,4,1024,512]{3,2,1,0:T(8,128)} %x_hbm.7, ...), custom_call_target="tpu_custom_call" | custom-call | tf_op jit(solution)/shard_map/pallas_call | solution.py:173
  5.9 1.7 %shard_map.106.h_ref = f32[256,256]{1,0:T(8,128)S(1)} custom-call(f32[1024,512]{1,0:T(8,128)S(1)} %get-tuple-element.45.t_ref, f32[1024,512]{1,0:T(8,128)S(1)} %get-tuple-element.46.c_ref, f32[264,256]{1,0:T(8,128)S(1)} %get-tuple-element.55.M_ref, f32[1024,256]{1,0:T(8,128)S(1)} %get-tuple-element.48.W_ref), custom_call_target="tpu_custom_call" | custom-call | tf_op jit(solution)/shard_map/pallas_call | solution.py:173
  7.8 1.7 %shard_map.103.h_ref = f32[256,256]{1,0:T(8,128)S(1)} custom-call(f32[1024,512]{1,0:T(8,128)S(1)} %get-tuple-element.45.t_ref, f32[1024,512]{1,0:T(8,128)S(1)} %get-tuple-element.46.c_ref, f32[264,256]{1,0:T(8,128)S(1)} %get-tuple-element.47.M_ref, f32[1024,256]{1,0:T(8,128)S(1)} %get-tuple-element.48.W_ref), custom_call_target="tpu_custom_call" | custom-call | tf_op jit(solution)/shard_map/pallas_call | solution.py:173
  9.6 1.8 %collective-permute-start = (f32[264,256]{1,0:T(8,128)S(1)}, f32[264,256]{1,0:T(8,128)S(1)}, u32[]{:S(2)}, u32[]{:S(2)}) collective-permute-start(f32[264,256]{1,0:T(8,128)S(1)} %get-tuple-element.54), channel_id=1, source_target_pairs={{0,1},{1,2},{2,3},{3,4},{4,5},{5,6},{6,7},{7,8},{8,9},{9,10},{10,1... | collective-permute-start | bytes 811016 | tf_op jit(solution)/shard_map/ppermute | solution.py:193
  11.5 3.1 %collective-permute-start.5 = (f32[264,256]{1,0:T(8,128)S(1)}, f32[264,256]{1,0:T(8,128)S(1)}, u32[]{:S(2)}, u32[]{:S(2)}) collective-permute-start(f32[264,256]{1,0:T(8,128)S(1)} %get-tuple-element.57), channel_id=1, source_target_pairs={{0,66},{1,67},{2,68},{3,69},{4,70},{5,71},{6,72},{7,73},{8,74},{9,... | collective-permute-start | bytes 811016 | tf_op jit(solution)/shard_map/ppermute | solution.py:193
  14.6 1.9 %shard_map.105 = (f32[1024,512]{1,0:T(8,128)S(1)}, f32[1024,512]{1,0:T(8,128)S(1)}) custom-call(s32[1,4,1024,512]{3,2,1,0:T(8,128)} %x_hbm.7, s32[8,128]{1,0:T(8,128)S(1)} %bitcast.3), custom_call_target="tpu_custom_call" | custom-call | tf_op jit(solution)/shard_map/pallas_call | solution.py:173
  16.5 2.2 %collective-permute-done.1.M_ref.M0_ref = f32[264,256]{1,0:T(8,128)S(1)} collective-permute-done((f32[264,256]{1,0:T(8,128)S(1)}, f32[264,256]{1,0:T(8,128)S(1)}, u32[]{:S(2)}, u32[]{:S(2)}) %collective-permute-start.1) | collective-permute-done | bytes 270368 | tf_op jit(solution)/shard_map/ppermute | solution.py:193
  18.7 1.6 %shard_map.108.g_ref = f32[1024,256]{1,0:T(8,128)S(1)} custom-call(f32[1024,512]{1,0:T(8,128)S(1)} %get-tuple-element.52.t_ref, f32[1024,512]{1,0:T(8,128)S(1)} %get-tuple-element.53.c_ref, f32[264,256]{1,0:T(8,128)S(1)} %collective-permute-done.1.M_ref.M0_ref, f32[1024,256]{1,0:T(8,128)S(1)} %get-tuple-element.48.W_ref), custom_call_target="tpu_custom_call" | custom-call | tf_op jit(solution)/shard_map/pallas_call | solution.py:173
  20.3 2.8 %collective-permute-done.M1_ref.M_ref = f32[264,256]{1,0:T(8,128)S(1)} collective-permute-done((f32[264,256]{1,0:T(8,128)S(1)}, f32[264,256]{1,0:T(8,128)S(1)}, u32[]{:S(2)}, u32[]{:S(2)}) %collective-permute-start) | collective-permute-done | bytes 270368 | tf_op jit(solution)/shard_map/ppermute | solution.py:193
  23.0 3.2 %shard_map.109 = (f32[1024,256]{1,0:T(8,128)S(1)}, f32[1024,256]{1,0:T(8,128)S(1)}, f32[256,256]{1,0:T(8,128)S(1)}) custom-call(f32[1024,512]{1,0:T(8,128)S(1)} %get-tuple-element.52.t_ref, f32[1024,512]{1,0:T(8,128)S(1)} %get-tuple-element.53.c_ref, f32[264,256]{1,0:T(8,128)S(1)} %collective-permute-done.1.M_ref.M0_ref, ...), custom_call_target="tpu_custom_call" | custom-call | tf_op jit(solution)/shard_map/pallas_call | solution.py:173
  26.3 1.7 %shard_map.110.h_ref = f32[256,256]{1,0:T(8,128)S(1)} custom-call(f32[1024,512]{1,0:T(8,128)S(1)} %get-tuple-element.52.t_ref, f32[1024,512]{1,0:T(8,128)S(1)} %get-tuple-element.53.c_ref, f32[264,256]{1,0:T(8,128)S(1)} %collective-permute-done.M1_ref.M_ref, f32[1024,256]{1,0:T(8,128)S(1)} %get-tuple-element.59.W_ref), custom_call_target="tpu_custom_call" | custom-call | tf_op jit(solution)/shard_map/pallas_call | solution.py:173
  28.3 2.1 %collective-permute-start.4 = (f32[256,256]{1,0:T(8,128)S(1)}, f32[256,256]{1,0:T(8,128)S(1)}, u32[]{:S(2)}, u32[]{:S(2)}) collective-permute-start(f32[256,256]{1,0:T(8,128)S(1)} %get-tuple-element.65), channel_id=1, source_target_pairs={{0,65},{1,66},{2,67},{3,68},{4,69},{5,70},{6,71},{7,72},{8,73},{9,... | collective-permute-start | bytes 786440 | tf_op jit(solution)/shard_map/ppermute | solution.py:193
  30.7 1.9 %shard_map.112 = (f32[1024,512]{1,0:T(8,128)S(1)}, f32[1024,512]{1,0:T(8,128)S(1)}) custom-call(s32[1,4,1024,512]{3,2,1,0:T(8,128)} %x_hbm.7, s32[8,128]{1,0:T(8,128)S(1)} %bitcast.4), custom_call_target="tpu_custom_call" | custom-call | tf_op jit(solution)/shard_map/pallas_call | solution.py:173
  32.6 14.6 %collective-permute-done.6.B_ref = f32[256,256]{1,0:T(8,128)S(1)} collective-permute-done((f32[256,256]{1,0:T(8,128)S(1)}, f32[256,256]{1,0:T(8,128)S(1)}, u32[]{:S(2)}, u32[]{:S(2)}) %collective-permute-start.6) | collective-permute-done | bytes 262176 | tf_op jit(solution)/shard_map/ppermute | solution.py:193
  47.2 7.7 %collective-permute-done.4.h_ref = f32[256,256]{1,0:T(8,128)S(1)} collective-permute-done((f32[256,256]{1,0:T(8,128)S(1)}, f32[256,256]{1,0:T(8,128)S(1)}, u32[]{:S(2)}, u32[]{:S(2)}) %collective-permute-start.4) | collective-permute-done | bytes 262176 | tf_op jit(solution)/shard_map/ppermute | solution.py:193
  55.0 1.6 %shard_map.114.g_ref = f32[1024,256]{1,0:T(8,128)S(1)} custom-call(f32[1024,512]{1,0:T(8,128)S(1)} %get-tuple-element.62.t_ref, f32[1024,512]{1,0:T(8,128)S(1)} %get-tuple-element.63.c_ref, f32[264,256]{1,0:T(8,128)S(1)} %get-tuple-element.67.M_ref.M0_ref, f32[1024,256]{1,0:T(8,128)S(1)} %get-tuple-element.59.W_ref), custom_call_target="tpu_custom_call" | custom-call | tf_op jit(solution)/shard_map/pallas_call | solution.py:173
  56.6 3.3 %shard_map.115 = (f32[1024,256]{1,0:T(8,128)S(1)}, f32[1024,256]{1,0:T(8,128)S(1)}, f32[256,256]{1,0:T(8,128)S(1)}) custom-call(f32[1024,512]{1,0:T(8,128)S(1)} %get-tuple-element.62.t_ref, f32[1024,512]{1,0:T(8,128)S(1)} %get-tuple-element.63.c_ref, f32[264,256]{1,0:T(8,128)S(1)} %get-tuple-element.67.M_ref.M0_ref, ...), custom_call_target="tpu_custom_call" | custom-call | tf_op jit(solution)/shard_map/pallas_call | solution.py:173
  60.0 1.7 %shard_map.116.h_ref = f32[256,256]{1,0:T(8,128)S(1)} custom-call(f32[1024,512]{1,0:T(8,128)S(1)} %get-tuple-element.62.t_ref, f32[1024,512]{1,0:T(8,128)S(1)} %get-tuple-element.63.c_ref, f32[264,256]{1,0:T(8,128)S(1)} %collective-permute-done.3.M1_ref.M_ref, f32[1024,256]{1,0:T(8,128)S(1)} %get-tuple-element.69.W_ref.refs_4_), custom_call_target="tpu_custom_call" | custom-call | tf_op jit(solution)/shard_map/pallas_call | solution.py:173
  62.4 1.9 %shard_map.118 = (f32[1024,512]{1,0:T(8,128)S(1)}, f32[1024,512]{1,0:T(8,128)S(1)}) custom-call(s32[1,4,1024,512]{3,2,1,0:T(8,128)} %x_hbm.7, s32[8,128]{1,0:T(8,128)S(1)} %bitcast.5), custom_call_target="tpu_custom_call" | custom-call | tf_op jit(solution)/shard_map/pallas_call | solution.py:173
  64.3 5.9 %collective-permute-done.8.M_ref.refs_2_.refs_1_ = f32[264,256]{1,0:T(8,128)S(1)} collective-permute-done((f32[264,256]{1,0:T(8,128)S(1)}, f32[264,256]{1,0:T(8,128)S(1)}, u32[]{:S(2)}, u32[]{:S(2)}) %collective-permute-start.8) | collective-permute-done | bytes 270368 | tf_op jit(solution)/shard_map/ppermute | solution.py:193
  70.1 1.6 %shard_map.120.refs_6_ = f32[1024,256]{1,0:T(8,128)S(1)} custom-call(f32[1024,512]{1,0:T(8,128)S(1)} %get-tuple-element.72.t_ref.refs_0_, f32[1024,512]{1,0:T(8,128)S(1)} %get-tuple-element.73.c_ref.refs_1_, f32[264,256]{1,0:T(8,128)S(1)} %collective-permute-done.8.M_ref.refs_2_.refs_1_, f32[1024,256]{1,0:T(8,128)S(1)} %get-tuple-element.69.W_ref.refs_4_), custom_call_target="tpu_custom_call" | custom-call | tf_op jit(solution)/shard_map/pallas_call | solution.py:173
  71.7 1.3 %collective-permute-done.9.refs_3_.refs_4_ = f32[264,256]{1,0:T(8,128)S(1)} collective-permute-done((f32[264,256]{1,0:T(8,128)S(1)}, f32[264,256]{1,0:T(8,128)S(1)}, u32[]{:S(2)}, u32[]{:S(2)}) %collective-permute-start.9) | collective-permute-done | bytes 270368 | tf_op jit(solution)/shard_map/ppermute | solution.py:193
  73.0 4.8 %shard_map.121 = (f32[1024,256]{1,0:T(8,128)}, f32[1024,256]{1,0:T(8,128)}, f32[256,256]{1,0:T(8,128)S(1)}, f32[256,256]{1,0:T(8,128)S(1)}) custom-call(f32[1024,512]{1,0:T(8,128)S(1)} %get-tuple-element.72.t_ref.refs_0_, f32[1024,512]{1,0:T(8,128)S(1)} %get-tuple-element.73.c_ref.refs_1_, f32[264,256]{1,0:T(8,128)S(1)} %collective-permute-done.8.M_ref.refs_2_.refs_1_, ...), custom_call_target="tpu_custom_call" | custom-call | tf_op jit(solution)/shard_map/pallas_call | solution.py:173
  78.6 1.1 %shard_map.122 = (f32[512,256]{1,0:T(8,128)}, f32[512,256]{1,0:T(8,128)}) custom-call(f32[256,256]{1,0:T(8,128)S(1)} %get-tuple-element.81.refs_0_, f32[264,256]{1,0:T(8,128)S(1)} %collective-permute-done.8.M_ref.refs_2_.refs_1_, f32[256,256]{1,0:T(8,128)S(1)} %collective-permute-done.10.refs_2_, f32[256,256]{1,0:T(8,128)S(1)} %get-tuple-element.83.refs_3_, ...), custom_call_target="tpu_custom_call" | custom-call | tf_op jit(solution)/shard_map/pallas_call | solution.py:173
  (23 shorter events, 2.5 us)
Async XLA Ops:
  7.7 11.0 %collective-permute-start.1 = (f32[264,256]{1,0:T(8,128)S(1)}, f32[264,256]{1,0:T(8,128)S(1)}, u32[]{:S(2)}, u32[]{:S(2)}) collective-permute-start(f32[264,256]{1,0:T(8,128)S(1)} %get-tuple-element.57), channel_id=1, source_target_pairs={{0,1},{1,2},{2,3},{3,4},{4,5},{5,6},{6,7},{7,8},{8,9},{9,10},{10,1... | collective-permute-start | bytes 811016 | tf_op jit(solution)/shard_map/ppermute | solution.py:193
  7.7 6.9 %copy-start = (s32[1024]{0:T(1024)S(1)}, s32[1024]{0:T(1024)}, u32[]{:S(2)}) copy-start(s32[1024]{0:T(1024)} %param.8) | copy-start | bytes 12292
  9.6 13.5 %collective-permute-start = (f32[264,256]{1,0:T(8,128)S(1)}, f32[264,256]{1,0:T(8,128)S(1)}, u32[]{:S(2)}, u32[]{:S(2)}) collective-permute-start(f32[264,256]{1,0:T(8,128)S(1)} %get-tuple-element.54), channel_id=1, source_target_pairs={{0,1},{1,2},{2,3},{3,4},{4,5},{5,6},{6,7},{7,8},{8,9},{9,10},{10,1... | collective-permute-start | bytes 811016 | tf_op jit(solution)/shard_map/ppermute | solution.py:193
  11.4 16.6 %collective-permute-start.2 = (f32[256,256]{1,0:T(8,128)S(1)}, f32[256,256]{1,0:T(8,128)S(1)}, u32[]{:S(2)}, u32[]{:S(2)}) collective-permute-start(f32[256,256]{1,0:T(8,128)S(1)} %get-tuple-element.50), channel_id=1, source_target_pairs={{0,1},{1,2},{2,3},{3,4},{4,5},{5,6},{6,7},{7,8},{8,9},{9,10},{10,1... | collective-permute-start | bytes 786440 | tf_op jit(solution)/shard_map/ppermute | solution.py:193
  11.5 35.8 %collective-permute-start.5 = (f32[264,256]{1,0:T(8,128)S(1)}, f32[264,256]{1,0:T(8,128)S(1)}, u32[]{:S(2)}, u32[]{:S(2)}) collective-permute-start(f32[264,256]{1,0:T(8,128)S(1)} %get-tuple-element.57), channel_id=1, source_target_pairs={{0,66},{1,67},{2,68},{3,69},{4,70},{5,71},{6,72},{7,73},{8,74},{9,... | collective-permute-start | bytes 811016 | tf_op jit(solution)/shard_map/ppermute | solution.py:193
  28.1 28.5 %collective-permute-start.3 = (f32[264,256]{1,0:T(8,128)S(1)}, f32[264,256]{1,0:T(8,128)S(1)}, u32[]{:S(2)}, u32[]{:S(2)}) collective-permute-start(f32[264,256]{1,0:T(8,128)S(1)} %get-tuple-element.64), channel_id=1, source_target_pairs={{0,65},{1,66},{2,67},{3,68},{4,69},{5,70},{6,71},{7,72},{8,73},{9,... | collective-permute-start | bytes 811016 | tf_op jit(solution)/shard_map/ppermute | solution.py:193
  28.2 19.1 %collective-permute-start.6 = (f32[256,256]{1,0:T(8,128)S(1)}, f32[256,256]{1,0:T(8,128)S(1)}, u32[]{:S(2)}, u32[]{:S(2)}) collective-permute-start(f32[256,256]{1,0:T(8,128)S(1)} %get-tuple-element.66), channel_id=1, source_target_pairs={{0,66},{1,67},{2,68},{3,69},{4,70},{5,71},{6,72},{7,73},{8,74},{9,... | collective-permute-start | bytes 786440 | tf_op jit(solution)/shard_map/ppermute | solution.py:193
  28.3 26.6 %collective-permute-start.4 = (f32[256,256]{1,0:T(8,128)S(1)}, f32[256,256]{1,0:T(8,128)S(1)}, u32[]{:S(2)}, u32[]{:S(2)}) collective-permute-start(f32[256,256]{1,0:T(8,128)S(1)} %get-tuple-element.65), channel_id=1, source_target_pairs={{0,65},{1,66},{2,67},{3,68},{4,69},{5,70},{6,71},{7,72},{8,73},{9,... | collective-permute-start | bytes 786440 | tf_op jit(solution)/shard_map/ppermute | solution.py:193
  30.3 31.4 %collective-permute-start.7 = (f32[256,256]{1,0:T(8,128)S(1)}, f32[256,256]{1,0:T(8,128)S(1)}, u32[]{:S(2)}, u32[]{:S(2)}) collective-permute-start(f32[256,256]{1,0:T(8,128)S(1)} %get-tuple-element.60), channel_id=1, source_target_pairs={{0,65},{1,66},{2,67},{3,68},{4,69},{5,70},{6,71},{7,72},{8,73},{9,... | collective-permute-start | bytes 786440 | tf_op jit(solution)/shard_map/ppermute | solution.py:193
  60.0 10.2 %collective-permute-start.8 = (f32[264,256]{1,0:T(8,128)S(1)}, f32[264,256]{1,0:T(8,128)S(1)}, u32[]{:S(2)}, u32[]{:S(2)}) collective-permute-start(f32[264,256]{1,0:T(8,128)S(1)} %get-tuple-element.76), channel_id=1, source_target_pairs={{0,1},{1,2},{2,3},{3,4},{4,5},{5,6},{6,7},{7,8},{8,9},{9,10},{10,1... | collective-permute-start | bytes 811016 | tf_op jit(solution)/shard_map/ppermute | solution.py:193
  61.8 11.2 %collective-permute-start.9 = (f32[264,256]{1,0:T(8,128)S(1)}, f32[264,256]{1,0:T(8,128)S(1)}, u32[]{:S(2)}, u32[]{:S(2)}) collective-permute-start(f32[264,256]{1,0:T(8,128)S(1)} %get-tuple-element.77), channel_id=1, source_target_pairs={{0,1},{1,2},{2,3},{3,4},{4,5},{5,6},{6,7},{7,8},{8,9},{9,10},{10,1... | collective-permute-start | bytes 811016 | tf_op jit(solution)/shard_map/ppermute | solution.py:193
  61.9 15.9 %collective-permute-start.10 = (f32[256,256]{1,0:T(8,128)S(1)}, f32[256,256]{1,0:T(8,128)S(1)}, u32[]{:S(2)}, u32[]{:S(2)}) collective-permute-start(f32[256,256]{1,0:T(8,128)S(1)} %get-tuple-element.82), channel_id=1, source_target_pairs={{0,1},{1,2},{2,3},{3,4},{4,5},{5,6},{6,7},{7,8},{8,9},{9,10},{10,1... | collective-permute-start | bytes 786440 | tf_op jit(solution)/shard_map/ppermute | solution.py:193
  62.0 16.6 %collective-permute-start.11 = (f32[256,256]{1,0:T(8,128)S(1)}, f32[256,256]{1,0:T(8,128)S(1)}, u32[]{:S(2)}, u32[]{:S(2)}) collective-permute-start(f32[256,256]{1,0:T(8,128)S(1)} %get-tuple-element.70), channel_id=1, source_target_pairs={{0,1},{1,2},{2,3},{3,4},{4,5},{5,6},{6,7},{7,8},{8,9},{9,10},{10,1... | collective-permute-start | bytes 786440 | tf_op jit(solution)/shard_map/ppermute | solution.py:193

commit v5 on v4

--- a/solution.py
+++ b/solution.py
@@ -11,6 +11,7 @@
 LOG_TOTAL = 17.0
 LEARNING = 0.05
 HALVES = 2
+FIRST = 256
 f32 = jnp.float32
 V, H, DMA = pltpu.VMEM, pltpu.HBM, pltpu.SemaphoreType.DMA
 
@@ -37,12 +38,12 @@
     return [pl.ds(start, size) for start in range(0, n, size)]
 
 
-def put_terms(x, row_logs, first, t_ref, c_ref, rows):
+def terms(x, row_logs, first):
     m = jnp.maximum(x.astype(f32), 1.0)
     lanes = row_logs.shape[0]
     logs = [row_logs[:, j : j + 1] for j in range(first, first + x.shape[0] // lanes)]
-    t_ref[rows, :] = jnp.log(m) - jnp.concatenate(logs, axis=0)
-    c_ref[rows, :] = jnp.where(x > 0, 0.1 + 0.25 * (m * lax.rsqrt(m)), 0.0)
+    target = jnp.log(m) - jnp.concatenate(logs, axis=0)
+    return target, jnp.where(x > 0, 0.1 + 0.25 * (m * lax.rsqrt(m)), 0.0)
 
 
 def errors(z, target, confidence, col_logs):
@@ -60,17 +61,16 @@
     row_logs = shifted_row_logs(rows_ref)
     for i, rows in enumerate(spans):
         copies[i].wait()
-        put_terms(x_buf[rows, :], row_logs, 2 * i, t_ref, c_ref, rows)
+        t_ref[rows, :], c_ref[rows, :] = terms(x_buf[rows, :], row_logs, 2 * i)
 
 
 def first_kernel(
-    x_hbm, rows_hbm, cols_hbm, W_hbm, A_hbm, C_hbm, B_hbm,
-    Wo_ref, Ao_ref, t_ref, c_ref, *rest,
+    x_hbm, rows_hbm, cols_hbm, W_hbm, A_hbm, C_hbm, B_hbm, Wo_ref, Ao_ref, t_ref, c_ref, h_ref, *rest
 ):
     M_refs, B_refs = rest[:HALVES], rest[HALVES : 2 * HALVES]
-    x_buf, W_buf, A_buf, rows_buf, cols_buf, sems, out_sems = rest[2 * HALVES :]
+    x_buf, W_buf, A_buf, rows_buf, cols_buf, sems, late_sems = rest[2 * HALVES :]
     n, width = B_refs[0].shape
-    spans = row_spans(x_buf.shape[0], 512)
+    spans = row_spans(x_buf.shape[0], FIRST)
     pairs = [(cols_hbm, cols_buf), (rows_hbm, rows_buf)]
     pairs += [(C_hbm.at[pl.ds(j * n, n)], M_refs[j].at[pl.ds(0, n)]) for j in range(HALVES)]
     head = len(pairs)
@@ -79,28 +79,36 @@
         pairs.append((x_hbm.at[0, 0, rows], x_buf.at[rows]))
         pairs.append((A_hbm.at[rows], A_buf.at[rows]))
     copies = fetches(pairs, sems)
-    late = fetches([(B_hbm.at[pl.ds(j * n, n)], B_refs[j]) for j in range(HALVES)], out_sems)
+    late = fetches([(B_hbm.at[pl.ds(j * n, n)], B_refs[j]) for j in range(HALVES)], late_sems)
     for copy in copies[:head]:
         copy.wait()
     col_logs = jnp.log(cols_buf[...].astype(f32))
     row_logs = shifted_row_logs(rows_buf)
     for j in range(HALVES):
         M_refs[j][n:, :] = jnp.broadcast_to(col_logs[:, j * n : (j + 1) * n], (8, width))
+    C0 = M_refs[0][:n, :]
     C = jnp.concatenate([ref[:n, :] for ref in M_refs], axis=0)
+    grad = None
     for i, rows in enumerate(spans):
         for copy in copies[head + 3 * i : head + 3 * i + 3]:
             copy.wait()
-        put_terms(x_buf[rows, :], row_logs, 4 * i, t_ref, c_ref, rows)
+        t, c = terms(x_buf[rows, :], row_logs, i * FIRST // row_logs.shape[0])
+        t_ref[rows, :] = t[:, n:]
+        c_ref[rows, :] = c[:, n:]
         W = W_buf[rows, :]
-        e = errors(dot(W, C, 1, 1), t_ref[rows, :], c_ref[rows, :], col_logs)
-        Wo_ref[rows, :], Ao_ref[rows, :] = adagrad(W, A_buf[rows, :], dot(e, C, 1, 0))
+        g = dot(errors(dot(W, C, 1, 1), t, c, col_logs), C, 1, 0)
+        W, Ao_ref[rows, :] = adagrad(W, A_buf[rows, :], g)
+        Wo_ref[rows, :] = W
+        part = dot(W, errors(dot(W, C0, 1, 1), t[:, :n], c[:, :n], col_logs[:, :n]), 0, 0)
+        grad = part if grad is None else grad + part
+    h_ref[...] = grad.T
     for copy in late:
         copy.wait()
 
 
 def half_errors(j, W, t_ref, c_ref, M_ref, rows):
     n = M_ref.shape[1]
-    cols = pl.ds(j * n, n)
+    cols = pl.ds(j * n if t_ref.shape[1] > n else 0, n)
     C = M_ref[:n, :]
     e = errors(dot(W, C, 1, 1), t_ref[rows, cols], c_ref[rows, cols], M_ref[n : n + 1, :])
     return e, C
@@ -161,12 +169,17 @@
 
 
 def final_kernel(*refs):
-    ins, (Co_ref, Bo_ref) = refs[:-2], refs[-2:]
+    ins, (Co_hbm, Bo_hbm, C_buf, B_buf, sems) = refs[:-5], refs[-5:]
     n = ins[0].shape[0]
+    copies = []
     for j in range(HALVES):
         h_ref, M_ref, B_ref = ins[3 * j : 3 * j + 3]
         rows = pl.ds(j * n, n)
-        Co_ref[rows, :], Bo_ref[rows, :] = adagrad(M_ref[:n, :], B_ref[...], h_ref[...])
+        C_buf[rows, :], B_buf[rows, :] = adagrad(M_ref[:n, :], B_ref[...], h_ref[...])
+        pairs = [(C_buf.at[rows], Co_hbm.at[rows]), (B_buf.at[rows], Bo_hbm.at[rows])]
+        copies += fetches(pairs, sems.at[j])
+    for copy in copies:
+        copy.wait()
 
 
 def call(kernel, operands, spaces, outs, out_spaces, scratch, mib):
@@ -184,9 +197,9 @@
     steps = tile_counts.shape[1]
     n_outer, n_inner = lax.axis_size("outer"), lax.axis_size("inner")
 
-    def move(block, across, by=1):
+    def move(block, across):
         route = [
-            (o * n_inner + i, (o + across) % n_outer * n_inner + (i + by) % n_inner)
+            (o * n_inner + i, (o + across) % n_outer * n_inner + (i + 1) % n_inner)
             for o in range(n_outer)
             for i in range(n_inner)
         ]
@@ -200,11 +213,12 @@
     tile = tile_counts.shape[2:]
     half = (tall[0] // HALVES, tall[1])
     message = (half[0] + 8, half[1])
-    W, A, t, c, *blocks = call(
+    part = (tile[0], half[0])
+    W, A, t, c, h, *blocks = call(
         first_kernel, hbm, [H] * 7,
-        [wide, wide, tile, tile] + [message] * HALVES + [half] * HALVES, [V] * (4 + 2 * HALVES),
+        [wide, wide, part, part, half] + [message] * HALVES + [half] * HALVES, [V] * (5 + 2 * HALVES),
         [V(tile, jnp.int32), V(wide, f32), V(wide, f32), V(rows.shape, jnp.int32),
-         V(cols.shape, jnp.int32), DMA((4 + 3 * 2,)), DMA((HALVES,))],
+         V(cols.shape, jnp.int32), DMA((4 + 3 * (tile[0] // FIRST),)), DMA((HALVES,))],
         24,
     )
     M, B = blocks[:HALVES], blocks[HALVES:]
@@ -212,48 +226,53 @@
     def update(h, value, total):
         return call(update_kernel, (h, value, total), [V] * 3, [message, half], [V] * 2, [], 4)
 
+    def next_terms(step, tie):
+        row_tie = lax.optimization_barrier((rows, tie))[0]
+        return call(
+            functools.partial(terms_kernel, step + 1), (hbm[0], row_tie), [H, V], [tile, tile], [V] * 2,
+            [V(tile, jnp.int32), DMA((4,))], 12,
+        )
+
     halfway = steps // 2
-    early = None
     for step in range(steps):
-        h = None
+        h1 = None
         if step > 0:
-            if step == halfway:
-                M[0], B[0] = update(M[0], *early)
-            part = call(row_part_kernel, (t, c, M[0], W), [V] * 4, [wide], [V], [], 12)[0]
-            operands = (t, c, M[0], M[1], W, A, part)
+            g = call(row_part_kernel, (t, c, M[0], W), [V] * 4, [wide], [V], [], 12)[0]
+            operands = (t, c, M[0], M[1], W, A, g)
             if step + 1 == steps:
-                W, A, *grads = call(
+                W, A, h, h1 = call(
                     last_kernel, operands, [V] * 7, [wide, wide, half, half], [H, H, V, V],
                     [V(wide, f32), V(wide, f32), DMA((2, 2))], 20,
                 )
                 break
-            W, A, h = call(
-                functools.partial(row_col_kernel, 256, (0,), lambda rows: None), operands, [V] * 7,
-                [wide, wide, half], [V] * 3, [], 16,
-            )
-        if h is None:
-            h = call(functools.partial(col_kernel, 0), (t, c, M[0], W), [V] * 4, [half], [V], [], 12)[0]
+            if step == halfway:
+                W, A, h, h1 = call(
+                    functools.partial(row_col_kernel, 512, (0, 1), lambda rows: None), operands, [V] * 7,
+                    [wide, wide, half, half], [V] * 4, [], 20,
+                )
+            else:
+                W, A, h = call(
+                    functools.partial(row_col_kernel, 256, (0,), lambda rows: None), operands, [V] * 7,
+                    [wide, wide, half], [V] * 3, [], 16,
+                )
         across = int(step + 1 == halfway)
-        if across:
-            sent = [move(h, across)]
+        value, total = update(h, M[0], B[0])
+        sent = [move(value, across)]
+        if h1 is None:
+            h1 = call(functools.partial(col_kernel, 1), (t, c, M[1], W), [V] * 4, [half], [V], [], 12)[0]
         else:
-            value, total = update(h, M[0], B[0])
-            sent = [move(value, across)]
-        h = call(functools.partial(col_kernel, 1), (t, c, M[1], W), [V] * 4, [half], [V], [], 12)[0]
-        last_value, last_total = update(h, M[1], B[1])
+            t, c = next_terms(step, total)
+            h1 = lax.optimization_barrier((h1, t))[0]
+        last_value, last_total = update(h1, M[1], B[1])
+        if step != halfway:
+            t, c = next_terms(step, last_total)
         sent.append(move(last_value, across))
-        row_tie = lax.optimization_barrier((rows, last_total))[0]
-        t, c = call(
-            functools.partial(terms_kernel, step + 1), (hbm[0], row_tie), [H, V], [tile, tile], [V] * 2,
-            [V(tile, jnp.int32), DMA((4,))], 12,
-        )
-        M, B = sent, [None, move(last_total, across)]
-        if step + 2 == halfway:
-            early = [move(value, 1, 2), move(total, 1, 2)]
-        elif not across:
-            B[0] = move(total, across)
-    operands = (grads[0], M[0], B[0], grads[1], M[1], B[1])
-    C, B = call(final_kernel, operands, [V] * 6, [tall, tall], [V] * 2, [], 6)
+        M, B = sent, [move(total, across), move(last_total, across)]
+    operands = (h, M[0], B[0], h1, M[1], B[1])
+    C, B = call(
+        final_kernel, operands, [V] * 6, [tall, tall], [H] * 2,
+        [V(tall, f32), V(tall, f32), DMA((HALVES, 2))], 6,
+    )
     return W, A, C, B
 
 

time: 79.9 us -> 70.5 us (0.88)
  waiting for transfers between devices: 35.2 us -> 27.1 us
  starting transfers between devices: 8.26 us -> 6.9 us
    ppermute x12, waiting for transfers between devices: 35.2 us -> 27.1 us  [move(): return lax.ppermute(block, ('outer', 'inner'), route)]
    ppermute x12, starting transfers between devices: 8.26 us -> 6.9 us  [move(): return lax.ppermute(block, ('outer', 'inner'), route)]
    pallas_call x21 -> x19, Pallas kernels: 35.4 us -> 35.3 us  [call(): pl.pallas_call(kernel, in_specs=[pl.BlockSpec(memory_space=s) for s in sp...]
  transfers between devices with their start and end apart: 12 -> 12, of which waited for: 7 -> 10; matrix products, arithmetic and copies ran while one was open for 0% -> 0% of each run, Pallas kernels for 34% -> 38%
where the time goes in v5:
time: 70.5 us; the launch traced here: 70.3 us
  Pallas kernels  35.3 us (50%)
  waiting for transfers between devices  27.1 us (38%)
  starting transfers between devices  6.9 us (10%)
  between operations  1.01 us (1%)
    pallas_call x19, Pallas kernels, call(): pl.pallas_call(kernel, in_specs=[pl.BlockSpec(memory_space=s) for s in sp...  35.3 us
    ppermute x12, waiting for transfers between devices, move(): return lax.ppermute(block, ('outer', 'inner'), route)  27.1 us
    ppermute x12, starting transfers between devices, move(): return lax.ppermute(block, ('outer', 'inner'), route)  6.9 us
  transfers between devices with their start and end apart: 12, of which 10 were waited for; matrix products, arithmetic and copies ran while one was open for 0% of the time, Pallas kernels for 38%

profile of v5, /device:TPU:0, one launch (start us, length us, event | category | flops | bytes accessed | tf_op | source)
XLA Modules:
  0.0 70.3 jit_solution(8209365114740672030)
XLA Ops:
  0.6 7.5 %shard_map.102 = (f32[1024,256]{1,0:T(8,128)S(1)}, f32[1024,256]{1,0:T(8,128)S(1)}, f32[1024,256]{1,0:T(8,128)S(1)}, f32[1024,256]{1,0:T(8,128)S(1)}, f32[256,25...) custom-call(s32[1,4,1024,512]{3,2,1,0:T(8,128)} %x_hbm.7, ...), custom_call_target="tpu_custom_call" | custom-call | tf_op jit(solution)/shard_map/pallas_call | solution.py:186
  8.3 1.7 %shard_map.103.h_ref = f32[256,256]{1,0:T(8,128)S(1)} custom-call(f32[1024,256]{1,0:T(8,128)S(1)} %get-tuple-element.48.t_ref, f32[1024,256]{1,0:T(8,128)S(1)} %get-tuple-element.49.c_ref, f32[264,256]{1,0:T(8,128)S(1)} %get-tuple-element.50.M_ref, f32[1024,256]{1,0:T(8,128)S(1)} %get-tuple-element.51.W_ref), custom_call_target="tpu_custom_call" | custom-call | tf_op jit(solution)/shard_map/pallas_call | solution.py:186
  10.1 1.8 %collective-permute-start = (f32[264,256]{1,0:T(8,128)S(1)}, f32[264,256]{1,0:T(8,128)S(1)}, u32[]{:S(2)}, u32[]{:S(2)}) collective-permute-start(f32[264,256]{1,0:T(8,128)S(1)} %get-tuple-element.57), channel_id=1, source_target_pairs={{0,1},{1,2},{2,3},{3,4},{4,5},{5,6},{6,7},{7,8},{8,9},{9,10},{10,1... | collective-permute-start | bytes 811016 | tf_op jit(solution)/shard_map/ppermute | solution.py:206
  12.1 1.4 %collective-permute-start.2 = (f32[256,256]{1,0:T(8,128)S(1)}, f32[256,256]{1,0:T(8,128)S(1)}, u32[]{:S(2)}, u32[]{:S(2)}) collective-permute-start(f32[256,256]{1,0:T(8,128)S(1)} %get-tuple-element.53), channel_id=1, source_target_pairs={{0,1},{1,2},{2,3},{3,4},{4,5},{5,6},{6,7},{7,8},{8,9},{9,10},{10,1... | collective-permute-start | bytes 786440 | tf_op jit(solution)/shard_map/ppermute | solution.py:206
  13.5 1.9 %shard_map.105 = (f32[1024,512]{1,0:T(8,128)S(1)}, f32[1024,512]{1,0:T(8,128)S(1)}) custom-call(s32[1,4,1024,512]{3,2,1,0:T(8,128)} %x_hbm.7, s32[8,128]{1,0:T(8,128)S(1)} %bitcast.3), custom_call_target="tpu_custom_call" | custom-call | tf_op jit(solution)/shard_map/pallas_call | solution.py:186
  15.4 3.9 %collective-permute-done.1.M_ref.M0_ref = f32[264,256]{1,0:T(8,128)S(1)} collective-permute-done((f32[264,256]{1,0:T(8,128)S(1)}, f32[264,256]{1,0:T(8,128)S(1)}, u32[]{:S(2)}, u32[]{:S(2)}) %collective-permute-start.1) | collective-permute-done | bytes 270368 | tf_op jit(solution)/shard_map/ppermute | solution.py:206
  19.2 1.6 %shard_map.107.g_ref = f32[1024,256]{1,0:T(8,128)S(1)} custom-call(f32[1024,512]{1,0:T(8,128)S(1)} %get-tuple-element.55.t_ref, f32[1024,512]{1,0:T(8,128)S(1)} %get-tuple-element.56.c_ref, f32[264,256]{1,0:T(8,128)S(1)} %collective-permute-done.1.M_ref.M0_ref, f32[1024,256]{1,0:T(8,128)S(1)} %get-tuple-element.51.W_ref), custom_call_target="tpu_custom_call" | custom-call | tf_op jit(solution)/shard_map/pallas_call | solution.py:186
  20.8 1.3 %collective-permute-done.M1_ref.M_ref = f32[264,256]{1,0:T(8,128)S(1)} collective-permute-done((f32[264,256]{1,0:T(8,128)S(1)}, f32[264,256]{1,0:T(8,128)S(1)}, u32[]{:S(2)}, u32[]{:S(2)}) %collective-permute-start) | collective-permute-done | bytes 270368 | tf_op jit(solution)/shard_map/ppermute | solution.py:206
  22.1 3.2 %shard_map.108 = (f32[1024,256]{1,0:T(8,128)S(1)}, f32[1024,256]{1,0:T(8,128)S(1)}, f32[256,256]{1,0:T(8,128)S(1)}) custom-call(f32[1024,512]{1,0:T(8,128)S(1)} %get-tuple-element.55.t_ref, f32[1024,512]{1,0:T(8,128)S(1)} %get-tuple-element.56.c_ref, f32[264,256]{1,0:T(8,128)S(1)} %collective-permute-done.1.M_ref.M0_ref, ...), custom_call_target="tpu_custom_call" | custom-call | tf_op jit(solution)/shard_map/pallas_call | solution.py:186
  25.6 1.7 %shard_map.109.h_ref = f32[256,256]{1,0:T(8,128)S(1)} custom-call(f32[1024,512]{1,0:T(8,128)S(1)} %get-tuple-element.55.t_ref, f32[1024,512]{1,0:T(8,128)S(1)} %get-tuple-element.56.c_ref, f32[264,256]{1,0:T(8,128)S(1)} %collective-permute-done.M1_ref.M_ref, f32[1024,256]{1,0:T(8,128)S(1)} %get-tuple-element.63.W_ref), custom_call_target="tpu_custom_call" | custom-call | tf_op jit(solution)/shard_map/pallas_call | solution.py:186
  28.0 1.9 %collective-permute-start.8 = (f32[256,256]{1,0:T(8,128)S(1)}, f32[256,256]{1,0:T(8,128)S(1)}, u32[]{:S(2)}, u32[]{:S(2)}) collective-permute-start(f32[256,256]{1,0:T(8,128)S(1)} %get-tuple-element.64), channel_id=1, source_target_pairs={{0,65},{1,66},{2,67},{3,68},{4,69},{5,70},{6,71},{7,72},{8,73},{9,... | collective-permute-start | bytes 786440 | tf_op jit(solution)/shard_map/ppermute | solution.py:206
  29.9 1.9 %shard_map.111 = (f32[1024,512]{1,0:T(8,128)S(1)}, f32[1024,512]{1,0:T(8,128)S(1)}) custom-call(s32[1,4,1024,512]{3,2,1,0:T(8,128)} %x_hbm.7, s32[8,128]{1,0:T(8,128)S(1)} %bitcast.4), custom_call_target="tpu_custom_call" | custom-call | tf_op jit(solution)/shard_map/pallas_call | solution.py:186
  31.8 7.2 %collective-permute-done.4.M_ref.M0_ref = f32[264,256]{1,0:T(8,128)S(1)} collective-permute-done((f32[264,256]{1,0:T(8,128)S(1)}, f32[264,256]{1,0:T(8,128)S(1)}, u32[]{:S(2)}, u32[]{:S(2)}) %collective-permute-start.4) | collective-permute-done | bytes 270368 | tf_op jit(solution)/shard_map/ppermute | solution.py:206
  39.0 1.6 %shard_map.113.g_ref = f32[1024,256]{1,0:T(8,128)S(1)} custom-call(f32[1024,512]{1,0:T(8,128)S(1)} %get-tuple-element.66.t_ref, f32[1024,512]{1,0:T(8,128)S(1)} %get-tuple-element.67.c_ref, f32[264,256]{1,0:T(8,128)S(1)} %collective-permute-done.4.M_ref.M0_ref, f32[1024,256]{1,0:T(8,128)S(1)} %get-tuple-element.63.W_ref), custom_call_target="tpu_custom_call" | custom-call | tf_op jit(solution)/shard_map/pallas_call | solution.py:186
  40.6 3.2 %collective-permute-done.5.M1_ref.M_ref = f32[264,256]{1,0:T(8,128)S(1)} collective-permute-done((f32[264,256]{1,0:T(8,128)S(1)}, f32[264,256]{1,0:T(8,128)S(1)}, u32[]{:S(2)}, u32[]{:S(2)}) %collective-permute-start.5) | collective-permute-done | bytes 270368 | tf_op jit(solution)/shard_map/ppermute | solution.py:206
  43.8 4.4 %shard_map.114 = (f32[1024,256]{1,0:T(8,128)S(1)}, f32[1024,256]{1,0:T(8,128)S(1)}, f32[256,256]{1,0:T(8,128)S(1)}, f32[256,256]{1,0:T(8,128)S(1)}) custom-call(f32[1024,512]{1,0:T(8,128)S(1)} %get-tuple-element.66.t_ref, f32[1024,512]{1,0:T(8,128)S(1)} %get-tuple-element.67.c_ref, f32[264,256]{1,0:T(8,128)S(1)} %collective-permute-done.4.M_ref.M0_ref, ...), custom_call_target="tpu_custom_call" | custom-call | tf_op jit(solution)/shard_map/pallas_call | solution.py:186
  49.2 1.9 %shard_map.116 = (f32[1024,512]{1,0:T(8,128)S(1)}, f32[1024,512]{1,0:T(8,128)S(1)}) custom-call(s32[1,4,1024,512]{3,2,1,0:T(8,128)} %x_hbm.7, s32[8,128]{1,0:T(8,128)S(1)} %bitcast.5), custom_call_target="tpu_custom_call" | custom-call | tf_op jit(solution)/shard_map/pallas_call | solution.py:186
  51.2 2.0 %collective-permute-done.8.B_ref = f32[256,256]{1,0:T(8,128)S(1)} collective-permute-done((f32[256,256]{1,0:T(8,128)S(1)}, f32[256,256]{1,0:T(8,128)S(1)}, u32[]{:S(2)}, u32[]{:S(2)}) %collective-permute-start.8) | collective-permute-done | bytes 262176 | tf_op jit(solution)/shard_map/ppermute | solution.py:206
  53.9 4.8 %collective-permute-done.7.M_ref.refs_2_.refs_1_ = f32[264,256]{1,0:T(8,128)S(1)} collective-permute-done((f32[264,256]{1,0:T(8,128)S(1)}, f32[264,256]{1,0:T(8,128)S(1)}, u32[]{:S(2)}, u32[]{:S(2)}) %collective-permute-start.7) | collective-permute-done | bytes 270368 | tf_op jit(solution)/shard_map/ppermute | solution.py:206
  58.7 1.6 %shard_map.118.refs_6_ = f32[1024,256]{1,0:T(8,128)S(1)} custom-call(f32[1024,512]{1,0:T(8,128)S(1)} %get-tuple-element.77.t_ref.refs_0_, f32[1024,512]{1,0:T(8,128)S(1)} %get-tuple-element.78.c_ref.refs_1_, f32[264,256]{1,0:T(8,128)S(1)} %collective-permute-done.7.M_ref.refs_2_.refs_1_, f32[1024,256]{1,0:T(8,128)S(1)} %get-tuple-element.83.W_ref.refs_4_), custom_call_target="tpu_custom_call" | custom-call | tf_op jit(solution)/shard_map/pallas_call | solution.py:186
  60.3 3.1 %collective-permute-done.9.refs_3_.refs_4_ = f32[264,256]{1,0:T(8,128)S(1)} collective-permute-done((f32[264,256]{1,0:T(8,128)S(1)}, f32[264,256]{1,0:T(8,128)S(1)}, u32[]{:S(2)}, u32[]{:S(2)}) %collective-permute-start.9) | collective-permute-done | bytes 270368 | tf_op jit(solution)/shard_map/ppermute | solution.py:206
  63.4 4.8 %shard_map.119 = (f32[1024,256]{1,0:T(8,128)}, f32[1024,256]{1,0:T(8,128)}, f32[256,256]{1,0:T(8,128)S(1)}, f32[256,256]{1,0:T(8,128)S(1)}) custom-call(f32[1024,512]{1,0:T(8,128)S(1)} %get-tuple-element.77.t_ref.refs_0_, f32[1024,512]{1,0:T(8,128)S(1)} %get-tuple-element.78.c_ref.refs_1_, f32[264,256]{1,0:T(8,128)S(1)} %collective-permute-done.7.M_ref.refs_2_.refs_1_, ...), custom_call_target="tpu_custom_call" | custom-call | tf_op jit(solution)/shard_map/pallas_call | solution.py:186
  68.2 0.8 %collective-permute-done.11.refs_5_ = f32[256,256]{1,0:T(8,128)S(1)} collective-permute-done((f32[256,256]{1,0:T(8,128)S(1)}, f32[256,256]{1,0:T(8,128)S(1)}, u32[]{:S(2)}, u32[]{:S(2)}) %collective-permute-start.11) | collective-permute-done | bytes 262176 | tf_op jit(solution)/shard_map/ppermute | solution.py:206
  69.0 1.1 %shard_map.120 = (f32[512,256]{1,0:T(8,128)}, f32[512,256]{1,0:T(8,128)}) custom-call(f32[256,256]{1,0:T(8,128)S(1)} %get-tuple-element.87.refs_0_, f32[264,256]{1,0:T(8,128)S(1)} %collective-permute-done.7.M_ref.refs_2_.refs_1_, f32[256,256]{1,0:T(8,128)S(1)} %collective-permute-done.10.refs_2_, f32[256,256]{1,0:T(8,128)S(1)} %get-tuple-element.88.refs_3_, ...), custom_call_target="tpu_custom_call" | custom-call | tf_op jit(solution)/shard_map/pallas_call | solution.py:186
  (21 shorter events, 2.9 us)
Async XLA Ops:
  8.2 11.0 %collective-permute-start.1 = (f32[264,256]{1,0:T(8,128)S(1)}, f32[264,256]{1,0:T(8,128)S(1)}, u32[]{:S(2)}, u32[]{:S(2)}) collective-permute-start(f32[264,256]{1,0:T(8,128)S(1)} %get-tuple-element.61), channel_id=1, source_target_pairs={{0,1},{1,2},{2,3},{3,4},{4,5},{5,6},{6,7},{7,8},{8,9},{9,10},{10,1... | collective-permute-start | bytes 811016 | tf_op jit(solution)/shard_map/ppermute | solution.py:206
  8.3 5.2 %copy-start = (s32[1024]{0:T(1024)S(1)}, s32[1024]{0:T(1024)}, u32[]{:S(2)}) copy-start(s32[1024]{0:T(1024)} %param.8) | copy-start | bytes 12292
  10.1 12.0 %collective-permute-start = (f32[264,256]{1,0:T(8,128)S(1)}, f32[264,256]{1,0:T(8,128)S(1)}, u32[]{:S(2)}, u32[]{:S(2)}) collective-permute-start(f32[264,256]{1,0:T(8,128)S(1)} %get-tuple-element.57), channel_id=1, source_target_pairs={{0,1},{1,2},{2,3},{3,4},{4,5},{5,6},{6,7},{7,8},{8,9},{9,10},{10,1... | collective-permute-start | bytes 811016 | tf_op jit(solution)/shard_map/ppermute | solution.py:206
  12.0 13.4 %collective-permute-start.3 = (f32[256,256]{1,0:T(8,128)S(1)}, f32[256,256]{1,0:T(8,128)S(1)}, u32[]{:S(2)}, u32[]{:S(2)}) collective-permute-start(f32[256,256]{1,0:T(8,128)S(1)} %get-tuple-element.69), channel_id=1, source_target_pairs={{0,1},{1,2},{2,3},{3,4},{4,5},{5,6},{6,7},{7,8},{8,9},{9,10},{10,1... | collective-permute-start | bytes 786440 | tf_op jit(solution)/shard_map/ppermute | solution.py:206
  12.1 15.7 %collective-permute-start.2 = (f32[256,256]{1,0:T(8,128)S(1)}, f32[256,256]{1,0:T(8,128)S(1)}, u32[]{:S(2)}, u32[]{:S(2)}) collective-permute-start(f32[256,256]{1,0:T(8,128)S(1)} %get-tuple-element.53), channel_id=1, source_target_pairs={{0,1},{1,2},{2,3},{3,4},{4,5},{5,6},{6,7},{7,8},{8,9},{9,10},{10,1... | collective-permute-start | bytes 786440 | tf_op jit(solution)/shard_map/ppermute | solution.py:206
  25.5 13.6 %collective-permute-start.4 = (f32[264,256]{1,0:T(8,128)S(1)}, f32[264,256]{1,0:T(8,128)S(1)}, u32[]{:S(2)}, u32[]{:S(2)}) collective-permute-start(f32[264,256]{1,0:T(8,128)S(1)} %get-tuple-element.70), channel_id=1, source_target_pairs={{0,65},{1,66},{2,67},{3,68},{4,69},{5,70},{6,71},{7,72},{8,73},{9,... | collective-permute-start | bytes 811016 | tf_op jit(solution)/shard_map/ppermute | solution.py:206
  27.8 16.0 %collective-permute-start.5 = (f32[264,256]{1,0:T(8,128)S(1)}, f32[264,256]{1,0:T(8,128)S(1)}, u32[]{:S(2)}, u32[]{:S(2)}) collective-permute-start(f32[264,256]{1,0:T(8,128)S(1)} %get-tuple-element.71), channel_id=1, source_target_pairs={{0,65},{1,66},{2,67},{3,68},{4,69},{5,70},{6,71},{7,72},{8,73},{9,... | collective-permute-start | bytes 811016 | tf_op jit(solution)/shard_map/ppermute | solution.py:206
  27.9 20.6 %collective-permute-start.6 = (f32[256,256]{1,0:T(8,128)S(1)}, f32[256,256]{1,0:T(8,128)S(1)}, u32[]{:S(2)}, u32[]{:S(2)}) collective-permute-start(f32[256,256]{1,0:T(8,128)S(1)} %get-tuple-element.74), channel_id=1, source_target_pairs={{0,65},{1,66},{2,67},{3,68},{4,69},{5,70},{6,71},{7,72},{8,73},{9,... | collective-permute-start | bytes 786440 | tf_op jit(solution)/shard_map/ppermute | solution.py:206
  28.0 25.2 %collective-permute-start.8 = (f32[256,256]{1,0:T(8,128)S(1)}, f32[256,256]{1,0:T(8,128)S(1)}, u32[]{:S(2)}, u32[]{:S(2)}) collective-permute-start(f32[256,256]{1,0:T(8,128)S(1)} %get-tuple-element.64), channel_id=1, source_target_pairs={{0,65},{1,66},{2,67},{3,68},{4,69},{5,70},{6,71},{7,72},{8,73},{9,... | collective-permute-start | bytes 786440 | tf_op jit(solution)/shard_map/ppermute | solution.py:206
  48.6 10.2 %collective-permute-start.7 = (f32[264,256]{1,0:T(8,128)S(1)}, f32[264,256]{1,0:T(8,128)S(1)}, u32[]{:S(2)}, u32[]{:S(2)}) collective-permute-start(f32[264,256]{1,0:T(8,128)S(1)} %get-tuple-element.79), channel_id=1, source_target_pairs={{0,1},{1,2},{2,3},{3,4},{4,5},{5,6},{6,7},{7,8},{8,9},{9,10},{10,1... | collective-permute-start | bytes 811016 | tf_op jit(solution)/shard_map/ppermute | solution.py:206
  53.2 10.2 %collective-permute-start.9 = (f32[264,256]{1,0:T(8,128)S(1)}, f32[264,256]{1,0:T(8,128)S(1)}, u32[]{:S(2)}, u32[]{:S(2)}) collective-permute-start(f32[264,256]{1,0:T(8,128)S(1)} %get-tuple-element.82), channel_id=1, source_target_pairs={{0,1},{1,2},{2,3},{3,4},{4,5},{5,6},{6,7},{7,8},{8,9},{9,10},{10,1... | collective-permute-start | bytes 811016 | tf_op jit(solution)/shard_map/ppermute | solution.py:206
  53.5 14.7 %collective-permute-start.10 = (f32[256,256]{1,0:T(8,128)S(1)}, f32[256,256]{1,0:T(8,128)S(1)}, u32[]{:S(2)}, u32[]{:S(2)}) collective-permute-start(f32[256,256]{1,0:T(8,128)S(1)} %get-tuple-element.75), channel_id=1, source_target_pairs={{0,1},{1,2},{2,3},{3,4},{4,5},{5,6},{6,7},{7,8},{8,9},{9,10},{10,1... | collective-permute-start | bytes 786440 | tf_op jit(solution)/shard_map/ppermute | solution.py:206
  53.6 15.5 %collective-permute-start.11 = (f32[256,256]{1,0:T(8,128)S(1)}, f32[256,256]{1,0:T(8,128)S(1)}, u32[]{:S(2)}, u32[]{:S(2)}) collective-permute-start(f32[256,256]{1,0:T(8,128)S(1)} %get-tuple-element.89), channel_id=1, source_target_pairs={{0,1},{1,2},{2,3},{3,4},{4,5},{5,6},{6,7},{7,8},{8,9},{9,10},{10,1... | collective-permute-start | bytes 786440 | tf_op jit(solution)/shard_map/ppermute | solution.py:206

commit v6 on v3

--- a/solution.py
+++ b/solution.py
@@ -6,6 +6,7 @@
 from jax.experimental import pallas as pl
 from jax.experimental.pallas import tpu as pltpu
 from jax.sharding import PartitionSpec as P
+
 
 LOG_TOTAL = 17.0
 LEARNING = 0.05
@@ -147,10 +148,13 @@
     grad = None
     for rows in row_spans(W_ref.shape[0], 256):
         W = W_ref[rows, :]
-        e, _ = half_errors(j, W, t_ref, c_ref, M_ref, rows)
-        part = dot(W, e, 0, 0)
+        part = dot(half_errors(j, W, t_ref, c_ref, M_ref, rows)[0], W, 0, 0)
         grad = part if grad is None else grad + part
-    h_ref[...] = grad.T
+    h_ref[...] = grad
+
+
+def join_kernel(a_ref, b_ref, o_ref):
+    o_ref[...] = a_ref[...] + b_ref[...]
 
 
 def update_kernel(h_ref, M_ref, B_ref, Mo_ref, Bo_ref):
@@ -168,7 +172,7 @@
         Co_ref[rows, :], Bo_ref[rows, :] = adagrad(M_ref[:n, :], B_ref[...], h_ref[...])
 
 
-def call(kernel, operands, spaces, outs, out_spaces, scratch, mib, name):
+def call(kernel, operands, spaces, outs, out_spaces, scratch, mib):
     return pl.pallas_call(
         kernel,
         in_specs=[pl.BlockSpec(memory_space=s) for s in spaces],
@@ -176,7 +180,6 @@
         out_shape=[jax.ShapeDtypeStruct(s, f32) for s in outs],
         scratch_shapes=scratch,
         compiler_params=pltpu.CompilerParams(vmem_limit_bytes=mib << 20),
-        name=name,
     )(*operands)
 
 
@@ -184,13 +187,18 @@
     steps = tile_counts.shape[1]
     n_outer, n_inner = lax.axis_size("outer"), lax.axis_size("inner")
 
-    def move(block, across):
+    def move(block, across, senders=(0, 1)):
         route = [
             (o * n_inner + i, (o + across) % n_outer * n_inner + (i + 1) % n_inner)
             for o in range(n_outer)
             for i in range(n_inner)
+            if i % 2 in senders
         ]
         return lax.ppermute(block, ("outer", "inner"), route)
+
+    def join(pair):
+        shape = pair[0].shape
+        return call(join_kernel, pair, [V] * 2, [shape], [V], [], 4)[0]
 
     rows = row_counts.reshape(-1, 128)
     cols = col_counts.reshape(1, -1)
@@ -205,43 +213,69 @@
         [wide, wide, tile, tile] + [message] * HALVES + [half] * HALVES, [V] * (4 + 2 * HALVES),
         [V(tile, jnp.int32), V(wide, f32), V(wide, f32), V(rows.shape, jnp.int32),
          V(cols.shape, jnp.int32), DMA((4 + 3 * 2,)), DMA((HALVES,))],
-        24, "first",
+        24,
     )
     M, B = blocks[:HALVES], blocks[HALVES:]
+
+    def update(h, value, total):
+        return call(update_kernel, (h, value, total), [V] * 3, [message, half], [V] * 2, [], 4)
+
+    def next_terms(step, tie):
+        row_tie = lax.optimization_barrier((rows, tie))[0]
+        return call(
+            functools.partial(terms_kernel, step + 1), (hbm[0], row_tie), [H, V], [tile, tile], [V] * 2,
+            [V(tile, jnp.int32), DMA((4,))], 12,
+        )
+
+    halfway = steps // 2
     for step in range(steps):
         h = None
         if step > 0:
-            part = call(row_part_kernel, (t, c, M[0], W), [V] * 4, [wide], [V], [], 12, "row")[0]
-            operands = (t, c, M[0], M[1], W, A, part)
+            g = call(row_part_kernel, (t, c, M[0], W), [V] * 4, [wide], [V], [], 12)[0]
+            operands = (t, c, M[0], M[1], W, A, g)
             if step + 1 == steps:
                 W, A, *grads = call(
                     last_kernel, operands, [V] * 7, [wide, wide, half, half], [H, H, V, V],
-                    [V(wide, f32), V(wide, f32), DMA((2, 2))], 20, "last",
+                    [V(wide, f32), V(wide, f32), DMA((2, 2))], 20,
                 )
                 break
-            W, A, h = call(
-                functools.partial(row_col_kernel, 256, (0,), lambda rows: None), operands, [V] * 7,
-                [wide, wide, half], [V] * 3, [], 16, "row_col",
-            )
-        across = int(step + 1 == steps // 2)
+            if step == halfway:
+                W, A, *grads = call(
+                    functools.partial(row_col_kernel, 512, (0, 1), lambda rows: None), operands, [V] * 7,
+                    [wide, wide, half, half], [V] * 4, [], 20,
+                )
+            else:
+                W, A, h = call(
+                    functools.partial(row_col_kernel, 256, (0,), lambda rows: None), operands, [V] * 7,
+                    [wide, wide, half], [V] * 3, [], 16,
+                )
+        if step == halfway:
+            odd = [update(grads[j], M[j], B[j][0])[0] for j in range(HALVES)]
+            to_even = [move(odd[j], 0, (1,)) for j in range(HALVES)]
+            tied = lax.optimization_barrier((*grads, *odd))[:HALVES]
+            both = [update(tied[j], M[j], join(B[j])) for j in range(HALVES)]
+            to_odd = [move(both[j][0], 0, (0,)) for j in range(HALVES)]
+            t, c = next_terms(step, both[1][1])
+            M = [join(pair) for pair in zip(to_even, to_odd)]
+            B = [move(both[j][1], 0) for j in range(HALVES)]
+            continue
+        across = int(step + 1 == halfway)
         sent, sums = [], []
         for j in range(HALVES):
             if h is None or j > 0:
                 operands = (t, c, M[j], W)
-                h = call(functools.partial(col_kernel, j), operands, [V] * 4, [half], [V], [], 12, "col")[0]
-            value, total = call(
-                update_kernel, (h, M[j], B[j]), [V] * 3, [message, half], [V] * 2, [], 4, "update"
-            )
+                h = call(functools.partial(col_kernel, j), operands, [V] * 4, [half], [V], [], 12)[0]
+            value, total = update(h, M[j], B[j])
             sent.append(move(value, across))
             sums.append(total)
-        row_tie = lax.optimization_barrier((rows, *sums))[0]
-        t, c = call(
-            functools.partial(terms_kernel, step + 1), (hbm[0], row_tie), [H, V], [tile, tile], [V] * 2,
-            [V(tile, jnp.int32), DMA((4,))], 12, "terms",
-        )
-        M, B = sent, [move(total, across) for total in sums]
+        t, c = next_terms(step, sums[-1])
+        M = sent
+        if across:
+            B = [(move(total, across, (0,)), move(total, across, (1,))) for total in sums]
+        else:
+            B = [move(total, across) for total in sums]
     operands = (grads[0], M[0], B[0], grads[1], M[1], B[1])
-    C, B = call(final_kernel, operands, [V] * 6, [tall, tall], [V] * 2, [], 6, "final")
+    C, B = call(final_kernel, operands, [V] * 6, [tall, tall], [V] * 2, [], 6)
     return W, A, C, B
 
 

time: 69.7 us -> 81.3 us (1.17)
  starting transfers between devices: 7.52 us -> 22.8 us
  waiting for transfers between devices: 25.8 us -> 21.3 us
    ppermute x12 -> x16, starting transfers between devices: 7.52 us -> 22.8 us  [move(): return lax.ppermute(block, ('outer', 'inner'), route)]
    ppermute x12 -> x16, waiting for transfers between devices: 25.8 us -> 21.3 us  [move(): return lax.ppermute(block, ('outer', 'inner'), route)]
    pallas_call x21 -> x26, Pallas kernels: 35.4 us -> 36 us  [call(): pl.pallas_call(kernel, in_specs=[pl.BlockSpec(memory_space=s) for s in sp...]
  transfers between devices with their start and end apart: 12 -> 16, of which waited for: 10 -> 8; matrix products, arithmetic and copies ran while one was open for 0% -> 0% of each run, Pallas kernels for 39% -> 35%
where the time goes in v6:
time: 81.3 us; the launch traced here: 81 us
  Pallas kernels  36 us (44%)
  starting transfers between devices  22.8 us (28%)
  waiting for transfers between devices  21.3 us (26%)
  between operations  0.92 us (1%)
    pallas_call x26, Pallas kernels, call(): pl.pallas_call(kernel, in_specs=[pl.BlockSpec(memory_space=s) for s in sp...  36 us
    ppermute x16, starting transfers between devices, move(): return lax.ppermute(block, ('outer', 'inner'), route)  22.8 us
    ppermute x16, waiting for transfers between devices, move(): return lax.ppermute(block, ('outer', 'inner'), route)  21.3 us
  transfers between devices with their start and end apart: 16, of which 8 were waited for; matrix products, arithmetic and copies ran while one was open for 0% of the time, Pallas kernels for 35%

profile of v6, /device:TPU:0, one launch (start us, length us, event | category | flops | bytes accessed | tf_op | source)
XLA Modules:
  0.0 81.0 jit_solution(3871806102716724813)
XLA Ops:
  0.6 5.2 %shard_map.102 = (f32[1024,256]{1,0:T(8,128)S(1)}, f32[1024,256]{1,0:T(8,128)S(1)}, f32[1024,512]{1,0:T(8,128)S(1)}, f32[1024,512]{1,0:T(8,128)S(1)}, f32[264,25...) custom-call(s32[1,4,1024,512]{3,2,1,0:T(8,128)} %x_hbm.7, ...), custom_call_target="tpu_custom_call" | custom-call | tf_op jit(solution)/shard_map/pallas_call | solution.py:176
  5.9 1.6 %shard_map.106.h_ref = f32[256,256]{1,0:T(8,128)S(1)} custom-call(f32[1024,512]{1,0:T(8,128)S(1)} %get-tuple-element.50.t_ref, f32[1024,512]{1,0:T(8,128)S(1)} %get-tuple-element.51.c_ref, f32[264,256]{1,0:T(8,128)S(1)} %get-tuple-element.60.M_ref, f32[1024,256]{1,0:T(8,128)S(1)} %get-tuple-element.53.W_ref), custom_call_target="tpu_custom_call" | custom-call | tf_op jit(solution)/shard_map/pallas_call | solution.py:176
  7.6 1.6 %shard_map.103.h_ref = f32[256,256]{1,0:T(8,128)S(1)} custom-call(f32[1024,512]{1,0:T(8,128)S(1)} %get-tuple-element.50.t_ref, f32[1024,512]{1,0:T(8,128)S(1)} %get-tuple-element.51.c_ref, f32[264,256]{1,0:T(8,128)S(1)} %get-tuple-element.52.M_ref, f32[1024,256]{1,0:T(8,128)S(1)} %get-tuple-element.53.W_ref), custom_call_target="tpu_custom_call" | custom-call | tf_op jit(solution)/shard_map/pallas_call | solution.py:176
  9.3 1.8 %collective-permute-start = (f32[264,256]{1,0:T(8,128)S(1)}, f32[264,256]{1,0:T(8,128)S(1)}, u32[]{:S(2)}, u32[]{:S(2)}) collective-permute-start(f32[264,256]{1,0:T(8,128)S(1)} %get-tuple-element.59), channel_id=1, source_target_pairs={{0,1},{1,2},{2,3},{3,4},{4,5},{5,6},{6,7},{7,8},{8,9},{9,10},{10,1... | collective-permute-start | bytes 811016 | tf_op jit(solution)/shard_map/ppermute | solution.py:197
  11.2 1.4 %collective-permute-start.2 = (f32[256,256]{1,0:T(8,128)S(1)}, f32[256,256]{1,0:T(8,128)S(1)}, u32[]{:S(2)}, u32[]{:S(2)}) collective-permute-start(f32[256,256]{1,0:T(8,128)S(1)} %get-tuple-element.55), channel_id=1, source_target_pairs={{0,1},{1,2},{2,3},{3,4},{4,5},{5,6},{6,7},{7,8},{8,9},{9,10},{10,1... | collective-permute-start | bytes 786440 | tf_op jit(solution)/shard_map/ppermute | solution.py:197
  12.6 1.9 %shard_map.105 = (f32[1024,512]{1,0:T(8,128)S(1)}, f32[1024,512]{1,0:T(8,128)S(1)}) custom-call(s32[1,4,1024,512]{3,2,1,0:T(8,128)} %x_hbm.7, s32[8,128]{1,0:T(8,128)S(1)} %bitcast.3), custom_call_target="tpu_custom_call" | custom-call | tf_op jit(solution)/shard_map/pallas_call | solution.py:176
  14.5 4.0 %collective-permute-done.1.M_ref.M0_ref = f32[264,256]{1,0:T(8,128)S(1)} collective-permute-done((f32[264,256]{1,0:T(8,128)S(1)}, f32[264,256]{1,0:T(8,128)S(1)}, u32[]{:S(2)}, u32[]{:S(2)}) %collective-permute-start.1) | collective-permute-done | bytes 270368 | tf_op jit(solution)/shard_map/ppermute | solution.py:197
  18.5 1.6 %shard_map.108.g_ref = f32[1024,256]{1,0:T(8,128)S(1)} custom-call(f32[1024,512]{1,0:T(8,128)S(1)} %get-tuple-element.57.t_ref, f32[1024,512]{1,0:T(8,128)S(1)} %get-tuple-element.58.c_ref, f32[264,256]{1,0:T(8,128)S(1)} %collective-permute-done.1.M_ref.M0_ref, f32[1024,256]{1,0:T(8,128)S(1)} %get-tuple-element.53.W_ref), custom_call_target="tpu_custom_call" | custom-call | tf_op jit(solution)/shard_map/pallas_call | solution.py:176
  20.1 1.3 %collective-permute-done.M1_ref.M_ref = f32[264,256]{1,0:T(8,128)S(1)} collective-permute-done((f32[264,256]{1,0:T(8,128)S(1)}, f32[264,256]{1,0:T(8,128)S(1)}, u32[]{:S(2)}, u32[]{:S(2)}) %collective-permute-start) | collective-permute-done | bytes 270368 | tf_op jit(solution)/shard_map/ppermute | solution.py:197
  21.4 3.2 %shard_map.109 = (f32[1024,256]{1,0:T(8,128)S(1)}, f32[1024,256]{1,0:T(8,128)S(1)}, f32[256,256]{1,0:T(8,128)S(1)}) custom-call(f32[1024,512]{1,0:T(8,128)S(1)} %get-tuple-element.57.t_ref, f32[1024,512]{1,0:T(8,128)S(1)} %get-tuple-element.58.c_ref, f32[264,256]{1,0:T(8,128)S(1)} %collective-permute-done.1.M_ref.M0_ref, ...), custom_call_target="tpu_custom_call" | custom-call | tf_op jit(solution)/shard_map/pallas_call | solution.py:176
  24.8 1.6 %shard_map.110.h_ref = f32[256,256]{1,0:T(8,128)S(1)} custom-call(f32[1024,512]{1,0:T(8,128)S(1)} %get-tuple-element.57.t_ref, f32[1024,512]{1,0:T(8,128)S(1)} %get-tuple-element.58.c_ref, f32[264,256]{1,0:T(8,128)S(1)} %collective-permute-done.M1_ref.M_ref, f32[1024,256]{1,0:T(8,128)S(1)} %get-tuple-element.64.W_ref), custom_call_target="tpu_custom_call" | custom-call | tf_op jit(solution)/shard_map/pallas_call | solution.py:176
  28.5 4.4 %collective-permute-start.6 = (f32[256,256]{1,0:T(8,128)S(1)}, f32[256,256]{1,0:T(8,128)S(1)}, u32[]{:S(2)}, u32[]{:S(2)}) collective-permute-start(f32[256,256]{1,0:T(8,128)S(1)} %get-tuple-element.76), channel_id=1, source_target_pairs={{0,65},{2,67},{4,69},{6,71},{8,73},{10,75},{12,77},{14,79},{16,81}... | collective-permute-start | bytes 786440 | tf_op jit(solution)/shard_map/ppermute | solution.py:197
  34.2 1.9 %shard_map.112 = (f32[1024,512]{1,0:T(8,128)S(1)}, f32[1024,512]{1,0:T(8,128)S(1)}) custom-call(s32[1,4,1024,512]{3,2,1,0:T(8,128)} %x_hbm.7, s32[8,128]{1,0:T(8,128)S(1)} %bitcast.4), custom_call_target="tpu_custom_call" | custom-call | tf_op jit(solution)/shard_map/pallas_call | solution.py:176
  36.1 11.6 %collective-permute-done.10.b_ref = f32[256,256]{1,0:T(8,128)S(1)} collective-permute-done((f32[256,256]{1,0:T(8,128)S(1)}, f32[256,256]{1,0:T(8,128)S(1)}, u32[]{:S(2)}, u32[]{:S(2)}) %collective-permute-start.10) | collective-permute-done | bytes 262176 | tf_op jit(solution)/shard_map/ppermute | solution.py:197
  47.8 1.5 %collective-permute-start.8 = (f32[256,256]{1,0:T(8,128)S(1)}, f32[256,256]{1,0:T(8,128)S(1)}, u32[]{:S(2)}, u32[]{:S(2)}) collective-permute-start(f32[256,256]{1,0:T(8,128)S(1)} %get-tuple-element.65), channel_id=1, source_target_pairs={{1,66},{3,68},{5,70},{7,72},{9,74},{11,76},{13,78},{15,80},{17,82}... | collective-permute-start | bytes 786440 | tf_op jit(solution)/shard_map/ppermute | solution.py:197
  49.3 1.6 %shard_map.114.g_ref = f32[1024,256]{1,0:T(8,128)S(1)} custom-call(f32[1024,512]{1,0:T(8,128)S(1)} %get-tuple-element.67.t_ref, f32[1024,512]{1,0:T(8,128)S(1)} %get-tuple-element.68.c_ref, f32[264,256]{1,0:T(8,128)S(1)} %collective-permute-done.4.M_ref.M0_ref, f32[1024,256]{1,0:T(8,128)S(1)} %get-tuple-element.64.W_ref), custom_call_target="tpu_custom_call" | custom-call | tf_op jit(solution)/shard_map/pallas_call | solution.py:176
  50.9 4.4 %shard_map.115 = (f32[1024,256]{1,0:T(8,128)S(1)}, f32[1024,256]{1,0:T(8,128)S(1)}, f32[256,256]{1,0:T(8,128)S(1)}, f32[256,256]{1,0:T(8,128)S(1)}) custom-call(f32[1024,512]{1,0:T(8,128)S(1)} %get-tuple-element.67.t_ref, f32[1024,512]{1,0:T(8,128)S(1)} %get-tuple-element.68.c_ref, f32[264,256]{1,0:T(8,128)S(1)} %collective-permute-done.4.M_ref.M0_ref, ...), custom_call_target="tpu_custom_call" | custom-call | tf_op jit(solution)/shard_map/pallas_call | solution.py:176
  56.9 2.0 %collective-permute-start.11 = (f32[264,256]{1,0:T(8,128)S(1)}, f32[264,256]{1,0:T(8,128)S(1)}, u32[]{:S(2)}, u32[]{:S(2)}) collective-permute-start(f32[264,256]{1,0:T(8,128)S(1)} %get-tuple-element.85), channel_id=1, source_target_pairs={{0,1},{2,3},{4,5},{6,7},{8,9},{10,11},{12,13},{14,15},{16,17},{18,... | collective-permute-start | bytes 811016 | tf_op jit(solution)/shard_map/ppermute | solution.py:197
  61.0 1.3 %collective-permute-start.13 = (f32[264,256]{1,0:T(8,128)S(1)}, f32[264,256]{1,0:T(8,128)S(1)}, u32[]{:S(2)}, u32[]{:S(2)}) collective-permute-start(f32[264,256]{1,0:T(8,128)S(1)} %get-tuple-element.86), channel_id=1, source_target_pairs={{0,1},{2,3},{4,5},{6,7},{8,9},{10,11},{12,13},{14,15},{16,17},{18,... | collective-permute-start | bytes 811016 | tf_op jit(solution)/shard_map/ppermute | solution.py:197
  63.6 4.5 %collective-permute-start.14 = (f32[256,256]{1,0:T(8,128)S(1)}, f32[256,256]{1,0:T(8,128)S(1)}, u32[]{:S(2)}, u32[]{:S(2)}) collective-permute-start(f32[256,256]{1,0:T(8,128)S(1)} %get-tuple-element.92), channel_id=1, source_target_pairs={{0,1},{1,2},{2,3},{3,4},{4,5},{5,6},{6,7},{7,8},{8,9},{9,10},{10,1... | collective-permute-start | bytes 786440 | tf_op jit(solution)/shard_map/ppermute | solution.py:197
  68.5 1.9 %shard_map.120 = (f32[1024,512]{1,0:T(8,128)S(1)}, f32[1024,512]{1,0:T(8,128)S(1)}) custom-call(s32[1,4,1024,512]{3,2,1,0:T(8,128)} %x_hbm.7, s32[8,128]{1,0:T(8,128)S(1)} %bitcast.5), custom_call_target="tpu_custom_call" | custom-call | tf_op jit(solution)/shard_map/pallas_call | solution.py:176
  71.0 1.6 %shard_map.125.refs_6_ = f32[1024,256]{1,0:T(8,128)S(1)} custom-call(f32[1024,512]{1,0:T(8,128)S(1)} %get-tuple-element.82.t_ref.refs_0_, f32[1024,512]{1,0:T(8,128)S(1)} %get-tuple-element.83.c_ref.refs_1_, f32[264,256]{1,0:T(8,128)S(1)} %shard_map.123.M_ref.refs_2_.refs_1_, f32[1024,256]{1,0:T(8,128)S(1)} %get-tuple-element.87.W_ref.refs_4_), custom_call_target="tpu_custom_call" | custom-call | tf_op jit(solution)/shard_map/pallas_call | solution.py:176
  72.6 1.7 %collective-permute-done.12.a_ref = f32[264,256]{1,0:T(8,128)S(1)} collective-permute-done((f32[264,256]{1,0:T(8,128)S(1)}, f32[264,256]{1,0:T(8,128)S(1)}, u32[]{:S(2)}, u32[]{:S(2)}) %collective-permute-start.12) | collective-permute-done | bytes 270368 | tf_op jit(solution)/shard_map/ppermute | solution.py:197
  74.3 4.8 %shard_map.126 = (f32[1024,256]{1,0:T(8,128)}, f32[1024,256]{1,0:T(8,128)}, f32[256,256]{1,0:T(8,128)S(1)}, f32[256,256]{1,0:T(8,128)S(1)}) custom-call(f32[1024,512]{1,0:T(8,128)S(1)} %get-tuple-element.82.t_ref.refs_0_, f32[1024,512]{1,0:T(8,128)S(1)} %get-tuple-element.83.c_ref.refs_1_, f32[264,256]{1,0:T(8,128)S(1)} %shard_map.123.M_ref.refs_2_.refs_1_, ...), custom_call_target="tpu_custom_call" | custom-call | tf_op jit(solution)/shard_map/pallas_call | solution.py:176
  (36 shorter events, 11.6 us)
Async XLA Ops:
  7.5 11.0 %collective-permute-start.1 = (f32[264,256]{1,0:T(8,128)S(1)}, f32[264,256]{1,0:T(8,128)S(1)}, u32[]{:S(2)}, u32[]{:S(2)}) collective-permute-start(f32[264,256]{1,0:T(8,128)S(1)} %get-tuple-element.62), channel_id=1, source_target_pairs={{0,1},{1,2},{2,3},{3,4},{4,5},{5,6},{6,7},{7,8},{8,9},{9,10},{10,1... | collective-permute-start | bytes 811016 | tf_op jit(solution)/shard_map/ppermute | solution.py:197
  7.6 5.0 %copy-start = (s32[1024]{0:T(1024)S(1)}, s32[1024]{0:T(1024)}, u32[]{:S(2)}) copy-start(s32[1024]{0:T(1024)} %param.8) | copy-start | bytes 12292
  9.3 12.1 %collective-permute-start = (f32[264,256]{1,0:T(8,128)S(1)}, f32[264,256]{1,0:T(8,128)S(1)}, u32[]{:S(2)}, u32[]{:S(2)}) collective-permute-start(f32[264,256]{1,0:T(8,128)S(1)} %get-tuple-element.59), channel_id=1, source_target_pairs={{0,1},{1,2},{2,3},{3,4},{4,5},{5,6},{6,7},{7,8},{8,9},{9,10},{10,1... | collective-permute-start | bytes 811016 | tf_op jit(solution)/shard_map/ppermute | solution.py:197
  11.1 13.5 %collective-permute-start.3 = (f32[256,256]{1,0:T(8,128)S(1)}, f32[256,256]{1,0:T(8,128)S(1)}, u32[]{:S(2)}, u32[]{:S(2)}) collective-permute-start(f32[256,256]{1,0:T(8,128)S(1)} %get-tuple-element.70), channel_id=1, source_target_pairs={{0,1},{1,2},{2,3},{3,4},{4,5},{5,6},{6,7},{7,8},{8,9},{9,10},{10,1... | collective-permute-start | bytes 786440 | tf_op jit(solution)/shard_map/ppermute | solution.py:197
  11.2 15.8 %collective-permute-start.2 = (f32[256,256]{1,0:T(8,128)S(1)}, f32[256,256]{1,0:T(8,128)S(1)}, u32[]{:S(2)}, u32[]{:S(2)}) collective-permute-start(f32[256,256]{1,0:T(8,128)S(1)} %get-tuple-element.55), channel_id=1, source_target_pairs={{0,1},{1,2},{2,3},{3,4},{4,5},{5,6},{6,7},{7,8},{8,9},{9,10},{10,1... | collective-permute-start | bytes 786440 | tf_op jit(solution)/shard_map/ppermute | solution.py:197
  24.8 24.6 %collective-permute-start.4 = (f32[264,256]{1,0:T(8,128)S(1)}, f32[264,256]{1,0:T(8,128)S(1)}, u32[]{:S(2)}, u32[]{:S(2)}) collective-permute-start(f32[264,256]{1,0:T(8,128)S(1)} %get-tuple-element.71), channel_id=1, source_target_pairs={{0,65},{1,66},{2,67},{3,68},{4,69},{5,70},{6,71},{7,72},{8,73},{9,... | collective-permute-start | bytes 811016 | tf_op jit(solution)/shard_map/ppermute | solution.py:197
  27.1 23.8 %collective-permute-start.5 = (f32[264,256]{1,0:T(8,128)S(1)}, f32[264,256]{1,0:T(8,128)S(1)}, u32[]{:S(2)}, u32[]{:S(2)}) collective-permute-start(f32[264,256]{1,0:T(8,128)S(1)} %get-tuple-element.72), channel_id=1, source_target_pairs={{0,65},{1,66},{2,67},{3,68},{4,69},{5,70},{6,71},{7,72},{8,73},{9,... | collective-permute-start | bytes 811016 | tf_op jit(solution)/shard_map/ppermute | solution.py:197
  27.2 20.6 %collective-permute-start.10 = (f32[256,256]{1,0:T(8,128)S(1)}, f32[256,256]{1,0:T(8,128)S(1)}, u32[]{:S(2)}, u32[]{:S(2)}) collective-permute-start(f32[256,256]{1,0:T(8,128)S(1)} %get-tuple-element.76), channel_id=1, source_target_pairs={{1,66},{3,68},{5,70},{7,72},{9,74},{11,76},{13,78},{15,80},{17,82}... | collective-permute-start | bytes 786440 | tf_op jit(solution)/shard_map/ppermute | solution.py:197
  28.5 20.8 %collective-permute-start.6 = (f32[256,256]{1,0:T(8,128)S(1)}, f32[256,256]{1,0:T(8,128)S(1)}, u32[]{:S(2)}, u32[]{:S(2)}) collective-permute-start(f32[256,256]{1,0:T(8,128)S(1)} %get-tuple-element.76), channel_id=1, source_target_pairs={{0,65},{2,67},{4,69},{6,71},{8,73},{10,75},{12,77},{14,79},{16,81}... | collective-permute-start | bytes 786440 | tf_op jit(solution)/shard_map/ppermute | solution.py:197
  32.9 23.2 %collective-permute-start.7 = (f32[256,256]{1,0:T(8,128)S(1)}, f32[256,256]{1,0:T(8,128)S(1)}, u32[]{:S(2)}, u32[]{:S(2)}) collective-permute-start(f32[256,256]{1,0:T(8,128)S(1)} %get-tuple-element.65), channel_id=1, source_target_pairs={{0,65},{2,67},{4,69},{6,71},{8,73},{10,75},{12,77},{14,79},{16,81}... | collective-permute-start | bytes 786440 | tf_op jit(solution)/shard_map/ppermute | solution.py:197
  47.8 13.1 %collective-permute-start.8 = (f32[256,256]{1,0:T(8,128)S(1)}, f32[256,256]{1,0:T(8,128)S(1)}, u32[]{:S(2)}, u32[]{:S(2)}) collective-permute-start(f32[256,256]{1,0:T(8,128)S(1)} %get-tuple-element.65), channel_id=1, source_target_pairs={{1,66},{3,68},{5,70},{7,72},{9,74},{11,76},{13,78},{15,80},{17,82}... | collective-permute-start | bytes 786440 | tf_op jit(solution)/shard_map/ppermute | solution.py:197
  56.9 11.2 %collective-permute-start.11 = (f32[264,256]{1,0:T(8,128)S(1)}, f32[264,256]{1,0:T(8,128)S(1)}, u32[]{:S(2)}, u32[]{:S(2)}) collective-permute-start(f32[264,256]{1,0:T(8,128)S(1)} %get-tuple-element.85), channel_id=1, source_target_pairs={{0,1},{2,3},{4,5},{6,7},{8,9},{10,11},{12,13},{14,15},{16,17},{18,... | collective-permute-start | bytes 811016 | tf_op jit(solution)/shard_map/ppermute | solution.py:197
  58.9 12.0 %collective-permute-start.9 = (f32[264,256]{1,0:T(8,128)S(1)}, f32[264,256]{1,0:T(8,128)S(1)}, u32[]{:S(2)}, u32[]{:S(2)}) collective-permute-start(f32[264,256]{1,0:T(8,128)S(1)} %get-tuple-element.77), channel_id=1, source_target_pairs={{1,2},{3,4},{5,6},{7,8},{9,10},{11,12},{13,14},{15,16},{17,18},{19... | collective-permute-start | bytes 811016 | tf_op jit(solution)/shard_map/ppermute | solution.py:197
  61.0 11.6 %collective-permute-start.13 = (f32[264,256]{1,0:T(8,128)S(1)}, f32[264,256]{1,0:T(8,128)S(1)}, u32[]{:S(2)}, u32[]{:S(2)}) collective-permute-start(f32[264,256]{1,0:T(8,128)S(1)} %get-tuple-element.86), channel_id=1, source_target_pairs={{0,1},{2,3},{4,5},{6,7},{8,9},{10,11},{12,13},{14,15},{16,17},{18,... | collective-permute-start | bytes 811016 | tf_op jit(solution)/shard_map/ppermute | solution.py:197
  62.3 12.0 %collective-permute-start.12 = (f32[264,256]{1,0:T(8,128)S(1)}, f32[264,256]{1,0:T(8,128)S(1)}, u32[]{:S(2)}, u32[]{:S(2)}) collective-permute-start(f32[264,256]{1,0:T(8,128)S(1)} %get-tuple-element.78), channel_id=1, source_target_pairs={{1,2},{3,4},{5,6},{7,8},{9,10},{11,12},{13,14},{15,16},{17,18},{19... | collective-permute-start | bytes 811016 | tf_op jit(solution)/shard_map/ppermute | solution.py:197
  63.6 15.6 %collective-permute-start.14 = (f32[256,256]{1,0:T(8,128)S(1)}, f32[256,256]{1,0:T(8,128)S(1)}, u32[]{:S(2)}, u32[]{:S(2)}) collective-permute-start(f32[256,256]{1,0:T(8,128)S(1)} %get-tuple-element.92), channel_id=1, source_target_pairs={{0,1},{1,2},{2,3},{3,4},{4,5},{5,6},{6,7},{7,8},{8,9},{9,10},{10,1... | collective-permute-start | bytes 786440 | tf_op jit(solution)/shard_map/ppermute | solution.py:197
  68.1 11.8 %collective-permute-start.15 = (f32[256,256]{1,0:T(8,128)S(1)}, f32[256,256]{1,0:T(8,128)S(1)}, u32[]{:S(2)}, u32[]{:S(2)}) collective-permute-start(f32[256,256]{1,0:T(8,128)S(1)} %get-tuple-element.80), channel_id=1, source_target_pairs={{0,1},{1,2},{2,3},{3,4},{4,5},{5,6},{6,7},{7,8},{8,9},{9,10},{10,1... | collective-permute-start | bytes 786440 | tf_op jit(solution)/shard_map/ppermute | solution.py:197

commit v7 on v3

--- a/solution.py
+++ b/solution.py
@@ -6,6 +6,7 @@
 from jax.experimental import pallas as pl
 from jax.experimental.pallas import tpu as pltpu
 from jax.sharding import PartitionSpec as P
+
 
 LOG_TOTAL = 17.0
 LEARNING = 0.05
@@ -147,10 +148,9 @@
     grad = None
     for rows in row_spans(W_ref.shape[0], 256):
         W = W_ref[rows, :]
-        e, _ = half_errors(j, W, t_ref, c_ref, M_ref, rows)
-        part = dot(W, e, 0, 0)
+        part = dot(half_errors(j, W, t_ref, c_ref, M_ref, rows)[0], W, 0, 0)
         grad = part if grad is None else grad + part
-    h_ref[...] = grad.T
+    h_ref[...] = grad
 
 
 def update_kernel(h_ref, M_ref, B_ref, Mo_ref, Bo_ref):
@@ -168,7 +168,7 @@
         Co_ref[rows, :], Bo_ref[rows, :] = adagrad(M_ref[:n, :], B_ref[...], h_ref[...])
 
 
-def call(kernel, operands, spaces, outs, out_spaces, scratch, mib, name):
+def call(kernel, operands, spaces, outs, out_spaces, scratch, mib):
     return pl.pallas_call(
         kernel,
         in_specs=[pl.BlockSpec(memory_space=s) for s in spaces],
@@ -176,7 +176,6 @@
         out_shape=[jax.ShapeDtypeStruct(s, f32) for s in outs],
         scratch_shapes=scratch,
         compiler_params=pltpu.CompilerParams(vmem_limit_bytes=mib << 20),
-        name=name,
     )(*operands)
 
 
@@ -205,43 +204,42 @@
         [wide, wide, tile, tile] + [message] * HALVES + [half] * HALVES, [V] * (4 + 2 * HALVES),
         [V(tile, jnp.int32), V(wide, f32), V(wide, f32), V(rows.shape, jnp.int32),
          V(cols.shape, jnp.int32), DMA((4 + 3 * 2,)), DMA((HALVES,))],
-        24, "first",
+        24,
     )
     M, B = blocks[:HALVES], blocks[HALVES:]
     for step in range(steps):
-        h = None
+        grads = []
         if step > 0:
-            part = call(row_part_kernel, (t, c, M[0], W), [V] * 4, [wide], [V], [], 12, "row")[0]
-            operands = (t, c, M[0], M[1], W, A, part)
+            g = call(row_part_kernel, (t, c, M[0], W), [V] * 4, [wide], [V], [], 12)[0]
+            operands = (t, c, M[0], M[1], W, A, g)
             if step + 1 == steps:
                 W, A, *grads = call(
                     last_kernel, operands, [V] * 7, [wide, wide, half, half], [H, H, V, V],
-                    [V(wide, f32), V(wide, f32), DMA((2, 2))], 20, "last",
+                    [V(wide, f32), V(wide, f32), DMA((2, 2))], 20,
                 )
                 break
-            W, A, h = call(
-                functools.partial(row_col_kernel, 256, (0,), lambda rows: None), operands, [V] * 7,
-                [wide, wide, half], [V] * 3, [], 16, "row_col",
+            size, halves = (512, (0, 1)) if step == steps // 2 else (256, (0,))
+            W, A, *grads = call(
+                functools.partial(row_col_kernel, size, halves, lambda rows: None), operands, [V] * 7,
+                [wide, wide] + [half] * len(halves), [V] * (2 + len(halves)), [], 20,
             )
         across = int(step + 1 == steps // 2)
         sent, sums = [], []
         for j in range(HALVES):
-            if h is None or j > 0:
+            if j == len(grads):
                 operands = (t, c, M[j], W)
-                h = call(functools.partial(col_kernel, j), operands, [V] * 4, [half], [V], [], 12, "col")[0]
-            value, total = call(
-                update_kernel, (h, M[j], B[j]), [V] * 3, [message, half], [V] * 2, [], 4, "update"
-            )
+                grads += call(functools.partial(col_kernel, j), operands, [V] * 4, [half], [V], [], 12)
+            value, total = call(update_kernel, (grads[j], M[j], B[j]), [V] * 3, [message, half], [V] * 2, [], 4)
             sent.append(move(value, across))
             sums.append(total)
         row_tie = lax.optimization_barrier((rows, *sums))[0]
         t, c = call(
             functools.partial(terms_kernel, step + 1), (hbm[0], row_tie), [H, V], [tile, tile], [V] * 2,
-            [V(tile, jnp.int32), DMA((4,))], 12, "terms",
+            [V(tile, jnp.int32), DMA((4,))], 12,
         )
         M, B = sent, [move(total, across) for total in sums]
     operands = (grads[0], M[0], B[0], grads[1], M[1], B[1])
-    C, B = call(final_kernel, operands, [V] * 6, [tall, tall], [V] * 2, [], 6, "final")
+    C, B = call(final_kernel, operands, [V] * 6, [tall, tall], [V] * 2, [], 6)
     return W, A, C, B
 
 

time: 69.7 us -> 69.6 us (level)
  waiting for transfers between devices: 25.8 us -> 27.5 us
  Pallas kernels: 35.4 us -> 34.4 us
  starting transfers between devices: 7.52 us -> 6.81 us
    ppermute x12, waiting for transfers between devices: 25.8 us -> 27.5 us  [move(): return lax.ppermute(block, ('outer', 'inner'), route)]
    pallas_call x21 -> x20, Pallas kernels: 35.4 us -> 34.4 us  [call(): pl.pallas_call(kernel, in_specs=[pl.BlockSpec(memory_space=s) for s in sp...]
    ppermute x12, starting transfers between devices: 7.52 us -> 6.81 us  [move(): return lax.ppermute(block, ('outer', 'inner'), route)]
  transfers between devices with their start and end apart: 12 -> 12, of which waited for: 10 -> 10; matrix products, arithmetic and copies ran while one was open for 0% -> 0% of each run, Pallas kernels for 39% -> 38%
where the time goes in v7:
time: 69.6 us; the launch traced here: 69.5 us
  Pallas kernels  34.4 us (49%)
  waiting for transfers between devices  27.5 us (40%)
  starting transfers between devices  6.81 us (10%)
  between operations  0.82 us (1%)
    pallas_call x20, Pallas kernels, call(): pl.pallas_call(kernel, in_specs=[pl.BlockSpec(memory_space=s) for s in sp...  34.4 us
    ppermute x12, waiting for transfers between devices, move(): return lax.ppermute(block, ('outer', 'inner'), route)  27.5 us
    ppermute x12, starting transfers between devices, move(): return lax.ppermute(block, ('outer', 'inner'), route)  6.81 us
  transfers between devices with their start and end apart: 12, of which 10 were waited for; matrix products, arithmetic and copies ran while one was open for 0% of the time, Pallas kernels for 38%

profile of v7, /device:TPU:0, one launch (start us, length us, event | category | flops | bytes accessed | tf_op | source)
XLA Modules:
  0.0 69.5 jit_solution(2328671031452955172)
XLA Ops:
  0.6 5.2 %shard_map.102 = (f32[1024,256]{1,0:T(8,128)S(1)}, f32[1024,256]{1,0:T(8,128)S(1)}, f32[1024,512]{1,0:T(8,128)S(1)}, f32[1024,512]{1,0:T(8,128)S(1)}, f32[264,25...) custom-call(s32[1,4,1024,512]{3,2,1,0:T(8,128)} %x_hbm.7, ...), custom_call_target="tpu_custom_call" | custom-call | tf_op jit(solution)/shard_map/pallas_call | solution.py:172
  5.9 1.6 %shard_map.103.h_ref = f32[256,256]{1,0:T(8,128)S(1)} custom-call(f32[1024,512]{1,0:T(8,128)S(1)} %get-tuple-element.46.t_ref, f32[1024,512]{1,0:T(8,128)S(1)} %get-tuple-element.47.c_ref, f32[264,256]{1,0:T(8,128)S(1)} %get-tuple-element.48.M_ref, f32[1024,256]{1,0:T(8,128)S(1)} %get-tuple-element.49.W_ref), custom_call_target="tpu_custom_call" | custom-call | tf_op jit(solution)/shard_map/pallas_call | solution.py:172
  7.6 1.6 %shard_map.105.h_ref = f32[256,256]{1,0:T(8,128)S(1)} custom-call(f32[1024,512]{1,0:T(8,128)S(1)} %get-tuple-element.46.t_ref, f32[1024,512]{1,0:T(8,128)S(1)} %get-tuple-element.47.c_ref, f32[264,256]{1,0:T(8,128)S(1)} %get-tuple-element.52.M_ref, f32[1024,256]{1,0:T(8,128)S(1)} %get-tuple-element.49.W_ref), custom_call_target="tpu_custom_call" | custom-call | tf_op jit(solution)/shard_map/pallas_call | solution.py:172
  9.3 1.8 %collective-permute-start.1 = (f32[264,256]{1,0:T(8,128)S(1)}, f32[264,256]{1,0:T(8,128)S(1)}, u32[]{:S(2)}, u32[]{:S(2)}) collective-permute-start(f32[264,256]{1,0:T(8,128)S(1)} %get-tuple-element.59), channel_id=1, source_target_pairs={{0,1},{1,2},{2,3},{3,4},{4,5},{5,6},{6,7},{7,8},{8,9},{9,10},{10,1... | collective-permute-start | bytes 811016 | tf_op jit(solution)/shard_map/ppermute | solution.py:192
  11.2 1.4 %collective-permute-start.3 = (f32[256,256]{1,0:T(8,128)S(1)}, f32[256,256]{1,0:T(8,128)S(1)}, u32[]{:S(2)}, u32[]{:S(2)}) collective-permute-start(f32[256,256]{1,0:T(8,128)S(1)} %get-tuple-element.54), channel_id=1, source_target_pairs={{0,1},{1,2},{2,3},{3,4},{4,5},{5,6},{6,7},{7,8},{8,9},{9,10},{10,1... | collective-permute-start | bytes 786440 | tf_op jit(solution)/shard_map/ppermute | solution.py:192
  12.6 1.9 %shard_map.107 = (f32[1024,512]{1,0:T(8,128)S(1)}, f32[1024,512]{1,0:T(8,128)S(1)}) custom-call(s32[1,4,1024,512]{3,2,1,0:T(8,128)} %x_hbm.7, s32[8,128]{1,0:T(8,128)S(1)} %bitcast.3), custom_call_target="tpu_custom_call" | custom-call | tf_op jit(solution)/shard_map/pallas_call | solution.py:172
  14.5 4.0 %collective-permute-done.M_ref.M0_ref = f32[264,256]{1,0:T(8,128)S(1)} collective-permute-done((f32[264,256]{1,0:T(8,128)S(1)}, f32[264,256]{1,0:T(8,128)S(1)}, u32[]{:S(2)}, u32[]{:S(2)}) %collective-permute-start) | collective-permute-done | bytes 270368 | tf_op jit(solution)/shard_map/ppermute | solution.py:192
  18.5 1.6 %shard_map.108.g_ref = f32[1024,256]{1,0:T(8,128)S(1)} custom-call(f32[1024,512]{1,0:T(8,128)S(1)} %get-tuple-element.56.t_ref, f32[1024,512]{1,0:T(8,128)S(1)} %get-tuple-element.57.c_ref, f32[264,256]{1,0:T(8,128)S(1)} %collective-permute-done.M_ref.M0_ref, f32[1024,256]{1,0:T(8,128)S(1)} %get-tuple-element.49.W_ref), custom_call_target="tpu_custom_call" | custom-call | tf_op jit(solution)/shard_map/pallas_call | solution.py:172
  20.1 1.3 %collective-permute-done.1.M1_ref.M_ref = f32[264,256]{1,0:T(8,128)S(1)} collective-permute-done((f32[264,256]{1,0:T(8,128)S(1)}, f32[264,256]{1,0:T(8,128)S(1)}, u32[]{:S(2)}, u32[]{:S(2)}) %collective-permute-start.1) | collective-permute-done | bytes 270368 | tf_op jit(solution)/shard_map/ppermute | solution.py:192
  21.4 3.3 %shard_map.109 = (f32[1024,256]{1,0:T(8,128)S(1)}, f32[1024,256]{1,0:T(8,128)S(1)}, f32[256,256]{1,0:T(8,128)S(1)}) custom-call(f32[1024,512]{1,0:T(8,128)S(1)} %get-tuple-element.56.t_ref, f32[1024,512]{1,0:T(8,128)S(1)} %get-tuple-element.57.c_ref, f32[264,256]{1,0:T(8,128)S(1)} %collective-permute-done.M_ref.M0_ref, ...), custom_call_target="tpu_custom_call" | custom-call | tf_op jit(solution)/shard_map/pallas_call | solution.py:172
  24.9 1.6 %shard_map.111.h_ref = f32[256,256]{1,0:T(8,128)S(1)} custom-call(f32[1024,512]{1,0:T(8,128)S(1)} %get-tuple-element.56.t_ref, f32[1024,512]{1,0:T(8,128)S(1)} %get-tuple-element.57.c_ref, f32[264,256]{1,0:T(8,128)S(1)} %collective-permute-done.1.M1_ref.M_ref, f32[1024,256]{1,0:T(8,128)S(1)} %get-tuple-element.63.W_ref), custom_call_target="tpu_custom_call" | custom-call | tf_op jit(solution)/shard_map/pallas_call | solution.py:172
  27.3 1.8 %collective-permute-start.7 = (f32[256,256]{1,0:T(8,128)S(1)}, f32[256,256]{1,0:T(8,128)S(1)}, u32[]{:S(2)}, u32[]{:S(2)}) collective-permute-start(f32[256,256]{1,0:T(8,128)S(1)} %get-tuple-element.64), channel_id=1, source_target_pairs={{0,65},{1,66},{2,67},{3,68},{4,69},{5,70},{6,71},{7,72},{8,73},{9,... | collective-permute-start | bytes 786440 | tf_op jit(solution)/shard_map/ppermute | solution.py:192
  29.1 1.9 %shard_map.113 = (f32[1024,512]{1,0:T(8,128)S(1)}, f32[1024,512]{1,0:T(8,128)S(1)}) custom-call(s32[1,4,1024,512]{3,2,1,0:T(8,128)} %x_hbm.7, s32[8,128]{1,0:T(8,128)S(1)} %bitcast.4), custom_call_target="tpu_custom_call" | custom-call | tf_op jit(solution)/shard_map/pallas_call | solution.py:172
  31.0 7.4 %collective-permute-done.4.M_ref.M0_ref = f32[264,256]{1,0:T(8,128)S(1)} collective-permute-done((f32[264,256]{1,0:T(8,128)S(1)}, f32[264,256]{1,0:T(8,128)S(1)}, u32[]{:S(2)}, u32[]{:S(2)}) %collective-permute-start.4) | collective-permute-done | bytes 270368 | tf_op jit(solution)/shard_map/ppermute | solution.py:192
  38.4 1.6 %shard_map.114.g_ref = f32[1024,256]{1,0:T(8,128)S(1)} custom-call(f32[1024,512]{1,0:T(8,128)S(1)} %get-tuple-element.66.t_ref, f32[1024,512]{1,0:T(8,128)S(1)} %get-tuple-element.67.c_ref, f32[264,256]{1,0:T(8,128)S(1)} %collective-permute-done.4.M_ref.M0_ref, f32[1024,256]{1,0:T(8,128)S(1)} %get-tuple-element.63.W_ref), custom_call_target="tpu_custom_call" | custom-call | tf_op jit(solution)/shard_map/pallas_call | solution.py:172
  40.0 3.2 %collective-permute-done.5.M1_ref.M_ref = f32[264,256]{1,0:T(8,128)S(1)} collective-permute-done((f32[264,256]{1,0:T(8,128)S(1)}, f32[264,256]{1,0:T(8,128)S(1)}, u32[]{:S(2)}, u32[]{:S(2)}) %collective-permute-start.5) | collective-permute-done | bytes 270368 | tf_op jit(solution)/shard_map/ppermute | solution.py:192
  43.1 4.4 %shard_map.115 = (f32[1024,256]{1,0:T(8,128)S(1)}, f32[1024,256]{1,0:T(8,128)S(1)}, f32[256,256]{1,0:T(8,128)S(1)}, f32[256,256]{1,0:T(8,128)S(1)}) custom-call(f32[1024,512]{1,0:T(8,128)S(1)} %get-tuple-element.66.t_ref, f32[1024,512]{1,0:T(8,128)S(1)} %get-tuple-element.67.c_ref, f32[264,256]{1,0:T(8,128)S(1)} %collective-permute-done.4.M_ref.M0_ref, ...), custom_call_target="tpu_custom_call" | custom-call | tf_op jit(solution)/shard_map/pallas_call | solution.py:172
  48.6 3.9 %collective-permute-done.7.B_ref = f32[256,256]{1,0:T(8,128)S(1)} collective-permute-done((f32[256,256]{1,0:T(8,128)S(1)}, f32[256,256]{1,0:T(8,128)S(1)}, u32[]{:S(2)}, u32[]{:S(2)}) %collective-permute-start.7) | collective-permute-done | bytes 262176 | tf_op jit(solution)/shard_map/ppermute | solution.py:192
  53.2 1.9 %shard_map.118 = (f32[1024,512]{1,0:T(8,128)S(1)}, f32[1024,512]{1,0:T(8,128)S(1)}) custom-call(s32[1,4,1024,512]{3,2,1,0:T(8,128)} %x_hbm.7, s32[8,128]{1,0:T(8,128)S(1)} %bitcast.5), custom_call_target="tpu_custom_call" | custom-call | tf_op jit(solution)/shard_map/pallas_call | solution.py:172
  55.2 2.9 %collective-permute-done.8.M_ref.refs_2_.refs_1_ = f32[264,256]{1,0:T(8,128)S(1)} collective-permute-done((f32[264,256]{1,0:T(8,128)S(1)}, f32[264,256]{1,0:T(8,128)S(1)}, u32[]{:S(2)}, u32[]{:S(2)}) %collective-permute-start.8) | collective-permute-done | bytes 270368 | tf_op jit(solution)/shard_map/ppermute | solution.py:192
  58.1 1.6 %shard_map.119.refs_6_ = f32[1024,256]{1,0:T(8,128)S(1)} custom-call(f32[1024,512]{1,0:T(8,128)S(1)} %get-tuple-element.76.t_ref.refs_0_, f32[1024,512]{1,0:T(8,128)S(1)} %get-tuple-element.77.c_ref.refs_1_, f32[264,256]{1,0:T(8,128)S(1)} %collective-permute-done.8.M_ref.refs_2_.refs_1_, f32[1024,256]{1,0:T(8,128)S(1)} %get-tuple-element.80.W_ref.refs_4_), custom_call_target="tpu_custom_call" | custom-call | tf_op jit(solution)/shard_map/pallas_call | solution.py:172
  59.6 3.1 %collective-permute-done.9.refs_3_.refs_4_ = f32[264,256]{1,0:T(8,128)S(1)} collective-permute-done((f32[264,256]{1,0:T(8,128)S(1)}, f32[264,256]{1,0:T(8,128)S(1)}, u32[]{:S(2)}, u32[]{:S(2)}) %collective-permute-start.9) | collective-permute-done | bytes 270368 | tf_op jit(solution)/shard_map/ppermute | solution.py:192
  62.8 4.8 %shard_map.120 = (f32[1024,256]{1,0:T(8,128)}, f32[1024,256]{1,0:T(8,128)}, f32[256,256]{1,0:T(8,128)S(1)}, f32[256,256]{1,0:T(8,128)S(1)}) custom-call(f32[1024,512]{1,0:T(8,128)S(1)} %get-tuple-element.76.t_ref.refs_0_, f32[1024,512]{1,0:T(8,128)S(1)} %get-tuple-element.77.c_ref.refs_1_, f32[264,256]{1,0:T(8,128)S(1)} %collective-permute-done.8.M_ref.refs_2_.refs_1_, ...), custom_call_target="tpu_custom_call" | custom-call | tf_op jit(solution)/shard_map/pallas_call | solution.py:172
  68.4 1.1 %shard_map.121 = (f32[512,256]{1,0:T(8,128)}, f32[512,256]{1,0:T(8,128)}) custom-call(f32[256,256]{1,0:T(8,128)S(1)} %get-tuple-element.84.refs_0_, f32[264,256]{1,0:T(8,128)S(1)} %collective-permute-done.8.M_ref.refs_2_.refs_1_, f32[256,256]{1,0:T(8,128)S(1)} %collective-permute-done.10.refs_2_, f32[256,256]{1,0:T(8,128)S(1)} %get-tuple-element.85.refs_3_, ...), custom_call_target="tpu_custom_call" | custom-call | tf_op jit(solution)/shard_map/pallas_call | solution.py:172
  (22 shorter events, 3.8 us)
Async XLA Ops:
  7.5 11.0 %collective-permute-start = (f32[264,256]{1,0:T(8,128)S(1)}, f32[264,256]{1,0:T(8,128)S(1)}, u32[]{:S(2)}, u32[]{:S(2)}) collective-permute-start(f32[264,256]{1,0:T(8,128)S(1)} %get-tuple-element.58), channel_id=1, source_target_pairs={{0,1},{1,2},{2,3},{3,4},{4,5},{5,6},{6,7},{7,8},{8,9},{9,10},{10,1... | collective-permute-start | bytes 811016 | tf_op jit(solution)/shard_map/ppermute | solution.py:192
  7.6 5.0 %copy-start = (s32[1024]{0:T(1024)S(1)}, s32[1024]{0:T(1024)}, u32[]{:S(2)}) copy-start(s32[1024]{0:T(1024)} %param.8) | copy-start | bytes 12292
  9.3 12.1 %collective-permute-start.1 = (f32[264,256]{1,0:T(8,128)S(1)}, f32[264,256]{1,0:T(8,128)S(1)}, u32[]{:S(2)}, u32[]{:S(2)}) collective-permute-start(f32[264,256]{1,0:T(8,128)S(1)} %get-tuple-element.59), channel_id=1, source_target_pairs={{0,1},{1,2},{2,3},{3,4},{4,5},{5,6},{6,7},{7,8},{8,9},{9,10},{10,1... | collective-permute-start | bytes 811016 | tf_op jit(solution)/shard_map/ppermute | solution.py:192
  11.1 13.6 %collective-permute-start.2 = (f32[256,256]{1,0:T(8,128)S(1)}, f32[256,256]{1,0:T(8,128)S(1)}, u32[]{:S(2)}, u32[]{:S(2)}) collective-permute-start(f32[256,256]{1,0:T(8,128)S(1)} %get-tuple-element.51), channel_id=1, source_target_pairs={{0,1},{1,2},{2,3},{3,4},{4,5},{5,6},{6,7},{7,8},{8,9},{9,10},{10,1... | collective-permute-start | bytes 786440 | tf_op jit(solution)/shard_map/ppermute | solution.py:192
  11.2 15.8 %collective-permute-start.3 = (f32[256,256]{1,0:T(8,128)S(1)}, f32[256,256]{1,0:T(8,128)S(1)}, u32[]{:S(2)}, u32[]{:S(2)}) collective-permute-start(f32[256,256]{1,0:T(8,128)S(1)} %get-tuple-element.54), channel_id=1, source_target_pairs={{0,1},{1,2},{2,3},{3,4},{4,5},{5,6},{6,7},{7,8},{8,9},{9,10},{10,1... | collective-permute-start | bytes 786440 | tf_op jit(solution)/shard_map/ppermute | solution.py:192
  24.8 13.6 %collective-permute-start.4 = (f32[264,256]{1,0:T(8,128)S(1)}, f32[264,256]{1,0:T(8,128)S(1)}, u32[]{:S(2)}, u32[]{:S(2)}) collective-permute-start(f32[264,256]{1,0:T(8,128)S(1)} %get-tuple-element.68), channel_id=1, source_target_pairs={{0,65},{1,66},{2,67},{3,68},{4,69},{5,70},{6,71},{7,72},{8,73},{9,... | collective-permute-start | bytes 811016 | tf_op jit(solution)/shard_map/ppermute | solution.py:192
  27.1 16.0 %collective-permute-start.5 = (f32[264,256]{1,0:T(8,128)S(1)}, f32[264,256]{1,0:T(8,128)S(1)}, u32[]{:S(2)}, u32[]{:S(2)}) collective-permute-start(f32[264,256]{1,0:T(8,128)S(1)} %get-tuple-element.69), channel_id=1, source_target_pairs={{0,65},{1,66},{2,67},{3,68},{4,69},{5,70},{6,71},{7,72},{8,73},{9,... | collective-permute-start | bytes 811016 | tf_op jit(solution)/shard_map/ppermute | solution.py:192
  27.2 20.6 %collective-permute-start.6 = (f32[256,256]{1,0:T(8,128)S(1)}, f32[256,256]{1,0:T(8,128)S(1)}, u32[]{:S(2)}, u32[]{:S(2)}) collective-permute-start(f32[256,256]{1,0:T(8,128)S(1)} %get-tuple-element.62), channel_id=1, source_target_pairs={{0,65},{1,66},{2,67},{3,68},{4,69},{5,70},{6,71},{7,72},{8,73},{9,... | collective-permute-start | bytes 786440 | tf_op jit(solution)/shard_map/ppermute | solution.py:192
  27.3 25.2 %collective-permute-start.7 = (f32[256,256]{1,0:T(8,128)S(1)}, f32[256,256]{1,0:T(8,128)S(1)}, u32[]{:S(2)}, u32[]{:S(2)}) collective-permute-start(f32[256,256]{1,0:T(8,128)S(1)} %get-tuple-element.64), channel_id=1, source_target_pairs={{0,65},{1,66},{2,67},{3,68},{4,69},{5,70},{6,71},{7,72},{8,73},{9,... | collective-permute-start | bytes 786440 | tf_op jit(solution)/shard_map/ppermute | solution.py:192
  47.9 10.2 %collective-permute-start.8 = (f32[264,256]{1,0:T(8,128)S(1)}, f32[264,256]{1,0:T(8,128)S(1)}, u32[]{:S(2)}, u32[]{:S(2)}) collective-permute-start(f32[264,256]{1,0:T(8,128)S(1)} %get-tuple-element.78), channel_id=1, source_target_pairs={{0,1},{1,2},{2,3},{3,4},{4,5},{5,6},{6,7},{7,8},{8,9},{9,10},{10,1... | collective-permute-start | bytes 811016 | tf_op jit(solution)/shard_map/ppermute | solution.py:192
  52.6 10.2 %collective-permute-start.9 = (f32[264,256]{1,0:T(8,128)S(1)}, f32[264,256]{1,0:T(8,128)S(1)}, u32[]{:S(2)}, u32[]{:S(2)}) collective-permute-start(f32[264,256]{1,0:T(8,128)S(1)} %get-tuple-element.79), channel_id=1, source_target_pairs={{0,1},{1,2},{2,3},{3,4},{4,5},{5,6},{6,7},{7,8},{8,9},{9,10},{10,1... | collective-permute-start | bytes 811016 | tf_op jit(solution)/shard_map/ppermute | solution.py:192
  52.8 14.7 %collective-permute-start.11 = (f32[256,256]{1,0:T(8,128)S(1)}, f32[256,256]{1,0:T(8,128)S(1)}, u32[]{:S(2)}, u32[]{:S(2)}) collective-permute-start(f32[256,256]{1,0:T(8,128)S(1)} %get-tuple-element.74), channel_id=1, source_target_pairs={{0,1},{1,2},{2,3},{3,4},{4,5},{5,6},{6,7},{7,8},{8,9},{9,10},{10,1... | collective-permute-start | bytes 786440 | tf_op jit(solution)/shard_map/ppermute | solution.py:192
  52.9 15.5 %collective-permute-start.10 = (f32[256,256]{1,0:T(8,128)S(1)}, f32[256,256]{1,0:T(8,128)S(1)}, u32[]{:S(2)}, u32[]{:S(2)}) collective-permute-start(f32[256,256]{1,0:T(8,128)S(1)} %get-tuple-element.72), channel_id=1, source_target_pairs={{0,1},{1,2},{2,3},{3,4},{4,5},{5,6},{6,7},{7,8},{8,9},{9,10},{10,1... | collective-permute-start | bytes 786440 | tf_op jit(solution)/shard_map/ppermute | solution.py:192
